TPU v7x, 32 devices: a whole 2x2x4 slice. The times are simulated.
32 devices in a mesh: dp: 4 (over z), blk: 2 (over core), head: 4 (over y, x).
Axes of the slice: x: 2, y: 2, z: 4, core: 2. Of those that a mesh axis runs over, the one named last changes fastest.
Arguments:
- stream_in: float32 [8, 2048, 1024], P('dp', ('blk', 'head')), may hold values from -6 to 6
- ln1_gain: bfloat16 [1024], P(('dp', 'blk', 'head')), may hold values from 0.5 to 1.5
- ln1_bias: bfloat16 [1024], P(('dp', 'blk', 'head')), may hold values from -1 to 1
- w_qkv: bfloat16 [1024, 3072], P(('dp', 'blk', 'head')), may hold values from -1 to 1, as said below
- b_qv: bfloat16 [2, 1024], P(None, ('dp', 'blk', 'head')), may hold values from -1 to 1
- w_out: bfloat16 [1024, 1024], P(('dp', 'blk', 'head')), may hold values from -1 to 1
- b_out: bfloat16 [1024], P(('dp', 'blk', 'head')), may hold values from -1 to 1
- ln2_gain: bfloat16 [1024], P(('dp', 'blk', 'head')), may hold values from 0.5 to 1.5
- ln2_bias: bfloat16 [1024], P(('dp', 'blk', 'head')), may hold values from -1 to 1
- w_fc: bfloat16 [1024, 4096], P(('dp', 'blk', 'head')), may hold values from -0.1875 to 0.1875
- b_fc: bfloat16 [4096], P(('dp', 'blk', 'head')), may hold values from -1 to 1
- w_proj: bfloat16 [4096, 1024], P(('dp', 'blk', 'head')), may hold values from -0.09375 to 0.09375
- b_proj: bfloat16 [1024], P(('dp', 'blk', 'head')), may hold values from -1 to 1
- cotangent: float32 [8, 2048, 1024], P('dp', ('blk', 'head')), may hold values from -6 to 6
Outputs:
- stream_out: float32 [8, 2048, 1024], P('dp', ('blk', 'head'))
- grad_in: float32 [8, 2048, 1024], P('dp', ('blk', 'head'))
- grad_ln1_gain: float32 [1024], P(('dp', 'blk', 'head'))
- grad_ln1_bias: float32 [1024], P(('dp', 'blk', 'head'))
- grad_w_qkv: float32 [1024, 3072], P(('dp', 'blk', 'head'))
- grad_b_qv: float32 [2, 1024], P(None, ('dp', 'blk', 'head'))
- grad_w_out: float32 [1024, 1024], P(('dp', 'blk', 'head'))
- grad_b_out: float32 [1024], P(('dp', 'blk', 'head'))
- grad_ln2_gain: float32 [1024], P(('dp', 'blk', 'head'))
- grad_ln2_bias: float32 [1024], P(('dp', 'blk', 'head'))
- grad_w_fc: float32 [1024, 4096], P(('dp', 'blk', 'head'))
- grad_b_fc: float32 [4096], P(('dp', 'blk', 'head'))
- grad_w_proj: float32 [4096, 1024], P(('dp', 'blk', 'head'))
- grad_b_proj: float32 [1024], P(('dp', 'blk', 'head'))
Inputs may be any that keep to these rules, and one draw needn't show every extreme that they name: `w_qkv`: entries are real numbers of order 1024 ** -0.5.
All inputs are finite; a program needn't handle non-finite values.
Results may differ from a plain program's by a relative error of at most 0.0095.
Values may be sent and summed in bfloat16 or wider, within the bound.
No kernel may reach another device: no remote copies, remote signals or barrier semaphores. Data moves between devices by JAX's collectives and lax.ppermute only.
A program may use at most 256 MiB of HBM per device.

v0:
```python
import math

import jax
import jax.numpy as jnp
from jax import lax
from jax.sharding import PartitionSpec as P

HD = 64


EPSILON = 1e-05
GELU_COEF = 0.044715
ROOT_TWO_PI = math.sqrt(2.0 / math.pi)


def passed_along(value, axis, steps):
    count = lax.axis_size(axis)
    initial, last = (max(0, -steps), min(count, count - steps))
    return lax.ppermute(value, axis, [(source, source + steps) for source in range(initial, last)])


def normalize(stream):
    centred = stream - jnp.mean(stream, axis=-1, keepdims=True)
    inv_std = lax.rsqrt(jnp.mean(centred * centred, axis=-1, keepdims=True) + EPSILON)
    return (centred * inv_std, inv_std)


def norm_back(grad_normed, normed, inv_std):
    return inv_std * (
        grad_normed
        - jnp.mean(grad_normed, axis=-1, keepdims=True)
        - normed * jnp.mean(grad_normed * normed, axis=-1, keepdims=True)
    )


def gelu_pair(pre_act):
    tangent = jnp.tanh(ROOT_TWO_PI * (pre_act + GELU_COEF * pre_act * pre_act * pre_act))
    value = 0.5 * pre_act * (1.0 + tangent)
    slope = 0.5 * (1.0 + tangent) + 0.5 * pre_act * (1.0 - tangent * tangent) * ROOT_TWO_PI * (
        1.0 + 3.0 * GELU_COEF * pre_act * pre_act
    )
    return (value, slope)


def matmul(left, right):
    return jnp.dot(left, right, preferred_element_type=jnp.float32)


def matmul_tn(left, right):
    return lax.dot_general(
        left, right, (((0,), (0,)), ((), ())), preferred_element_type=jnp.float32
    )


def matmul_nt(left, right):
    return lax.dot_general(
        left, right, (((1,), (1,)), ((), ())), preferred_element_type=jnp.float32
    )


def flatten(matrix):
    return matrix.reshape(-1, 128)


def block_scores(queries, keys_all, start, qblock, half_len, later):
    count = half_len + start + qblock
    scale = 1.0 / math.sqrt(HD)
    scores = (
        jnp.einsum(
            "shdq,shdk->shqk",
            queries[..., start : start + qblock],
            keys_all[..., :count],
            preferred_element_type=jnp.float32,
        )
        * scale
    )
    column = jnp.arange(count)[None, :]
    row_pos = start + jnp.arange(qblock)[:, None]
    own_ok = (column >= half_len) & (column - half_len <= row_pos)
    cross_ok = (column < half_len) & later
    return (jnp.where((own_ok | cross_ok)[None, None], scores, -jnp.inf), count)


def on_device(
    stream_in,
    ln1_gain,
    ln1_bias,
    w_qkv,
    b_qv,
    w_out,
    b_out,
    ln2_gain,
    ln2_bias,
    w_fc,
    b_fc,
    w_proj,
    b_proj,
    cotangent,
):
    seq_dev, tok_rows, width = stream_in.shape
    rows = seq_dev * tok_rows
    head_devs = lax.axis_size("head")
    group_width = width // head_devs
    heads_dev = group_width // HD
    scale = 1.0 / math.sqrt(HD)
    (
        full_g1,
        full_b1,
        flat_wqkv,
        full_bqv,
        flat_wout,
        full_bout,
        full_g2,
        full_b2,
        flat_wfc,
        full_bfc,
        flat_wproj,
        full_bproj,
    ) = (
        lax.all_gather(ln1_gain, ("dp", "blk", "head"), axis=0, tiled=True),
        lax.all_gather(ln1_bias, ("dp", "blk", "head"), axis=0, tiled=True),
        lax.all_gather(flatten(w_qkv), ("dp", "blk", "head"), axis=0, tiled=True),
        lax.all_gather(b_qv, ("dp", "blk", "head"), axis=1, tiled=True),
        lax.all_gather(flatten(w_out), ("dp", "blk", "head"), axis=0, tiled=True),
        lax.all_gather(b_out, ("dp", "blk", "head"), axis=0, tiled=True),
        lax.all_gather(ln2_gain, ("dp", "blk", "head"), axis=0, tiled=True),
        lax.all_gather(ln2_bias, ("dp", "blk", "head"), axis=0, tiled=True),
        lax.all_gather(flatten(w_fc), ("dp", "blk", "head"), axis=0, tiled=True),
        lax.all_gather(b_fc, ("dp", "blk", "head"), axis=0, tiled=True),
        lax.all_gather(flatten(w_proj), ("dp", "blk", "head"), axis=0, tiled=True),
        lax.all_gather(b_proj, ("dp", "blk", "head"), axis=0, tiled=True),
    )
    hidden_width = full_bfc.shape[0]
    full_wqkv = flat_wqkv.reshape(width, 3 * width)
    full_wout = flat_wout.reshape(width, width)
    full_wfc = flat_wfc.reshape(width, hidden_width)
    full_wproj = flat_wproj.reshape(hidden_width, width)
    stream_rows = stream_in.reshape(rows, width)
    normed_one, inv_one = normalize(stream_rows)
    act_one = (normed_one * full_g1.astype(jnp.float32) + full_b1.astype(jnp.float32)).astype(
        jnp.bfloat16
    )
    act_three = act_one.reshape(seq_dev, tok_rows, width)
    qkv_bias = jnp.concatenate(
        [
            full_bqv[0].astype(jnp.float32),
            jnp.zeros((width,), jnp.float32),
            full_bqv[1].astype(jnp.float32),
        ]
    )
    qkv_cols = (
        (
            jnp.einsum("std,de->set", act_three, full_wqkv, preferred_element_type=jnp.float32)
            + qkv_bias[None, :, None]
        )
        .astype(jnp.bfloat16)
        .reshape(seq_dev, 3, width, tok_rows)
    )
    qkv_heads = lax.all_to_all(qkv_cols, "head", split_axis=2, concat_axis=3, tiled=True)
    half_len = qkv_heads.shape[3]
    earlier = passed_along(qkv_heads[:, 1:3], "blk", 1)
    keys_all = jnp.concatenate([earlier[:, 0], qkv_heads[:, 1]], axis=2).reshape(
        seq_dev, heads_dev, HD, 2 * half_len
    )
    values_all = jnp.concatenate([earlier[:, 1], qkv_heads[:, 2]], axis=2).reshape(
        seq_dev, heads_dev, HD, 2 * half_len
    )
    queries = qkv_heads[:, 0].reshape(seq_dev, heads_dev, HD, half_len)
    later = lax.axis_index("blk") > 0
    qblock = min(512, half_len)
    out_blocks = []
    lse_blocks = []
    for start in range(0, half_len, qblock):
        scores, count = block_scores(queries, keys_all, start, qblock, half_len, later)
        top = jnp.max(scores, axis=-1, keepdims=True)
        lse = top + jnp.log(jnp.sum(jnp.exp(scores - top), axis=-1, keepdims=True))
        probs_low = jnp.exp(scores - lse).astype(jnp.bfloat16)
        result = jnp.einsum(
            "shqk,shdk->shdq",
            probs_low,
            values_all[..., :count],
            preferred_element_type=jnp.float32,
        )
        out_blocks.append(result.astype(jnp.bfloat16))
        lse_blocks.append(lse)
    attn_heads = jnp.concatenate(out_blocks, axis=3)
    attn_cols = lax.all_to_all(
        attn_heads.reshape(seq_dev, group_width, half_len),
        "head",
        split_axis=2,
        concat_axis=1,
        tiled=True,
    )
    resid = (
        stream_rows
        + jnp.einsum(
            "sdt,de->ste", attn_cols, full_wout, preferred_element_type=jnp.float32
        ).reshape(rows, width)
        + full_bout.astype(jnp.float32)
    )
    normed_two, inv_two = normalize(resid)
    ctx = (normed_two * full_g2.astype(jnp.float32) + full_b2.astype(jnp.float32)).astype(
        jnp.bfloat16
    )
    pre_act = matmul(ctx, full_wfc) + full_bfc.astype(jnp.float32)
    gelu_val, gelu_slope = gelu_pair(pre_act)
    hidden = gelu_val.astype(jnp.bfloat16)
    stream_out = resid + matmul(hidden, full_wproj) + full_bproj.astype(jnp.float32)
    back_g1, flat_bqkv, flat_bout, back_g2, flat_bfc, flat_bproj = (
        lax.all_gather(ln1_gain, ("dp", "blk", "head"), axis=0, tiled=True),
        lax.all_gather(flatten(w_qkv), ("dp", "blk", "head"), axis=0, tiled=True),
        lax.all_gather(flatten(w_out), ("dp", "blk", "head"), axis=0, tiled=True),
        lax.all_gather(ln2_gain, ("dp", "blk", "head"), axis=0, tiled=True),
        lax.all_gather(flatten(w_fc), ("dp", "blk", "head"), axis=0, tiled=True),
        lax.all_gather(flatten(w_proj), ("dp", "blk", "head"), axis=0, tiled=True),
    )
    back_wqkv = flat_bqkv.reshape(width, 3 * width)
    back_wout = flat_bout.reshape(width, width)
    back_wfc = flat_bfc.reshape(width, hidden_width)
    back_wproj = flat_bproj.reshape(hidden_width, width)
    gain_one = back_g1.astype(jnp.float32)
    gain_two = back_g2.astype(jnp.float32)
    cot_rows = cotangent.reshape(rows, width)
    cot_low = cot_rows.astype(jnp.bfloat16)
    grad_b_proj = jnp.sum(cot_rows, axis=0)
    grad_w_proj = matmul_tn(hidden, cot_low)
    grad_pre = matmul_nt(cot_low, back_wproj) * gelu_slope
    grad_b_fc = jnp.sum(grad_pre, axis=0)
    pre_low = grad_pre.astype(jnp.bfloat16)
    grad_w_fc = matmul_tn(ctx, pre_low)
    grad_ctx = matmul_nt(pre_low, back_wfc)
    grad_ln2_gain = jnp.sum(grad_ctx * normed_two, axis=0)
    grad_ln2_bias = jnp.sum(grad_ctx, axis=0)
    grad_resid = cot_rows + norm_back(grad_ctx * gain_two, normed_two, inv_two)
    grad_b_out = jnp.sum(grad_resid, axis=0)
    resid_low = grad_resid.astype(jnp.bfloat16)
    resid_three = resid_low.reshape(seq_dev, tok_rows, width)
    grad_w_out = jnp.einsum(
        "sdt,ste->de", attn_cols, resid_three, preferred_element_type=jnp.float32
    )
    grad_attn_cols = jnp.einsum(
        "ste,de->sdt", resid_three, back_wout, preferred_element_type=jnp.float32
    ).astype(jnp.bfloat16)
    grad_attn_heads = lax.all_to_all(
        grad_attn_cols, "head", split_axis=1, concat_axis=2, tiled=True
    ).reshape(seq_dev, heads_dev, HD, half_len)
    delta_all = jnp.sum(
        grad_attn_heads.astype(jnp.float32) * attn_heads.astype(jnp.float32), axis=2
    )
    grad_keys = jnp.zeros((seq_dev, heads_dev, HD, 2 * half_len), jnp.float32)
    grad_values = jnp.zeros((seq_dev, heads_dev, HD, 2 * half_len), jnp.float32)
    grad_queries = []
    for block_index, start in enumerate(range(0, half_len, qblock)):
        scores, count = block_scores(queries, keys_all, start, qblock, half_len, later)
        probs = jnp.exp(scores - lse_blocks[block_index])
        probs_low = probs.astype(jnp.bfloat16)
        grad_rows = grad_attn_heads[..., start : start + qblock]
        delta = delta_all[:, :, start : start + qblock][..., None]
        dprob = jnp.einsum(
            "shdq,shdk->shqk",
            grad_rows,
            values_all[..., :count],
            preferred_element_type=jnp.float32,
        )
        dscore = (probs * (dprob - delta) * scale).astype(jnp.bfloat16)
        grad_queries.append(
            jnp.einsum(
                "shqk,shdk->shdq", dscore, keys_all[..., :count], preferred_element_type=jnp.float32
            )
        )
        grad_keys = grad_keys.at[..., :count].add(
            jnp.einsum(
                "shqk,shdq->shdk",
                dscore,
                queries[..., start : start + qblock],
                preferred_element_type=jnp.float32,
            )
        )
        grad_values = grad_values.at[..., :count].add(
            jnp.einsum("shqk,shdq->shdk", probs_low, grad_rows, preferred_element_type=jnp.float32)
        )
    cross_terms = jnp.stack(
        [grad_keys[..., :half_len], grad_values[..., :half_len]], axis=1
    ).reshape(seq_dev, 2, group_width, half_len)
    returned = passed_along(cross_terms.astype(jnp.bfloat16), "blk", -1).astype(cross_terms.dtype)
    grad_k = grad_keys[..., half_len:].reshape(seq_dev, group_width, half_len) + returned[:, 0]
    grad_v = grad_values[..., half_len:].reshape(seq_dev, group_width, half_len) + returned[:, 1]
    grad_q = jnp.concatenate(grad_queries, axis=3).reshape(seq_dev, group_width, half_len)
    grad_heads_all = jnp.stack([grad_q, grad_k, grad_v], axis=1).astype(jnp.bfloat16)
    grad_qkv_four = lax.all_to_all(grad_heads_all, "head", split_axis=3, concat_axis=2, tiled=True)
    grad_qkv_cols = grad_qkv_four.reshape(seq_dev, 3 * width, tok_rows)
    grad_b_qv = jnp.stack(
        [
            jnp.sum(grad_qkv_four[:, 0].astype(jnp.float32), axis=(0, 2)),
            jnp.sum(grad_qkv_four[:, 2].astype(jnp.float32), axis=(0, 2)),
        ]
    )
    grad_w_qkv = jnp.einsum(
        "std,set->de", act_three, grad_qkv_cols, preferred_element_type=jnp.float32
    )
    grad_act = jnp.einsum(
        "set,de->std", grad_qkv_cols, back_wqkv, preferred_element_type=jnp.float32
    ).reshape(rows, width)
    grad_ln1_gain = jnp.sum(grad_act * normed_one, axis=0)
    grad_ln1_bias = jnp.sum(grad_act, axis=0)
    grad_rows_in = grad_resid + norm_back(grad_act * gain_one, normed_one, inv_one)
    shards = (
        lax.psum_scatter(grad_ln1_gain, ("dp", "blk", "head"), scatter_dimension=0, tiled=True),
        lax.psum_scatter(grad_ln1_bias, ("dp", "blk", "head"), scatter_dimension=0, tiled=True),
        lax.psum_scatter(
            flatten(grad_w_qkv), ("dp", "blk", "head"), scatter_dimension=0, tiled=True
        ),
        lax.psum_scatter(grad_b_qv, ("dp", "blk", "head"), scatter_dimension=1, tiled=True),
        lax.psum_scatter(
            flatten(grad_w_out), ("dp", "blk", "head"), scatter_dimension=0, tiled=True
        ),
        lax.psum_scatter(grad_b_out, ("dp", "blk", "head"), scatter_dimension=0, tiled=True),
        lax.psum_scatter(grad_ln2_gain, ("dp", "blk", "head"), scatter_dimension=0, tiled=True),
        lax.psum_scatter(grad_ln2_bias, ("dp", "blk", "head"), scatter_dimension=0, tiled=True),
        lax.psum_scatter(
            flatten(grad_w_fc), ("dp", "blk", "head"), scatter_dimension=0, tiled=True
        ),
        lax.psum_scatter(grad_b_fc, ("dp", "blk", "head"), scatter_dimension=0, tiled=True),
        lax.psum_scatter(
            flatten(grad_w_proj), ("dp", "blk", "head"), scatter_dimension=0, tiled=True
        ),
        lax.psum_scatter(grad_b_proj, ("dp", "blk", "head"), scatter_dimension=0, tiled=True),
    )
    return (
        stream_out.reshape(seq_dev, tok_rows, width),
        grad_rows_in.reshape(seq_dev, tok_rows, width),
        shards[0],
        shards[1],
        shards[2].reshape(-1, 3 * width),
        shards[3],
        shards[4].reshape(-1, width),
        shards[5],
        shards[6],
        shards[7],
        shards[8].reshape(-1, hidden_width),
        shards[9],
        shards[10].reshape(-1, width),
        shards[11],
    )


def solution(mesh):
    in_specs = (
        P("dp", ("blk", "head"), None),
        P(("dp", "blk", "head")),
        P(("dp", "blk", "head")),
        P(("dp", "blk", "head"), None),
        P(None, ("dp", "blk", "head")),
        P(("dp", "blk", "head"), None),
        P(("dp", "blk", "head")),
        P(("dp", "blk", "head")),
        P(("dp", "blk", "head")),
        P(("dp", "blk", "head"), None),
        P(("dp", "blk", "head")),
        P(("dp", "blk", "head"), None),
        P(("dp", "blk", "head")),
        P("dp", ("blk", "head"), None),
    )
    out_specs = (
        P("dp", ("blk", "head"), None),
        P("dp", ("blk", "head"), None),
        P(("dp", "blk", "head")),
        P(("dp", "blk", "head")),
        P(("dp", "blk", "head"), None),
        P(None, ("dp", "blk", "head")),
        P(("dp", "blk", "head"), None),
        P(("dp", "blk", "head")),
        P(("dp", "blk", "head")),
        P(("dp", "blk", "head")),
        P(("dp", "blk", "head"), None),
        P(("dp", "blk", "head")),
        P(("dp", "blk", "head"), None),
        P(("dp", "blk", "head")),
    )
    return jax.shard_map(
        on_device, mesh=mesh, in_specs=in_specs, out_specs=out_specs, check_vma=False
    )
```

profile of v0, /device:TPU:0, one launch (start us, length us, event | category | flops | bytes accessed | tf_op | source)
XLA Modules:
  0.0 1815.9 jit_solution(9376393486118762822)
XLA Ops:
  19.4 42.4 %all-reduce.16 = (bf16[1024]{0:T(1024)(128)(2,1)S(1)}, bf16[1024]{0:T(1024)(128)(2,1)S(1)}, bf16[1024]{0:T(1024)(128)(2,1)S(1)}, bf16[1024]{0:T(1024)(128)(2,1)}...) all-reduce(bf16[1024]{0:T(1024)(128)(2,1)S(1)} %dynamic-update-slic, ...), channel_id=1, replica_groups=mesh['dp'=4,'blk'=2,'head'=4] {'dp','blk','head'}, use_global_device_ids=true, to_apply=%add.3 | all-reduce | flops 6144 | bytes 24576
  65.1 66.2 %all-gather = bf16[32,32,2]{1,2,0:T(2,128)(2,1)S(1)} all-gather(bf16[1,32,2]{1,2,0:T(2,128)(2,1)S(1)} %bitcast.189), channel_id=1, replica_groups=mesh['dp'=4,'blk'=2,'head'=4] {'dp','blk','head'}, dimensions={0}, use_global_device_ids=true | all-gather | bytes 4224 | tf_op jit(solution)/shard_map/all_gather | solution.py:123
  156.1 43.0 %all_to_all.69 = bf16[2,3,1024,256]{3,0,1,2:T(2,128)(2,1)S(1)} all-to-all(bf16[2,3,1024,256]{3,0,1,2:T(2,128)(2,1)S(1)} %copy.103), channel_id=1, replica_groups=mesh['dp'=4,'blk'=2,'head'=4] {'head'}, dimensions={2} | all-to-all | bytes 6291456 | tf_op jit(solution)/shard_map/all_to_all | solution.py:159
  250.1 14.3 fusion.2
  264.4 15.1 exponential_reduce_fusion
  279.6 13.8 convolution_convert_fusion.2
  293.4 15.9 fusion.25
  316.5 66.8 %all-gather.1 = bf16[32,1,128]{2,1,0:T(2,128)(2,1)S(1)} all-gather(bf16[1,1,128]{2,1,0:T(2,128)(2,1)S(1)} %bitcast.190), channel_id=1, replica_groups=mesh['dp'=4,'blk'=2,'head'=4] {'dp','blk','head'}, dimensions={0}, use_global_device_ids=true | all-gather | bytes 8448 | tf_op jit(solution)/shard_map/all_gather | solution.py:129
  405.5 13.3 reshape.558
  438.7 13.5 fusion.61
  495.4 17.3 multiply_convert_fusion.1
  519.8 19.1 %pad_add_fusion = f32[2,4,64,2048]{3,2,1,0:T(8,128)} fusion(f32[2,4,64,1536]{3,2,1,0:T(8,128)} %fusion.30, bf16[2,4,64,1024]{3,2,1,0:T(8,128)(2,1)} %copy-done.21, f32[2,4,512,2048]{3,2,1,0:T(8,128)} %get-tuple-element.122, f32[2,4,512]{2,1,0:T(4,128)S(1)} %bitcast.174, pred[512,2048]{1,0:T(8,128)(4,1)} %and_or_fusion), kind=kOutput, calls=%fused_computation.23 | convolution fusion | flops 1108344832 | bytes 42483712 | tf_op jit(solution)/shard_map/shqk,shdq->shdk/dot_general | solution.py:280
  538.9 22.8 %multiply_convert_fusion = bf16[2,4,512,2048]{3,2,1,0:T(8,128)(2,1)} fusion(f32[2,4,512,2048]{3,2,1,0:T(8,128)} %get-tuple-element.122, f32[2,4,512]{2,1,0:T(4,128)S(1)} %get-tuple-element.113, f32[2,4,512]{2,1,0:T(4,128)S(1)} %bitcast.175, pred[512,2048]{1,0:T(8,128)(4,1)} %and_or_fusion, bf16[2,4,64,1024]{3,2,1,0:T(8,128)(2,1)} %bitcast.157, ...), kind=kOutput, calls=%fused_computation | convolution fusion | flops 1136656384 | bytes 54034432 | tf_op jit(solution)/shard_map/shdq,shdk->shqk/dot_general | solution.py:259
  604.2 41.5 %all_to_all.71 = bf16[2,3,256,1024]{2,0,1,3:T(2,128)(2,1)} all-to-all(bf16[2,3,256,1024]{2,0,1,3:T(2,128)(2,1)} %copy.116), channel_id=1, replica_groups=mesh['dp'=4,'blk'=2,'head'=4] {'head'}, dimensions={3} | all-to-all | bytes 6291456 | tf_op jit(solution)/shard_map/all_to_all | solution.py:290
  672.9 13.8 reshape.567
  686.8 15.8 fusion.55
  702.6 18.0 reshape.573
  721.3 13.5 fusion.17
  734.8 18.3 %reshape.571 = f32[32768,128]{1,0:T(8,128)} reshape(f32[1024,4096]{1,0:T(8,128)} %fusion.17) | data formatting | bytes 33554432 | tf_op jit(solution)/shard_map/reshape | solution.py:62
  789.9 39.1 %all-reduce.15 = (f32[1024]{0:T(1024)S(1)}, f32[1024]{0:T(1024)S(1)}, f32[1024]{0:T(1024)S(1)}, f32[1024]{0:T(1024)S(1)}, f32[1024]{0:T(1024)S(1)}, /*index=5*/f32[4096]{0:T(1024)S(1)}, f32[1024]{0:T(1024)S(1)}) all-reduce(f32[1024]{0:T(1024)S(1)} %get-tuple-element.80, ...), channel_id=2, replica_groups=mesh['dp'=4,'blk'=2,'head'=4] {'dp','blk','head'}, use_global_device_ids=true, to_apply=%region_14.15.clone | all-reduce | flops 10240 | bytes 81920
  838.7 87.1 %reduce-scatter.10.cloned.1.call-done = f32[256,128]{1,0:T(8,128)} async-done(((f32[8192,128]{1,0:T(8,128)}), f32[256,128]{1,0:T(8,128)}) %reduce-scatter.10.cloned.1.call-update) | async-done | bytes 131088 | tf_op jit(solution)/shard_map/reduce_scatter | solution.py:314
  927.4 159.3 %reduce-scatter.8.cloned.1.call-done = f32[768,128]{1,0:T(8,128)} async-done(((f32[24576,128]{1,0:T(8,128)}), f32[768,128]{1,0:T(8,128)}) %reduce-scatter.8.cloned.1.call-update) | async-done | bytes 393232 | tf_op jit(solution)/shard_map/reduce_scatter | solution.py:310
  1088.4 357.2 %reduce-scatter.14.cloned.1.call-done = f32[1024,128]{1,0:T(8,128)} async-done(((f32[32768,128]{1,0:T(8,128)}), f32[1024,128]{1,0:T(8,128)}) %reduce-scatter.14.cloned.1.call-update) | async-done | bytes 524304 | tf_op jit(solution)/shard_map/reduce_scatter | solution.py:324
  1447.6 359.4 %reduce-scatter.12.cloned.1.call-done = f32[1024,128]{1,0:T(8,128)} async-done(((f32[32768,128]{1,0:T(8,128)}), f32[1024,128]{1,0:T(8,128)}) %reduce-scatter.12.cloned.1.call-update) | async-done | bytes 524304 | tf_op jit(solution)/shard_map/reduce_scatter | solution.py:320
  (282 shorter events, 314.1 us)
Async XLA Ops:
  7.2 57.0 %copy-start = (f32[2,256,1024]{2,1,0:T(8,128)S(1)}, f32[2,256,1024]{2,1,0:T(8,128)}, u32[]{:S(2)}) copy-start(f32[2,256,1024]{2,1,0:T(8,128)} %param.26) | copy-start | bytes 6291460
  7.2 57.9 %copy-start.56 = (bf16[2,32]{1,0:T(2,128)(2,1)S(1)}, bf16[2,32]{1,0:T(2,128)(2,1)}, u32[]{:S(2)}) copy-start(bf16[2,32]{1,0:T(2,128)(2,1)} %param.30) | copy-start | bytes 388
  7.2 124.3 %all-gather.7.cloned.1.call-start = ((), (), s32[]{:S(2)}) async-start(), calls=%async_computation.9 | async-start | bytes 6488064 | tf_op jit(solution)/shard_map/all_gather | solution.py:122
  9.1 376.4 %all-gather.9.cloned.1.call-start = ((), (), s32[]{:S(2)}) async-start(), calls=%async_computation.10 | async-start | bytes 2162688 | tf_op jit(solution)/shard_map/all_gather | solution.py:124
  10.7 381.5 %all-gather.11.cloned.1.call-start = ((), (), s32[]{:S(2)}) async-start(), calls=%async_computation.11 | async-start | bytes 8650752 | tf_op jit(solution)/shard_map/all_gather | solution.py:128
  12.5 392.9 %all-gather.13.cloned.1.call-start = ((), (), s32[]{:S(2)}) async-start(), calls=%async_computation.12 | async-start | bytes 8650752 | tf_op jit(solution)/shard_map/all_gather | solution.py:130
  61.8 80.0 %copy-start.49 = (f32[1024]{0:T(1024)}, f32[1024]{0:T(1024)S(1)}, u32[]{:S(2)}) copy-start(f32[1024]{0:T(1024)S(1)} %convert_element_type.111) | copy-start | bytes 12292
  64.2 77.6 %copy-start.43 = (f32[2,256]{1,0:T(2,128)}, f32[2,256]{1,0:T(2,128)S(1)}, u32[]{:S(2)}) copy-start(f32[2,256]{1,0:T(2,128)S(1)} %get-tuple-element.120) | copy-start | bytes 6148
  65.1 76.7 %copy-start.54 = (f32[2,256]{1,0:T(2,128)}, f32[2,256]{1,0:T(2,128)S(1)}, u32[]{:S(2)}) copy-start(f32[2,256]{1,0:T(2,128)S(1)} %get-tuple-element.118) | copy-start | bytes 6148
  65.1 76.7 %copy-start.36 = (f32[1024]{0:T(1024)}, f32[1024]{0:T(1024)S(1)}, u32[]{:S(2)}) copy-start(f32[1024]{0:T(1024)S(1)} %convert_element_type.110) | copy-start | bytes 12292
  206.0 12.9 collective-permute-start
  309.3 73.9 %copy-start.10 = (f32[2,256,1024]{2,1,0:T(8,128)S(1)}, f32[2,256,1024]{2,1,0:T(8,128)}, u32[]{:S(2)}) copy-start(f32[2,256,1024]{2,1,0:T(8,128)} %param.39) | copy-start | bytes 6291460
  312.8 106.0 %all-to-all-start.1 = ((bf16[2,256,1024]{1,0,2:T(2,128)(2,1)}), bf16[2,256,1024]{1,0,2:T(2,128)(2,1)S(1)}, u32[]{:S(2)}, u32[]{:S(2)}) async-start(bf16[2,256,1024]{1,0,2:T(2,128)(2,1)} %copy.111), calls=%async_computation.1 | async-start | bytes 2097152 | tf_op jit(solution)/shard_map/all_to_all | solution.py:187
  316.4 521.0 %reduce-scatter.16.cloned.1.call-start = ((), (), s32[]{:S(2)}) async-start(), calls=%async_computation.17 | async-start | bytes 540672
  316.4 143.8 %copy-start.38 = (f32[1024]{0:T(1024)}, f32[1024]{0:T(1024)S(1)}, u32[]{:S(2)}) copy-start(f32[1024]{0:T(1024)S(1)} %convert_element_type.124) | copy-start | bytes 12292
  316.4 110.8 %copy-start.51 = (f32[1024]{0:T(1024)}, f32[1024]{0:T(1024)S(1)}, u32[]{:S(2)}) copy-start(f32[1024]{0:T(1024)S(1)} %convert_element_type.125) | copy-start | bytes 12292
  426.9 33.3 %copy-start.32 = (f32[512]{0:T(512)}, f32[512]{0:T(512)S(1)}, u32[]{:S(2)}) copy-start(f32[512]{0:T(512)S(1)} %broadcast_multiply_fusion.4) | copy-start | bytes 6148
  427.3 33.0 %copy-start.45 = (f32[512]{0:T(512)}, f32[512]{0:T(512)S(1)}, u32[]{:S(2)}) copy-start(f32[512]{0:T(512)S(1)} %add_rsqrt_fusion) | copy-start | bytes 6148
  572.9 21.2 %collective-permute-start.1 = (bf16[2,2,256,1024]{3,2,1,0:T(8,128)(2,1)}, bf16[2,2,256,1024]{3,2,1,0:T(8,128)(2,1)}, u32[]{:S(2)}, u32[]{:S(2)}) collective-permute-start(bf16[2,2,256,1024]{3,2,1,0:T(8,128)(2,1)} %pad_maximum_fusion.3), channel_id=1, source_target_pairs={{4,0},{5,1},{6,2},{7,3},{12,8},{13,9},{14,10},{15,11},{20,16},{21,... | collective-permute-start | bytes 6291464 | tf_op jit(solution)/shard_map/ppermute | solution.py:19
  654.1 271.7 %reduce-scatter.10.cloned.1.call-start = ((), (), s32[]{:S(2)}) async-start(), calls=%async_computation.14 | async-start | bytes 4325376 | tf_op jit(solution)/shard_map/reduce_scatter | solution.py:314
  663.8 422.8 %reduce-scatter.8.cloned.1.call-start = ((), (), s32[]{:S(2)}) async-start(), calls=%async_computation.13 | async-start | bytes 12976128 | tf_op jit(solution)/shard_map/reduce_scatter | solution.py:310
  686.8 758.9 %reduce-scatter.14.cloned.1.call-start = ((), (), s32[]{:S(2)}) async-start(), calls=%async_computation.16 | async-start | bytes 17301504 | tf_op jit(solution)/shard_map/reduce_scatter | solution.py:324
  720.7 1086.3 %reduce-scatter.12.cloned.1.call-start = ((), (), s32[]{:S(2)}) async-start(), calls=%async_computation.15 | async-start | bytes 17301504 | tf_op jit(solution)/shard_map/reduce_scatter | solution.py:320
  780.3 52.8 %copy-start.2 = (f32[2,256,1024]{2,1,0:T(8,128)S(1)}, f32[2,256,1024]{2,1,0:T(8,128)}, u32[]{:S(2)}) copy-start(f32[2,256,1024]{2,1,0:T(8,128)} %param.26) | copy-start | bytes 6291460
  (52 other events, 432.9 us)
Sparse Core Ops, SparseCore 0:
  11.5 72.3 all-gather.6
  87.3 55.0 all-gather.8
  145.3 86.6 all-gather.10
  235.3 76.1 all-gather.12
  654.2 131.6 reduce-scatter.15
  788.1 137.5 reduce-scatter.9
  932.8 153.7 reduce-scatter.7
  1088.9 356.6 reduce-scatter.13
  1448.0 358.9 reduce-scatter.11
where the time goes:
time: 1830 us; the launch traced here: 1820 us
  waiting for transfers between devices  963 us (53%)
  blocking collectives  311 us (17%)
  matrix products  274 us (15%)
  local copies, waits for them, and re-layouts  192 us (10%)
  other arithmetic  51.4 us (3%)
    reduce_scatter x1, waiting for transfers between devices, on_device(): lax.psum_scatter(flatten(grad_w_fc), ('dp', 'blk', 'head'), scatter_dimen...  359 us
    reduce_scatter x1, waiting for transfers between devices, on_device(): lax.psum_scatter(flatten(grad_w_proj), ('dp', 'blk', 'head'), scatter_dim...  357 us
    reduce_scatter x1, waiting for transfers between devices, on_device(): lax.psum_scatter(flatten(grad_w_qkv), ('dp', 'blk', 'head'), scatter_dime...  159 us
    reduce_scatter x1, waiting for transfers between devices, on_device(): lax.psum_scatter(flatten(grad_w_out), ('dp', 'blk', 'head'), scatter_dime...  87.1 us
    unnamed x2, blocking collectives  81.5 us
    all_gather x1, blocking collectives, on_device(): lax.all_gather(b_fc, ('dp', 'blk', 'head'), axis=0, tiled=True)  66.8 us
    all_gather x1, blocking collectives, on_device(): lax.all_gather(b_qv, ('dp', 'blk', 'head'), axis=1, tiled=True)  66.2 us
    reshape x8, local copies, waits for them, and re-layouts, flatten(): return matrix.reshape(-1, 128)  61.9 us
  transfers between devices with their start and end apart: 12, of which 4 were waited for; matrix products, arithmetic and copies ran while one was open for 19% of the time, Pallas kernels for 0%

commit v1 on v0

v1 whole, which is shorter than its diff:
```python
import functools
import math

import jax
import jax.numpy as jnp
from jax import lax
from jax.experimental import pallas as pl
from jax.experimental.pallas import tpu as pltpu
from jax.sharding import PartitionSpec as P

HD = 64
EPSILON = 1e-05
GELU_COEF = 0.044715
ROOT_TWO_PI = math.sqrt(2.0 / math.pi)
SCALE = 1.0 / math.sqrt(HD)
LOG2E = math.log2(math.e)
F32 = jnp.float32
BF16 = jnp.bfloat16
VMEM_LIMIT = 48 * 1024 * 1024


def normalize(stream):
    centred = stream - jnp.mean(stream, axis=-1, keepdims=True)
    inv_std = lax.rsqrt(jnp.mean(centred * centred, axis=-1, keepdims=True) + EPSILON)
    return (centred * inv_std, inv_std)


def norm_back(grad_normed, normed, inv_std):
    return inv_std * (
        grad_normed
        - jnp.mean(grad_normed, axis=-1, keepdims=True)
        - normed * jnp.mean(grad_normed * normed, axis=-1, keepdims=True)
    )


def gelu_pair(pre_act):
    tangent = jnp.tanh(ROOT_TWO_PI * (pre_act + GELU_COEF * pre_act * pre_act * pre_act))
    value = 0.5 * pre_act * (1.0 + tangent)
    slope = 0.5 * (1.0 + tangent) + 0.5 * pre_act * (1.0 - tangent * tangent) * ROOT_TWO_PI * (
        1.0 + 3.0 * GELU_COEF * pre_act * pre_act
    )
    return (value, slope)


def dot(left, right, left_dim, right_dim):
    return lax.dot_general(
        left, right, (((left_dim,), (right_dim,)), ((), ())), preferred_element_type=F32
    )


def to_xor(value, step):
    count = lax.axis_size("head")
    return lax.ppermute(value, "head", [(i, i ^ step) for i in range(count)])


def to_shift(value, step):
    count = lax.axis_size("dp")
    return lax.ppermute(value, "dp", [(i, (i + step) % count) for i in range(count)])


def to_other_core(value):
    return lax.ppermute(value, "blk", [(0, 1), (1, 0)])


def pick(stacked, index, axis=0):
    return lax.dynamic_index_in_dim(stacked, index, axis, keepdims=False)


def by_half(core, own, other):
    return jnp.where(core == 0, jnp.stack([own, other]), jnp.stack([other, own]))


def place_kernel(counts, ids, *refs):
    dp_count, _, head_count = counts
    pieces, out, sem = refs[: 2 * head_count], refs[2 * head_count], refs[2 * head_count + 1]
    dp, core, head = ids[0], ids[1], ids[2]
    copies = []
    for which in range(2):
        for slot in range(head_count):
            for step in range(dp_count):
                source = lax.rem(dp + (dp_count - step), dp_count)
                copies.append(
                    pltpu.make_async_copy(
                        pieces[which * head_count + slot].at[step],
                        out.at[source, core ^ which, head ^ slot],
                        sem.at[len(copies)],
                    )
                )
    for copy in copies:
        copy.start()
    for copy in copies:
        copy.wait()


def place(pieces, ids):
    counts = (lax.axis_size("dp"), 2, lax.axis_size("head"))
    shape = pieces[0].shape[1:]
    return pl.pallas_call(
        functools.partial(place_kernel, counts),
        out_shape=jax.ShapeDtypeStruct(counts + shape, pieces[0].dtype),
        grid_spec=pltpu.PrefetchScalarGridSpec(
            num_scalar_prefetch=1,
            grid=(1,),
            in_specs=[pl.BlockSpec(memory_space=pl.ANY)] * len(pieces),
            out_specs=pl.BlockSpec(memory_space=pl.ANY),
            scratch_shapes=[pltpu.SemaphoreType.DMA((counts[0] * 2 * counts[2],))],
        ),
        name="place",
    )(ids, *pieces)


def gather_z(shard):
    return jnp.stack([shard] + [to_shift(shard, k) for k in range(1, lax.axis_size("dp"))])


def gather_plane(own):
    return [own] + [to_xor(own, j) for j in range(1, lax.axis_size("head"))]


def gather_rows(shard, ids):
    mine = gather_plane(gather_z(shard))
    theirs = [to_other_core(piece) for piece in mine]
    return place(mine + theirs, ids)


def scatter_rows(grad, core, head, dp):
    dp_count, _, head_count = grad.shape[:3]
    plane = []
    for slot in range(head_count):
        row = pick(grad, head ^ slot, 2)
        arrived = to_other_core(pick(row, 1 - core, 1))
        both = pick(row, core, 1).astype(F32) + arrived.astype(F32)
        plane.append(both if slot == 0 else to_xor(both.astype(BF16), slot))
    total = plane[0]
    for piece in plane[1:]:
        total = total + piece.astype(F32)
    low = total.astype(BF16)
    result = pick(total, dp)
    for step in range(1, dp_count):
        result = result + to_shift(pick(low, lax.rem(dp + step, dp_count)), step).astype(F32)
    return result


def gather_small(vector, ids):
    dp_count, head_count = lax.axis_size("dp"), lax.axis_size("head")
    rows = gather_z(vector[None])
    rows = jnp.stack(gather_plane(rows))
    rows = jnp.stack([rows, to_other_core(rows)])
    total = 2 * head_count * dp_count
    slot = jnp.arange(total)
    which, plane, step = slot // (head_count * dp_count), (slot // dp_count) % head_count, slot % dp_count
    source = ((ids[0] - step) % dp_count) * 2 * head_count + (ids[1] ^ which) * head_count + (ids[2] ^ plane)
    chosen = (source[None, :] == jnp.arange(total)[:, None]).astype(F32)
    return jnp.dot(chosen, rows.reshape(total, -1), precision=lax.Precision.HIGHEST)


def scatter_small(rows, core, head, dp):
    dp_count, _, head_count = rows.shape[:3]
    half = pick(rows, core, 1) + to_other_core(pick(rows, 1 - core, 1))
    total = pick(half, head, 1)
    for slot in range(1, head_count):
        total = total + to_xor(pick(half, head ^ slot, 1), slot)
    result = pick(total, dp)
    for step in range(1, dp_count):
        result = result + to_shift(pick(total, lax.rem(dp + step, dp_count)), step)
    return result


SLOTS = 4


def causal(block):
    key = lax.broadcasted_iota(jnp.int32, (block, block), 0)
    query = lax.broadcasted_iota(jnp.int32, (block, block), 1)
    return key <= query


def forward_kernel(block, me_ref, qkv, out, lse, scores_a, scores_b):
    me = me_ref[0]
    factor = SCALE * LOG2E
    mask = causal(block)

    def part(which, pos):
        return qkv[(pos % SLOTS) ^ me, which, :, pl.ds((pos // SLOTS) * block, block)]

    for row in range(2 * SLOTS):
        scores = scores_a if row % 2 == 0 else scores_b
        query = part(0, row)
        top = None
        for col in range(row + 1):
            tile = dot(part(1, col), query, 0, 0)
            if col == row:
                tile = jnp.where(mask, tile, -jnp.inf)
            scores[pl.ds(col * block, block), :] = tile
            high = jnp.max(tile, axis=0, keepdims=True)
            top = high if top is None else jnp.maximum(top, high)
        shift = top * factor
        total = jnp.zeros_like(top)
        result = jnp.zeros((HD, block), F32)
        for col in range(row + 1):
            probs = jnp.exp2(scores[pl.ds(col * block, block), :] * factor - shift)
            total = total + jnp.sum(probs, axis=0, keepdims=True)
            result = result + dot(part(2, col), probs.astype(BF16), 1, 0)
        out[(row % SLOTS) ^ me, :, pl.ds((row // SLOTS) * block, block)] = (result / total).astype(BF16)
        lse[pl.ds(row, 1), :] = shift + jnp.log2(total)


def backward_kernel(block, me_ref, qkv, attn, grad_attn, lse, out, grad_q, delta):
    me = me_ref[0]
    factor = SCALE * LOG2E
    mask = causal(block)

    def part(which, pos):
        return qkv[(pos % SLOTS) ^ me, which, :, pl.ds((pos // SLOTS) * block, block)]

    def tokens(ref, pos):
        return ref[(pos % SLOTS) ^ me, :, pl.ds((pos // SLOTS) * block, block)]

    for row in range(2 * SLOTS):
        product = tokens(grad_attn, row).astype(F32) * tokens(attn, row).astype(F32)
        delta[pl.ds(row, 1), :] = jnp.sum(product, axis=0, keepdims=True)
    for col in range(2 * SLOTS):
        key, value = part(1, col), part(2, col)
        grad_key = jnp.zeros((HD, block), F32)
        grad_value = jnp.zeros((HD, block), F32)
        for row in range(col, 2 * SLOTS):
            query, grad_row = part(0, row), tokens(grad_attn, row)
            probs = jnp.exp2(dot(key, query, 0, 0) * factor - lse[pl.ds(row, 1), :])
            if row == col:
                probs = jnp.where(mask, probs, 0.0)
            grad_probs = dot(value, grad_row, 0, 0)
            grad_scores = (probs * (grad_probs - delta[pl.ds(row, 1), :])).astype(BF16)
            grad_value = grad_value + dot(grad_row, probs.astype(BF16), 1, 1)
            grad_key = grad_key + dot(query, grad_scores, 1, 1)
            term = dot(key, grad_scores, 1, 0)
            if col == 0:
                grad_q[row] = term
            else:
                grad_q[row] += term
        where = ((col % SLOTS) ^ me, pl.ds((col // SLOTS) * block, block))
        out[where[0], 1, :, where[1]] = (grad_key * SCALE).astype(BF16)
        out[where[0], 2, :, where[1]] = grad_value.astype(BF16)
    for row in range(2 * SLOTS):
        where = ((row % SLOTS) ^ me, pl.ds((row // SLOTS) * block, block))
        out[where[0], 0, :, where[1]] = (grad_q[row] * SCALE).astype(BF16)


def head_spec(width):
    return pl.BlockSpec((SLOTS, None, HD, width), lambda h, me: (0, h, 0, 0))


def triple_spec(width):
    return pl.BlockSpec((SLOTS, 3, None, HD, width), lambda h, me: (0, 0, h, 0, 0))


def attend(me, qkv):
    heads, width = qkv.shape[2], qkv.shape[4]
    block = width // 2
    length = SLOTS * width
    return pl.pallas_call(
        functools.partial(forward_kernel, block),
        out_shape=(
            jax.ShapeDtypeStruct((SLOTS, heads, HD, width), BF16),
            jax.ShapeDtypeStruct((heads, 2 * SLOTS, block), F32),
        ),
        grid_spec=pltpu.PrefetchScalarGridSpec(
            num_scalar_prefetch=1,
            grid=(heads,),
            in_specs=[triple_spec(width)],
            out_specs=(
                head_spec(width),
                pl.BlockSpec((None, 2 * SLOTS, block), lambda h, me: (h, 0, 0)),
            ),
            scratch_shapes=[pltpu.VMEM((length, block), F32)] * 2,
        ),
        compiler_params=pltpu.CompilerParams(vmem_limit_bytes=VMEM_LIMIT),
        cost_estimate=pl.CostEstimate(
            flops=2 * heads * length * length * HD,
            bytes_accessed=8 * heads * HD * length,
            transcendentals=heads * length * length // 2,
        ),
        name="attend",
    )(me, qkv)


def attend_back(me, qkv, attn, grad_attn, lse):
    heads, width = qkv.shape[2], qkv.shape[4]
    block = width // 2
    length = SLOTS * width
    return pl.pallas_call(
        functools.partial(backward_kernel, block),
        out_shape=jax.ShapeDtypeStruct(qkv.shape, BF16),
        grid_spec=pltpu.PrefetchScalarGridSpec(
            num_scalar_prefetch=1,
            grid=(heads,),
            in_specs=[
                triple_spec(width),
                head_spec(width),
                head_spec(width),
                pl.BlockSpec((None, 2 * SLOTS, block), lambda h, me: (h, 0, 0)),
            ],
            out_specs=triple_spec(width),
            scratch_shapes=[
                pltpu.VMEM((2 * SLOTS, HD, block), F32),
                pltpu.VMEM((2 * SLOTS, block), F32),
            ],
        ),
        compiler_params=pltpu.CompilerParams(vmem_limit_bytes=VMEM_LIMIT),
        cost_estimate=pl.CostEstimate(
            flops=5 * heads * length * length * HD,
            bytes_accessed=16 * heads * HD * length,
            transcendentals=heads * length * length // 2,
        ),
        name="attend_back",
    )(me, qkv, attn, grad_attn, lse)


def to_attention(slots, head):
    count, features, width = slots.shape
    if count == SLOTS:
        return head.reshape(1), slots
    order = jnp.arange(count) ^ head
    natural = slots[order].reshape(count, features, 2, width // 2)
    tokens = natural.transpose(1, 2, 0, 3).reshape(features, 2, SLOTS, -1)
    return jnp.zeros((1,), jnp.int32), tokens.transpose(2, 0, 1, 3).reshape(SLOTS, features, -1)


def from_attention(tokens, head, count):
    if count == SLOTS:
        return tokens
    features = tokens.shape[1]
    natural = tokens.reshape(SLOTS, features, 2, -1).transpose(1, 2, 0, 3)
    natural = natural.reshape(features, 2, count, -1).transpose(2, 0, 1, 3)
    return natural.reshape(count, features, -1)[jnp.arange(count) ^ head]


def on_device(
    stream_in,
    ln1_gain,
    ln1_bias,
    w_qkv,
    b_qv,
    w_out,
    b_out,
    ln2_gain,
    ln2_bias,
    w_fc,
    b_fc,
    w_proj,
    b_proj,
    cotangent,
):
    seq_dev, tok_rows, width = stream_in.shape
    rows = seq_dev * tok_rows
    dp_count, head_count = lax.axis_size("dp"), lax.axis_size("head")
    devices = dp_count * 2 * head_count
    grid = (dp_count, 2, head_count)
    dp, core, head = lax.axis_index("dp"), lax.axis_index("blk"), lax.axis_index("head")
    ids = jnp.stack([dp, core, head]).astype(jnp.int32)
    group = width // head_count
    heads = group // HD
    own_rows = w_qkv.shape[0]
    hidden_width = w_fc.shape[1]

    sizes = [own_rows] * 8 + [b_fc.shape[0]]
    small = jnp.concatenate(
        [ln1_gain, ln1_bias, b_qv[0], b_qv[1], b_out, ln2_gain, ln2_bias, b_proj, b_fc]
    ).astype(F32)
    small = gather_small(small, ids)
    edges = [sum(sizes[:i]) for i in range(len(sizes) + 1)]
    full = [small[:, edges[i] : edges[i + 1]].reshape(-1) for i in range(len(sizes))]
    gain_one, bias_one, bias_q, bias_v, bias_out, gain_two, bias_two, bias_proj, bias_fc = full

    stream_rows = stream_in.reshape(rows, width)
    normed_one, inv_one = normalize(stream_rows)
    act_one = (normed_one * gain_one + bias_one).astype(BF16).reshape(seq_dev, tok_rows, width)

    columns = w_qkv.reshape(own_rows, 3, head_count, group)
    parts = [
        pick(columns, head ^ slot, 2).reshape(own_rows, 3 * group) for slot in range(head_count)
    ]
    parts = [parts[0]] + [to_xor(parts[slot], slot) for slot in range(1, head_count)]
    shard = jnp.stack(parts)
    theirs_z = gather_z(shard)
    core_z = to_other_core(theirs_z)
    group_w = place(
        [theirs_z[:, slot] for slot in range(head_count)]
        + [core_z[:, slot] for slot in range(head_count)],
        ids,
    ).reshape(width, 3 * group)

    own_half = by_half(core, pick(act_one, core), to_other_core(pick(act_one, 1 - core)))
    own_half = own_half.reshape(2 * tok_rows, width)
    acts = gather_plane(own_half)
    qkv_bias = jnp.concatenate(
        [
            pick(bias_q.reshape(head_count, group), head),
            jnp.zeros((group,), F32),
            pick(bias_v.reshape(head_count, group), head),
        ]
    )[:, None]
    qkv_slots = jnp.stack([(dot(group_w, act, 0, 1) + qkv_bias).astype(BF16) for act in acts])
    me, qkv = to_attention(qkv_slots, head)
    qkv = qkv.reshape(SLOTS, 3, heads, HD, -1)
    attn, lse = attend(me, qkv)

    full_wout = gather_rows(w_out, ids).reshape(width, width)
    full_wfc = gather_rows(w_fc, ids).reshape(width, hidden_width)
    full_wproj = gather_rows(w_proj, ids).reshape(hidden_width, width)

    attn_slots = from_attention(attn.reshape(SLOTS, group, -1), head, head_count)
    attn_all = jnp.zeros((head_count, group, 2 * tok_rows), BF16)
    for slot in range(head_count):
        piece = attn_slots[slot]
        piece = to_xor(piece, slot) if slot else piece
        attn_all = lax.dynamic_update_index_in_dim(attn_all, piece, head ^ slot, 0)
    attn_all = attn_all.reshape(width, 2, tok_rows)
    attn_all = attn_all.reshape(width, 2 * tok_rows)
    first, second = attn_all[:, :tok_rows], attn_all[:, tok_rows:]
    keep = jnp.where(core == 0, first, second)
    away = jnp.where(core == 0, second, first)
    attn_cols = by_half(core, keep, to_other_core(away))

    resid = (
        stream_rows
        + jnp.einsum("sdt,de->ste", attn_cols, full_wout, preferred_element_type=F32).reshape(
            rows, width
        )
        + bias_out
    )
    normed_two, inv_two = normalize(resid)
    ctx = (normed_two * gain_two + bias_two).astype(BF16)
    pre_act = dot(ctx, full_wfc, 1, 0) + bias_fc
    gelu_val, gelu_slope = gelu_pair(pre_act)
    hidden = gelu_val.astype(BF16)
    stream_out = resid + dot(hidden, full_wproj, 1, 0) + bias_proj

    cot_rows = cotangent.reshape(rows, width)
    cot_low = cot_rows.astype(BF16)
    grad_b_proj = jnp.sum(cot_rows, axis=0)
    grad_w_proj = dot(hidden, cot_low, 0, 0).astype(BF16)
    grad_pre = dot(cot_low, full_wproj, 1, 1) * gelu_slope
    grad_b_fc = jnp.sum(grad_pre, axis=0)
    pre_low = grad_pre.astype(BF16)
    grad_w_fc = dot(ctx, pre_low, 0, 0).astype(BF16)
    grad_ctx = dot(pre_low, full_wfc, 1, 1)
    grad_ln2_gain = jnp.sum(grad_ctx * normed_two, axis=0)
    grad_ln2_bias = jnp.sum(grad_ctx, axis=0)
    grad_resid = cot_rows + norm_back(grad_ctx * gain_two, normed_two, inv_two)
    grad_b_out = jnp.sum(grad_resid, axis=0)
    resid_low = grad_resid.astype(BF16)
    resid_three = resid_low.reshape(seq_dev, tok_rows, width)
    grad_w_out = jnp.einsum(
        "sdt,ste->de", attn_cols, resid_three, preferred_element_type=F32
    ).astype(BF16)
    grad_attn_cols = jnp.einsum(
        "ste,de->sdt", resid_three, full_wout, preferred_element_type=F32
    ).astype(BF16)

    shard_wproj = scatter_rows(grad_w_proj.reshape(grid + (-1, width)), core, head, dp)
    shard_wfc = scatter_rows(grad_w_fc.reshape(grid + (-1, hidden_width)), core, head, dp)
    shard_wout = scatter_rows(grad_w_out.reshape(grid + (-1, width)), core, head, dp)

    kept = pick(grad_attn_cols, core)
    arrived = to_other_core(pick(grad_attn_cols, 1 - core))
    grad_half = jnp.where(
        core == 0,
        jnp.concatenate([kept, arrived], axis=1),
        jnp.concatenate([arrived, kept], axis=1),
    ).reshape(head_count, group, 2 * tok_rows)
    grad_slots = jnp.stack(
        [pick(grad_half, head)]
        + [to_xor(pick(grad_half, head ^ slot), slot) for slot in range(1, head_count)]
    )
    _, grad_attn = to_attention(grad_slots, head)
    grad_attn = grad_attn.reshape(SLOTS, heads, HD, -1)
    grad_qkv = attend_back(me, qkv, attn, grad_attn, lse)
    grad_qkv = from_attention(grad_qkv.reshape(SLOTS, 3 * group, -1), head, head_count)

    grad_act_slots = [
        dot(grad_qkv[slot], group_w, 0, 1).astype(BF16) for slot in range(head_count)
    ]
    sums = grad_act_slots[0].astype(F32)
    for slot in range(1, head_count):
        sums = sums + to_xor(grad_act_slots[slot], slot).astype(F32)
    sums = sums.reshape(2, tok_rows, width)
    grad_act = by_half(
        core, pick(sums, core), to_other_core(pick(sums, 1 - core))
    ).reshape(rows, width)

    grad_group_w = dot(acts[0], grad_qkv[0], 0, 1)
    for slot in range(1, head_count):
        grad_group_w = grad_group_w + dot(acts[slot], grad_qkv[slot], 0, 1)
    grad_group_w = grad_group_w.astype(BF16).reshape(grid + (own_rows, 3 * group))
    half_w = pick(grad_group_w, core, 1).astype(F32) + to_other_core(
        pick(grad_group_w, 1 - core, 1)
    ).astype(F32)
    half_low = half_w.astype(BF16)
    shard_w = pick(half_w, dp)
    for step in range(1, dp_count):
        shard_w = shard_w + to_shift(pick(half_low, lax.rem(dp + step, dp_count)), step).astype(F32)
    shard_wqkv = jnp.zeros((own_rows, 3, head_count, group), F32)
    for slot in range(head_count):
        piece = pick(shard_w, head ^ slot)
        piece = to_xor(piece, slot) if slot else piece
        shard_wqkv = lax.dynamic_update_index_in_dim(
            shard_wqkv, piece.reshape(own_rows, 3, group), head ^ slot, 2
        )
    shard_wqkv = shard_wqkv.reshape(own_rows, 3 * width)

    token_sums = jnp.sum(grad_qkv.astype(F32), axis=(0, 2)).reshape(3, group)
    grad_bias = jnp.zeros((3, head_count, group), F32)
    grad_bias = lax.dynamic_update_index_in_dim(grad_bias, token_sums, head, 1).reshape(3, width)

    grad_ln1_gain = jnp.sum(grad_act * normed_one, axis=0)
    grad_ln1_bias = jnp.sum(grad_act, axis=0)
    grad_rows_in = grad_resid + norm_back(grad_act * gain_one, normed_one, inv_one)

    vectors = [
        grad_ln1_gain,
        grad_ln1_bias,
        grad_bias[0],
        grad_bias[2],
        grad_b_out,
        grad_ln2_gain,
        grad_ln2_bias,
        grad_b_proj,
        grad_b_fc,
    ]
    packed = jnp.concatenate([v.reshape(devices, -1) for v in vectors], axis=1)
    mine = scatter_small(packed.reshape(grid + (-1,)), core, head, dp)
    cut = [mine[edges[i] : edges[i + 1]] for i in range(len(sizes))]
    return (
        stream_out.reshape(seq_dev, tok_rows, width),
        grad_rows_in.reshape(seq_dev, tok_rows, width),
        cut[0],
        cut[1],
        shard_wqkv,
        jnp.stack([cut[2], cut[3]]),
        shard_wout.reshape(-1, width),
        cut[4],
        cut[5],
        cut[6],
        shard_wfc.reshape(-1, hidden_width),
        cut[8],
        shard_wproj.reshape(-1, width),
        cut[7],
    )


def solution(mesh):
    every = ("dp", "blk", "head")
    tokens = P("dp", ("blk", "head"), None)
    vector, matrix = P(every), P(every, None)
    in_specs = (
        tokens,
        vector,
        vector,
        matrix,
        P(None, every),
        matrix,
        vector,
        vector,
        vector,
        matrix,
        vector,
        matrix,
        vector,
        tokens,
    )
    out_specs = (
        tokens,
        tokens,
        vector,
        vector,
        matrix,
        P(None, every),
        matrix,
        vector,
        vector,
        vector,
        matrix,
        vector,
        matrix,
        vector,
    )
    return jax.shard_map(
        on_device, mesh=mesh, in_specs=in_specs, out_specs=out_specs, check_vma=False
    )
```

time: 1830 us -> 1270 us (0.69)
  waiting for transfers between devices: 963 us -> 244 us
  Pallas kernels: 0 us -> 685 us
  blocking collectives: 311 us -> 0 us
  matrix products: 274 us -> 91.6 us
  local copies, waits for them, and re-layouts: 192 us -> 84.9 us
  starting transfers between devices: 8.5 us -> 98.7 us
    reduce_scatter x4 -> x0, waiting for transfers between devices: 963 us -> none  [the longest x1 359 us: on_device(): lax.psum_scatter(flatten(grad_w_fc), ('dp', 'blk', 'head'), scatter_dimen...]
    pallas_call x0 -> x6, Pallas kernels: none -> 685 us  [the longest x4 628 us: place(): pl.pallas_call(functools.partial(place_kernel, counts), out_shape=jax.Sha...]
    ppermute x2 -> x104, waiting for transfers between devices: 0.01 us -> 244 us  [the longest x42 169 us: to_xor(): return lax.ppermute(value, 'head', [(i, i ^ step) for i in range(count)])]
    dot_general x23 -> x21, matrix products: 269 us -> 90.3 us  [the longest x18 85.8 us: dot(): lax.dot_general(left, right, (((left_dim,), (right_dim,)), ((), ())), pre...]
    all_gather x2 -> x0, blocking collectives: 133 us -> none  [the longest x1 66.8 us: on_device(): lax.all_gather(b_fc, ('dp', 'blk', 'head'), axis=0, tiled=True)]
    reshape x21 -> x3, local copies, waits for them, and re-layouts: 129 us -> 2.03 us  [the longest x1 1.06 us: on_device(): columns = w_qkv.reshape(own_rows, 3, head_count, group)]
    all_to_all x3 -> x0, blocking collectives: 97 us -> none  [the longest x1 43 us: on_device(): lax.all_to_all(qkv_cols, 'head', split_axis=2, concat_axis=3, tiled=True)]
    ppermute x2 -> x104, starting transfers between devices: 4.4 us -> 98.7 us  [the longest x42 48.1 us: to_xor(): return lax.ppermute(value, 'head', [(i, i ^ step) for i in range(count)])]
  transfers between devices with their start and end apart: 12 -> 104, of which waited for: 4 -> 29; matrix products, arithmetic and copies ran while one was open for 19% -> 14% of each run, Pallas kernels for 0% -> 54%
where the time goes in v1:
time: 1270 us; the launch traced here: 1260 us
  Pallas kernels  685 us (54%)
  waiting for transfers between devices  244 us (19%)
  starting transfers between devices  98.7 us (8%)
  matrix products  91.6 us (7%)
  local copies, waits for them, and re-layouts  84.9 us (7%)
  other arithmetic  56.3 us (4%)
    pallas_call x4, Pallas kernels, place(): pl.pallas_call(functools.partial(place_kernel, counts), out_shape=jax.Sha...  628 us
    ppermute x42, waiting for transfers between devices, to_xor(): return lax.ppermute(value, 'head', [(i, i ^ step) for i in range(count)])  169 us
    dot_general x18, matrix products, dot(): lax.dot_general(left, right, (((left_dim,), (right_dim,)), ((), ())), pre...  85.8 us
    ppermute x30, waiting for transfers between devices, to_shift(): lax.ppermute(value, 'dp', [(i, (i + step) % count) for i in range(count)])  71.7 us
    ppermute x42, starting transfers between devices, to_xor(): return lax.ppermute(value, 'head', [(i, i ^ step) for i in range(count)])  48.1 us
    ppermute x30, starting transfers between devices, to_shift(): lax.ppermute(value, 'dp', [(i, (i + step) % count) for i in range(count)])  44.5 us
    pallas_call x1, Pallas kernels, attend_back(): pl.pallas_call(functools.partial(backward_kernel, block), out_shape=jax.S...  38.2 us
    dynamic_update_slice x4, local copies, waits for them, and re-layouts, on_device(): attn_all = lax.dynamic_update_index_in_dim(attn_all, piece, head ^ slot, 0)  29.8 us
  transfers between devices with their start and end apart: 104, of which 29 were waited for; matrix products, arithmetic and copies ran while one was open for 14% of the time, Pallas kernels for 54%

profile of v1, /device:TPU:0, one launch (start us, length us, event | category | flops | bytes accessed | tf_op | source)
XLA Modules:
  0.0 1262.6 jit_solution(4413294103330002030)
XLA Ops:
  46.2 14.2 %collective-permute-done.4 = bf16[4,32,768]{2,1,0:T(8,128)(2,1)S(1)} collective-permute-done((bf16[4,32,768]{2,1,0:T(8,128)(2,1)S(1)}, bf16[4,32,768]{2,1,0:T(8,128)(2,1)S(1)}, u32[]{:S(2)}, u32[]{:S(2)}) %collective-permute-start.4) | collective-permute-done | bytes 196640 | tf_op jit(solution)/shard_map/ppermute | solution.py:58
  65.4 11.0 collective-permute-done.43
  82.3 13.9 %collective-permute-done.33 = bf16[32,4096]{1,0:T(8,128)(2,1)S(1)} collective-permute-done((bf16[32,4096]{1,0:T(8,128)(2,1)}, bf16[32,4096]{1,0:T(8,128)(2,1)S(1)}, u32[]{:S(2)}, u32[]{:S(2)}) %collective-permute-start.33) | collective-permute-done | bytes 262176 | tf_op jit(solution)/shard_map/ppermute | solution.py:58
  113.8 49.7 %place.4 = bf16[4,2,4,32,768]{4,3,2,1,0:T(8,128)(2,1)} custom-call(s32[3]{0:T(128)} %pad_add_fusion.ids, bf16[4,32,768]{2,1,0:T(8,128)(2,1)} %get-tuple-element.105.refs_0_, bf16[4,32,768]{2,1,0:T(8,128)(2,1)} %get-tuple-element.104.refs_1_, bf16[4,32,768]{2,1,0:T(8,128)(2,1)} %get-tuple-element.103.refs_2_, bf16[4,32,768]{2,1,0:T(8,128)(2,1)} %get-tuple-element.102.refs_3_, ...), custom_call_target="tpu_custom_call" | custom-call | tf_op jit(solution)/shard_map/place/pallas_call | solution.py:98
  173.1 29.5 %collective-permute-done.46.refs_2_ = bf16[4,128,1024]{2,1,0:T(8,128)(2,1)} collective-permute-done((bf16[4,128,1024]{2,1,0:T(8,128)(2,1)S(1)}, bf16[4,128,1024]{2,1,0:T(8,128)(2,1)}, u32[]{:S(2)}, u32[]{:S(2)}) %collective-permute-start.46) | collective-permute-done | bytes 1048608 | tf_op jit(solution)/shard_map/ppermute | solution.py:53
  208.0 18.8 %attend.1 = (bf16[4,4,64,512]{3,2,1,0:T(8,128)(2,1)S(1)}, f32[4,8,256]{2,1,0:T(8,128)S(1)}) custom-call(s32[1]{0:T(128)} %bitcast.1.me_ref, bf16[4,3,4,64,512]{4,3,2,1,0:T(8,128)(2,1)S(1)} %pad_maximum_fusion.qkv), custom_call_target="tpu_custom_call" | custom-call | flops 2147483648 | bytes 4194304 | tf_op jit(solution)/shard_map/attend/pallas_call | solution.py:260
  228.5 21.3 %collective-permute-done.36.refs_2_ = bf16[4,32,4096]{2,1,0:T(8,128)(2,1)} collective-permute-done((bf16[4,32,4096]{2,1,0:T(8,128)(2,1)S(1)}, bf16[4,32,4096]{2,1,0:T(8,128)(2,1)}, u32[]{:S(2)}, u32[]{:S(2)}) %collective-permute-start.36) | collective-permute-done | bytes 1048608 | tf_op jit(solution)/shard_map/ppermute | solution.py:53
  283.5 9.7 dynamic_update_slice.32
  304.5 65.6 %place.5 = bf16[4,2,4,32,1024]{4,3,2,1,0:T(8,128)(2,1)} custom-call(s32[3]{0:T(128)} %pad_add_fusion.ids, bf16[4,32,1024]{2,1,0:T(8,128)(2,1)} %copy-done.38, bf16[4,32,1024]{2,1,0:T(8,128)(2,1)} %copy-done.40, bf16[4,32,1024]{2,1,0:T(8,128)(2,1)} %copy-done.41, bf16[4,32,1024]{2,1,0:T(8,128)(2,1)} %copy-done.42, bf16[4,32,1024]{2,1,0:T(8,128)(2,1)} %copy-done.43, ...), custom_call_target="tpu_custom_call" | custom-call | tf_op jit(solution)/shard_map/place/pallas_call | solution.py:98
  370.1 256.2 %place.7 = bf16[4,2,4,128,1024]{4,3,2,1,0:T(8,128)(2,1)} custom-call(s32[3]{0:T(128)} %pad_add_fusion.ids, bf16[4,128,1024]{2,1,0:T(8,128)(2,1)} %copy-done.13, bf16[4,128,1024]{2,1,0:T(8,128)(2,1)} %collective-permute-done.45.refs_1_, bf16[4,128,1024]{2,1,0:T(8,128)(2,1)} %collective-permute-done.46.refs_2_, ...), custom_call_target="tpu_custom_call" | custom-call | tf_op jit(solution)/shard_map/place/pallas_call | solution.py:98
  626.4 256.3 %place.6 = bf16[4,2,4,32,4096]{4,3,2,1,0:T(8,128)(2,1)} custom-call(s32[3]{0:T(128)} %pad_add_fusion.ids, bf16[4,32,4096]{2,1,0:T(8,128)(2,1)} %copy-done.14, bf16[4,32,4096]{2,1,0:T(8,128)(2,1)} %collective-permute-done.35.refs_1_, bf16[4,32,4096]{2,1,0:T(8,128)(2,1)} %collective-permute-done.36.refs_2_, ...), custom_call_target="tpu_custom_call" | custom-call | tf_op jit(solution)/shard_map/place/pallas_call | solution.py:98
  888.3 7.5 fusion.62
  895.9 10.4 add_add_fusion
  906.2 13.3 %fusion.77 = (f32[4096]{0:T(1024)}, bf16[512,4096]{1,0:T(8,128)(2,1)}) fusion(f32[512,4096]{1,0:T(8,128)} %fusion.62, f32[4096]{0:T(1024)S(1)} %slice_bitcast_fusion.8, bf16[4096,1024]{1,0:T(8,128)(2,1)S(1)} %bitcast.399, bf16[512,1024]{1,0:T(8,128)(2,1)S(1)} %bitcast.437), kind=kOutput, calls=%fused_computation.240 | convolution fusion | flops 4339003392 | bytes 22052864 | tf_op jit(solution)/shard_map/dot_general | solution.py:46
  919.5 7.8 multiply_reduce_fusion
  935.0 9.9 convolution_convert_fusion
  945.0 10.3 convolution_convert_fusion.1
  993.6 38.2 %attend_back.1 = bf16[4,3,4,64,512]{4,3,2,1,0:T(8,128)(2,1)S(1)} custom-call(s32[1]{0:T(128)} %bitcast.1.me_ref, bf16[4,3,4,64,512]{4,3,2,1,0:T(8,128)(2,1)} %copy-done, bf16[4,4,64,512]{3,2,1,0:T(8,128)(2,1)S(1)} %copy-done.2, bf16[4,4,64,512]{3,2,1,0:T(8,128)(2,1)S(1)} %pad_maximum_fusion.3.grad_attn, f32[4,8,256]{2,1,0:T(8,128)S(1)} %get-tuple-element.17.lse), custom_call_target="tpu_custom_call" | custom-call | flops 5368709120 | bytes 8388608 | tf_op jit(solution)/shard_map/attend_back/pallas_call | solution.py:290
  1066.7 8.9 collective-permute-done.69
  1085.0 15.8 %collective-permute-done.57 = bf16[512,1024]{1,0:T(8,128)(2,1)S(1)} collective-permute-done((bf16[512,1024]{1,0:T(8,128)(2,1)S(1)}, bf16[512,1024]{1,0:T(8,128)(2,1)S(1)}, u32[]{:S(2)}, u32[]{:S(2)}) %collective-permute-start.57) | collective-permute-done | bytes 1048608 | tf_op jit(solution)/shard_map/ppermute | solution.py:53
  1102.1 21.1 %collective-permute-done.100 = bf16[4,128,1024]{2,1,0:T(8,128)(2,1)S(1)} collective-permute-done((bf16[4,128,1024]{2,1,0:T(8,128)(2,1)S(1)}, bf16[4,128,1024]{2,1,0:T(8,128)(2,1)S(1)}, u32[]{:S(2)}, u32[]{:S(2)}) %collective-permute-start.100) | collective-permute-done | bytes 1048608 | tf_op jit(solution)/shard_map/ppermute | solution.py:53
  1124.7 21.0 %collective-permute-done.98 = bf16[4,128,1024]{2,1,0:T(8,128)(2,1)S(1)} collective-permute-done((bf16[4,128,1024]{2,1,0:T(8,128)(2,1)S(1)}, bf16[4,128,1024]{2,1,0:T(8,128)(2,1)S(1)}, u32[]{:S(2)}, u32[]{:S(2)}) %collective-permute-start.98) | collective-permute-done | bytes 1048608 | tf_op jit(solution)/shard_map/ppermute | solution.py:53
  1169.6 20.3 %collective-permute-done.88 = bf16[4,32,4096]{2,1,0:T(8,128)(2,1)} collective-permute-done((bf16[4,32,4096]{2,1,0:T(8,128)(2,1)}, bf16[4,32,4096]{2,1,0:T(8,128)(2,1)}, u32[]{:S(2)}, u32[]{:S(2)}) %collective-permute-start.88) | collective-permute-done | bytes 1048608 | tf_op jit(solution)/shard_map/ppermute | solution.py:53
  1222.7 15.9 %collective-permute-done.92 = bf16[32,4096]{1,0:T(8,128)(2,1)} collective-permute-done((bf16[32,4096]{1,0:T(8,128)(2,1)}, bf16[32,4096]{1,0:T(8,128)(2,1)}, u32[]{:S(2)}, u32[]{:S(2)}) %collective-permute-start.92) | collective-permute-done | bytes 262176 | tf_op jit(solution)/shard_map/ppermute | solution.py:58
  (536 shorter events, 313.5 us)
Async XLA Ops:
  35.8 62.9 %collective-permute-start.14 = (bf16[256,1024]{1,0:T(8,128)(2,1)S(1)}, bf16[256,1024]{1,0:T(8,128)(2,1)S(1)}, u32[]{:S(2)}, u32[]{:S(2)}) collective-permute-start(bf16[256,1024]{1,0:T(8,128)(2,1)S(1)} %get-tuple-element.94), channel_id=1, source_target_pairs={{0,4},{4,0},{1,5},{5,1},{2,6},{6,2},{3,7},{7,3},{8,12},{12,8},{9,1... | collective-permute-start | bytes 1572872 | tf_op jit(solution)/shard_map/ppermute | solution.py:62
  102.2 61.3 %collective-permute-start.45 = (bf16[4,128,1024]{2,1,0:T(8,128)(2,1)S(1)}, bf16[4,128,1024]{2,1,0:T(8,128)(2,1)}, u32[]{:S(2)}, u32[]{:S(2)}) collective-permute-start(bf16[4,128,1024]{2,1,0:T(8,128)(2,1)S(1)} %pad_maximum_fusion.2.refs_0_), channel_id=1, source_target_pairs={{0,1},{1,0},{2,3},{3,2},{4,5},{5,4},{6,7},{7,6},{8,9},{9,8},{10,11... | collective-permute-start | bytes 3145736 | tf_op jit(solution)/shard_map/ppermute | solution.py:53
  104.8 61.0 %collective-permute-start.17 = (bf16[512,1024]{1,0:T(8,128)(2,1)S(1)}, bf16[512,1024]{1,0:T(8,128)(2,1)}, u32[]{:S(2)}, u32[]{:S(2)}) collective-permute-start(bf16[512,1024]{1,0:T(8,128)(2,1)S(1)} %bitcast.404), channel_id=1, source_target_pairs={{0,3},{1,2},{2,1},{3,0},{4,7},{5,6},{6,5},{7,4},{8,11},{9,10},{10,... | collective-permute-start | bytes 3145736 | tf_op jit(solution)/shard_map/ppermute | solution.py:53
  109.6 61.0 %collective-permute-start.16 = (bf16[512,1024]{1,0:T(8,128)(2,1)S(1)}, bf16[512,1024]{1,0:T(8,128)(2,1)}, u32[]{:S(2)}, u32[]{:S(2)}) collective-permute-start(bf16[512,1024]{1,0:T(8,128)(2,1)S(1)} %bitcast.405), channel_id=1, source_target_pairs={{0,2},{1,3},{2,0},{3,1},{4,6},{5,7},{6,4},{7,5},{8,10},{9,11},{10,... | collective-permute-start | bytes 3145736 | tf_op jit(solution)/shard_map/ppermute | solution.py:53
  111.5 91.1 %collective-permute-start.46 = (bf16[4,128,1024]{2,1,0:T(8,128)(2,1)S(1)}, bf16[4,128,1024]{2,1,0:T(8,128)(2,1)}, u32[]{:S(2)}, u32[]{:S(2)}) collective-permute-start(bf16[4,128,1024]{2,1,0:T(8,128)(2,1)S(1)} %pad_maximum_fusion.2.refs_0_), channel_id=1, source_target_pairs={{0,2},{1,3},{2,0},{3,1},{4,6},{5,7},{6,4},{7,5},{8,10},{9,11},{10,... | collective-permute-start | bytes 3145736 | tf_op jit(solution)/shard_map/ppermute | solution.py:53
  112.9 90.2 %collective-permute-start.15 = (bf16[512,1024]{1,0:T(8,128)(2,1)S(1)}, bf16[512,1024]{1,0:T(8,128)(2,1)}, u32[]{:S(2)}, u32[]{:S(2)}) collective-permute-start(bf16[512,1024]{1,0:T(8,128)(2,1)S(1)} %bitcast.406), channel_id=1, source_target_pairs={{0,1},{1,0},{2,3},{3,2},{4,5},{5,4},{6,7},{7,6},{8,9},{9,8},{10,11... | collective-permute-start | bytes 3145736 | tf_op jit(solution)/shard_map/ppermute | solution.py:53
  170.6 56.2 %collective-permute-start.35 = (bf16[4,32,4096]{2,1,0:T(8,128)(2,1)S(1)}, bf16[4,32,4096]{2,1,0:T(8,128)(2,1)}, u32[]{:S(2)}, u32[]{:S(2)}) collective-permute-start(bf16[4,32,4096]{2,1,0:T(8,128)(2,1)S(1)} %pad_maximum_fusion.1.refs_0_), channel_id=1, source_target_pairs={{0,1},{1,0},{2,3},{3,2},{4,5},{5,4},{6,7},{7,6},{8,9},{9,8},{10,11... | collective-permute-start | bytes 3145736 | tf_op jit(solution)/shard_map/ppermute | solution.py:53
  206.2 57.8 %collective-permute-start.49 = (bf16[4,128,1024]{2,1,0:T(8,128)(2,1)}, bf16[4,128,1024]{2,1,0:T(8,128)(2,1)}, u32[]{:S(2)}, u32[]{:S(2)}) collective-permute-start(bf16[4,128,1024]{2,1,0:T(8,128)(2,1)} %collective-permute-done.45.refs_1_), channel_id=1, source_target_pairs={{0,4},{4,0},{1,5},{5,1},{2,6},{6,2},{3,7},{7,3},{8,12},{12,8},{9,1... | collective-permute-start | bytes 3145736 | tf_op jit(solution)/shard_map/ppermute | solution.py:62
  206.3 58.2 %collective-permute-start.50 = (bf16[4,128,1024]{2,1,0:T(8,128)(2,1)}, bf16[4,128,1024]{2,1,0:T(8,128)(2,1)}, u32[]{:S(2)}, u32[]{:S(2)}) collective-permute-start(bf16[4,128,1024]{2,1,0:T(8,128)(2,1)} %collective-permute-done.46.refs_2_), channel_id=1, source_target_pairs={{0,4},{4,0},{1,5},{5,1},{2,6},{6,2},{3,7},{7,3},{8,12},{12,8},{9,1... | collective-permute-start | bytes 3145736 | tf_op jit(solution)/shard_map/ppermute | solution.py:62
  226.9 74.4 %collective-permute-start.51 = (bf16[4,128,1024]{2,1,0:T(8,128)(2,1)}, bf16[4,128,1024]{2,1,0:T(8,128)(2,1)}, u32[]{:S(2)}, u32[]{:S(2)}) collective-permute-start(bf16[4,128,1024]{2,1,0:T(8,128)(2,1)} %collective-permute-done.47.refs_3_), channel_id=1, source_target_pairs={{0,4},{4,0},{1,5},{5,1},{2,6},{6,2},{3,7},{7,3},{8,12},{12,8},{9,1... | collective-permute-start | bytes 3145736 | tf_op jit(solution)/shard_map/ppermute | solution.py:62
  256.8 369.5 %collective-permute-start.38 = (bf16[4,32,4096]{2,1,0:T(8,128)(2,1)S(1)}, bf16[4,32,4096]{2,1,0:T(8,128)(2,1)}, u32[]{:S(2)}, u32[]{:S(2)}) collective-permute-start(bf16[4,32,4096]{2,1,0:T(8,128)(2,1)S(1)} %pad_maximum_fusion.1.refs_0_), channel_id=1, source_target_pairs={{0,4},{4,0},{1,5},{5,1},{2,6},{6,2},{3,7},{7,3},{8,12},{12,8},{9,1... | collective-permute-start | bytes 3145736 | tf_op jit(solution)/shard_map/ppermute | solution.py:62
  263.9 362.4 %collective-permute-start.39 = (bf16[4,32,4096]{2,1,0:T(8,128)(2,1)}, bf16[4,32,4096]{2,1,0:T(8,128)(2,1)}, u32[]{:S(2)}, u32[]{:S(2)}) collective-permute-start(bf16[4,32,4096]{2,1,0:T(8,128)(2,1)} %collective-permute-done.35.refs_1_), channel_id=1, source_target_pairs={{0,4},{4,0},{1,5},{5,1},{2,6},{6,2},{3,7},{7,3},{8,12},{12,8},{9,1... | collective-permute-start | bytes 3145736 | tf_op jit(solution)/shard_map/ppermute | solution.py:62
  264.0 362.4 %collective-permute-start.40 = (bf16[4,32,4096]{2,1,0:T(8,128)(2,1)}, bf16[4,32,4096]{2,1,0:T(8,128)(2,1)}, u32[]{:S(2)}, u32[]{:S(2)}) collective-permute-start(bf16[4,32,4096]{2,1,0:T(8,128)(2,1)} %collective-permute-done.36.refs_2_), channel_id=1, source_target_pairs={{0,4},{4,0},{1,5},{5,1},{2,6},{6,2},{3,7},{7,3},{8,12},{12,8},{9,1... | collective-permute-start | bytes 3145736 | tf_op jit(solution)/shard_map/ppermute | solution.py:62
  264.5 361.9 %collective-permute-start.41 = (bf16[4,32,4096]{2,1,0:T(8,128)(2,1)}, bf16[4,32,4096]{2,1,0:T(8,128)(2,1)}, u32[]{:S(2)}, u32[]{:S(2)}) collective-permute-start(bf16[4,32,4096]{2,1,0:T(8,128)(2,1)} %collective-permute-done.37.refs_3_), channel_id=1, source_target_pairs={{0,4},{4,0},{1,5},{5,1},{2,6},{6,2},{3,7},{7,3},{8,12},{12,8},{9,1... | collective-permute-start | bytes 3145736 | tf_op jit(solution)/shard_map/ppermute | solution.py:62
  301.2 581.5 %collective-permute-start.21 = (bf16[1024,256]{0,1:T(8,128)(2,1)}, bf16[1024,256]{0,1:T(8,128)(2,1)}, u32[]{:S(2)}, u32[]{:S(2)}) collective-permute-start(bf16[1024,256]{0,1:T(8,128)(2,1)} %get-tuple-element.88), channel_id=1, source_target_pairs={{0,4},{4,0},{1,5},{5,1},{2,6},{6,2},{3,7},{7,3},{8,12},{12,8},{9,1... | collective-permute-start | bytes 1572872 | tf_op jit(solution)/shard_map/ppermute | solution.py:62
  985.0 64.0 %collective-permute-start.85 = (bf16[4,32,4096]{2,1,0:T(8,128)(2,1)}, bf16[4,32,4096]{2,1,0:T(8,128)(2,1)}, u32[]{:S(2)}, u32[]{:S(2)}) collective-permute-start(bf16[4,32,4096]{2,1,0:T(8,128)(2,1)} %get-tuple-element.54), channel_id=1, source_target_pairs={{0,4},{4,0},{1,5},{5,1},{2,6},{6,2},{3,7},{7,3},{8,12},{12,8},{9,1... | collective-permute-start | bytes 3145736 | tf_op jit(solution)/shard_map/ppermute | solution.py:62
  985.0 64.6 %collective-permute-start.89 = (bf16[4,32,4096]{2,1,0:T(8,128)(2,1)}, bf16[4,32,4096]{2,1,0:T(8,128)(2,1)}, u32[]{:S(2)}, u32[]{:S(2)}) collective-permute-start(bf16[4,32,4096]{2,1,0:T(8,128)(2,1)} %get-tuple-element.55), channel_id=1, source_target_pairs={{0,4},{4,0},{1,5},{5,1},{2,6},{6,2},{3,7},{7,3},{8,12},{12,8},{9,1... | collective-permute-start | bytes 3145736 | tf_op jit(solution)/shard_map/ppermute | solution.py:62
  988.4 62.3 %collective-permute-start.87 = (bf16[4,32,4096]{2,1,0:T(8,128)(2,1)}, bf16[4,32,4096]{2,1,0:T(8,128)(2,1)}, u32[]{:S(2)}, u32[]{:S(2)}) collective-permute-start(bf16[4,32,4096]{2,1,0:T(8,128)(2,1)} %get-tuple-element.53), channel_id=1, source_target_pairs={{0,4},{4,0},{1,5},{5,1},{2,6},{6,2},{3,7},{7,3},{8,12},{12,8},{9,1... | collective-permute-start | bytes 3145736 | tf_op jit(solution)/shard_map/ppermute | solution.py:62
  991.6 63.5 %collective-permute-start.95 = (bf16[4,128,1024]{2,1,0:T(8,128)(2,1)}, bf16[4,128,1024]{2,1,0:T(8,128)(2,1)}, u32[]{:S(2)}, u32[]{:S(2)}) collective-permute-start(bf16[4,128,1024]{2,1,0:T(8,128)(2,1)} %get-tuple-element.47), channel_id=1, source_target_pairs={{0,4},{4,0},{1,5},{5,1},{2,6},{6,2},{3,7},{7,3},{8,12},{12,8},{9,1... | collective-permute-start | bytes 3145736 | tf_op jit(solution)/shard_map/ppermute | solution.py:62
  1077.0 68.8 %collective-permute-start.98 = (bf16[4,128,1024]{2,1,0:T(8,128)(2,1)S(1)}, bf16[4,128,1024]{2,1,0:T(8,128)(2,1)S(1)}, u32[]{:S(2)}, u32[]{:S(2)}) collective-permute-start(bf16[4,128,1024]{2,1,0:T(8,128)(2,1)S(1)} %get-tuple-element.51), channel_id=1, source_target_pairs={{0,2},{1,3},{2,0},{3,1},{4,6},{5,7},{6,4},{7,5},{8,10},{9,11},{10,... | collective-permute-start | bytes 3145736 | tf_op jit(solution)/shard_map/ppermute | solution.py:53
  1078.8 75.6 %collective-permute-start.96 = (bf16[4,128,1024]{2,1,0:T(8,128)(2,1)}, bf16[4,128,1024]{2,1,0:T(8,128)(2,1)}, u32[]{:S(2)}, u32[]{:S(2)}) collective-permute-start(bf16[4,128,1024]{2,1,0:T(8,128)(2,1)} %get-tuple-element.49), channel_id=1, source_target_pairs={{0,1},{1,0},{2,3},{3,2},{4,5},{5,4},{6,7},{7,6},{8,9},{9,8},{10,11... | collective-permute-start | bytes 3145736 | tf_op jit(solution)/shard_map/ppermute | solution.py:53
  1100.8 59.4 %collective-permute-start.84 = (bf16[4,32,4096]{2,1,0:T(8,128)(2,1)}, bf16[4,32,4096]{2,1,0:T(8,128)(2,1)}, u32[]{:S(2)}, u32[]{:S(2)}) collective-permute-start(bf16[4,32,4096]{2,1,0:T(8,128)(2,1)} %get-tuple-element.52), channel_id=1, source_target_pairs={{0,4},{4,0},{1,5},{5,1},{2,6},{6,2},{3,7},{7,3},{8,12},{12,8},{9,1... | collective-permute-start | bytes 3145736 | tf_op jit(solution)/shard_map/ppermute | solution.py:62
  1100.8 67.5 %collective-permute-start.90 = (bf16[4,32,4096]{2,1,0:T(8,128)(2,1)}, bf16[4,32,4096]{2,1,0:T(8,128)(2,1)}, u32[]{:S(2)}, u32[]{:S(2)}) collective-permute-start(bf16[4,32,4096]{2,1,0:T(8,128)(2,1)} %get-tuple-element.57), channel_id=1, source_target_pairs={{0,3},{1,2},{2,1},{3,0},{4,7},{5,6},{6,5},{7,4},{8,11},{9,10},{10,... | collective-permute-start | bytes 3145736 | tf_op jit(solution)/shard_map/ppermute | solution.py:53
  1123.2 66.7 %collective-permute-start.88 = (bf16[4,32,4096]{2,1,0:T(8,128)(2,1)}, bf16[4,32,4096]{2,1,0:T(8,128)(2,1)}, u32[]{:S(2)}, u32[]{:S(2)}) collective-permute-start(bf16[4,32,4096]{2,1,0:T(8,128)(2,1)} %get-tuple-element.58), channel_id=1, source_target_pairs={{0,2},{1,3},{2,0},{3,1},{4,6},{5,7},{6,4},{7,5},{8,10},{9,11},{10,... | collective-permute-start | bytes 3145736 | tf_op jit(solution)/shard_map/ppermute | solution.py:53
  (172 other events, 3032.7 us)

commit v2 on v1

--- a/solution.py
+++ b/solution.py
@@ -70,43 +70,77 @@
     return jnp.where(core == 0, jnp.stack([own, other]), jnp.stack([other, own]))
 
 
-def place_kernel(counts, ids, *refs):
-    dp_count, _, head_count = counts
-    pieces, out, sem = refs[: 2 * head_count], refs[2 * head_count], refs[2 * head_count + 1]
-    dp, core, head = ids[0], ids[1], ids[2]
+def place_kernel(widths, ids, *refs):
+    count = (len(refs) - 1 - len(widths)) // 2
+    pieces, outs, sem = refs[: 2 * count], refs[2 * count : -1], refs[-1]
+    core, head = ids[1], ids[2]
     copies = []
     for which in range(2):
-        for slot in range(head_count):
-            for step in range(dp_count):
-                source = lax.rem(dp + (dp_count - step), dp_count)
+        for slot in range(count):
+            start = 0
+            for out, columns in zip(outs, widths):
                 copies.append(
                     pltpu.make_async_copy(
-                        pieces[which * head_count + slot].at[step],
-                        out.at[source, core ^ which, head ^ slot],
+                        pieces[which * count + slot].at[:, :, pl.ds(start, columns)],
+                        out.at[:, core ^ which, head ^ slot],
                         sem.at[len(copies)],
                     )
                 )
+                start += columns
     for copy in copies:
         copy.start()
     for copy in copies:
         copy.wait()
 
 
-def place(pieces, ids):
-    counts = (lax.axis_size("dp"), 2, lax.axis_size("head"))
-    shape = pieces[0].shape[1:]
-    return pl.pallas_call(
-        functools.partial(place_kernel, counts),
-        out_shape=jax.ShapeDtypeStruct(counts + shape, pieces[0].dtype),
+def place(mine, widths, ids):
+    dp_count, rows, _ = mine[0].shape
+    pieces = list(mine) + [to_other_core(piece) for piece in mine]
+    shapes = [(dp_count, 2, len(mine), rows, columns) for columns in widths]
+    outs = pl.pallas_call(
+        functools.partial(place_kernel, widths),
+        out_shape=[jax.ShapeDtypeStruct(shape, BF16) for shape in shapes],
         grid_spec=pltpu.PrefetchScalarGridSpec(
             num_scalar_prefetch=1,
             grid=(1,),
             in_specs=[pl.BlockSpec(memory_space=pl.ANY)] * len(pieces),
-            out_specs=pl.BlockSpec(memory_space=pl.ANY),
-            scratch_shapes=[pltpu.SemaphoreType.DMA((counts[0] * 2 * counts[2],))],
-        ),
+            out_specs=[
+                pl.BlockSpec(
+                    shape, lambda i, ids: (0, 0, 0, 0, 0), pipeline_mode=pl.Buffered(1)
+                )
+                for shape in shapes
+            ],
+            scratch_shapes=[pltpu.SemaphoreType.DMA((len(pieces) * len(widths),))],
+        ),
+        compiler_params=pltpu.CompilerParams(vmem_limit_bytes=VMEM_LIMIT),
         name="place",
     )(ids, *pieces)
+    return [out.reshape(-1, columns) for out, columns in zip(outs, widths)]
+
+
+def gather_dp(shard):
+    full = lax.all_gather(shard, "dp", axis=0, tiled=True)
+    return full.reshape((-1,) + shard.shape)
+
+
+def split_terms(grad, core):
+    return (
+        pick(grad, core, 1).transpose(1, 0, 2, 3),
+        pick(grad, 1 - core, 1).transpose(1, 0, 2, 3),
+    )
+
+
+def chip_terms(own, away):
+    total = (own.astype(F32) + to_other_core(away).astype(F32)).astype(BF16)
+    return total.reshape(-1, total.shape[-1])
+
+
+def scatter_plane(terms):
+    return lax.psum_scatter(terms, "head", scatter_dimension=0, tiled=True)
+
+
+def scatter_dp(terms):
+    return lax.psum_scatter(terms, "dp", scatter_dimension=0, tiled=True).astype(F32)
 
 
 def gather_z(shard):
@@ -117,28 +151,67 @@
     return [own] + [to_xor(own, j) for j in range(1, lax.axis_size("head"))]
 
 
-def gather_rows(shard, ids):
-    mine = gather_plane(gather_z(shard))
-    theirs = [to_other_core(piece) for piece in mine]
-    return place(mine + theirs, ids)
-
-
-def scatter_rows(grad, core, head, dp):
-    dp_count, _, head_count = grad.shape[:3]
-    plane = []
-    for slot in range(head_count):
-        row = pick(grad, head ^ slot, 2)
-        arrived = to_other_core(pick(row, 1 - core, 1))
-        both = pick(row, core, 1).astype(F32) + arrived.astype(F32)
-        plane.append(both if slot == 0 else to_xor(both.astype(BF16), slot))
-    total = plane[0]
-    for piece in plane[1:]:
+def plane_near(own):
+    return to_xor(own, 1), to_xor(own, 2)
+
+
+def plane_far(own, near, axis):
+    half = own.shape[axis] // 2
+    lower = to_xor(lax.slice_in_dim(near[0], 0, half, axis=axis), 2)
+    upper = to_xor(lax.slice_in_dim(near[1], half, 2 * half, axis=axis), 1)
+    return [own, near[0], near[1], jnp.concatenate([lower, upper], axis=axis)]
+
+
+def sum_far(parts, axis):
+    half = parts[3].shape[axis] // 2
+    return (
+        to_xor(lax.slice_in_dim(parts[3], 0, half, axis=axis), 1),
+        to_xor(lax.slice_in_dim(parts[3], half, 2 * half, axis=axis), 2),
+    )
+
+
+def sum_near(parts, arrived, axis):
+    half = parts[3].shape[axis] // 2
+    cut = lambda value, low: lax.slice_in_dim(value, low, low + half, axis=axis)
+    to_y = jnp.concatenate(
+        [
+            (cut(parts[2], 0).astype(F32) + arrived[0].astype(F32)).astype(BF16),
+            cut(parts[2], half),
+        ],
+        axis=axis,
+    )
+    to_x = jnp.concatenate(
+        [
+            cut(parts[1], 0),
+            (cut(parts[1], half).astype(F32) + arrived[1].astype(F32)).astype(BF16),
+        ],
+        axis=axis,
+    )
+    return to_xor(to_x, 1), to_xor(to_y, 2)
+
+
+def core_terms(grad, core):
+    return to_other_core(pick(grad, 1 - core, 1))
+
+
+def plane_total(own, terms):
+    total = own
+    for piece in terms:
         total = total + piece.astype(F32)
+    return total
+
+
+def scatter_z(total, dp):
+    dp_count = total.shape[0]
     low = total.astype(BF16)
     result = pick(total, dp)
     for step in range(1, dp_count):
         result = result + to_shift(pick(low, lax.rem(dp + step, dp_count)), step).astype(F32)
     return result
+
+
+def together(*values):
+    return lax.optimization_barrier(values)
 
 
 def gather_small(vector, ids):
@@ -315,6 +388,192 @@
     )(me, qkv, attn, grad_attn, lse)
 
 
+def feed_kernel(ctx, weight, bias, hidden, slope):
+    pre = dot(ctx[...], weight[...], 1, 0) + bias[...]
+    value, steep = gelu_pair(pre)
+    hidden[...] = value.astype(BF16)
+    slope[...] = steep
+
+
+def feed(ctx, weight, bias):
+    rows, width = ctx.shape
+    units = weight.shape[1]
+    block = min(512, units)
+    return pl.pallas_call(
+        feed_kernel,
+        out_shape=(
+            jax.ShapeDtypeStruct((rows, units), BF16),
+            jax.ShapeDtypeStruct((rows, units), F32),
+        ),
+        grid=(units // block,),
+        in_specs=[
+            pl.BlockSpec((rows, width), lambda i: (0, 0)),
+            pl.BlockSpec((width, block), lambda i: (0, i)),
+            pl.BlockSpec((1, block), lambda i: (0, i)),
+        ],
+        out_specs=(
+            pl.BlockSpec((rows, block), lambda i: (0, i)),
+            pl.BlockSpec((rows, block), lambda i: (0, i)),
+        ),
+        compiler_params=pltpu.CompilerParams(vmem_limit_bytes=VMEM_LIMIT),
+        cost_estimate=pl.CostEstimate(
+            flops=2 * rows * width * units,
+            bytes_accessed=2 * width * units + 6 * rows * units,
+            transcendentals=rows * units,
+        ),
+        name="feed",
+    )(ctx, weight, bias.reshape(1, -1))
+
+
+def feed_back_kernel(
+    cot, hidden, slope, w_fc, w_proj, base, pre_low, grad_bias, grad_ctx, stream, sum_ctx, sum_out
+):
+    step = pl.program_id(0)
+    grad_pre = dot(cot[...], w_proj[...], 1, 1) * slope[...]
+    grad_bias[...] = jnp.sum(grad_pre, axis=0, keepdims=True)
+    low = grad_pre.astype(BF16)
+    pre_low[...] = low
+    back = dot(low, w_fc[...], 1, 1)
+    ahead = dot(hidden[...], w_proj[...], 1, 0)
+
+    @pl.when(step == 0)
+    def _():
+        sum_ctx[...] = back
+        sum_out[...] = base[...] + ahead
+
+    @pl.when(step > 0)
+    def _():
+        sum_ctx[...] += back
+        sum_out[...] += ahead
+
+    @pl.when(step == pl.num_programs(0) - 1)
+    def _():
+        grad_ctx[...] = sum_ctx[...]
+        stream[...] = sum_out[...]
+
+
+def feed_back(cot, hidden, slope, w_fc, w_proj, base):
+    rows, width = cot.shape
+    units = hidden.shape[1]
+    block = min(512, units)
+    whole = pl.BlockSpec((rows, width), lambda i: (0, 0))
+    columns = pl.BlockSpec((rows, block), lambda i: (0, i))
+    return pl.pallas_call(
+        feed_back_kernel,
+        out_shape=(
+            jax.ShapeDtypeStruct((rows, units), BF16),
+            jax.ShapeDtypeStruct((1, units), F32),
+            jax.ShapeDtypeStruct((rows, width), F32),
+            jax.ShapeDtypeStruct((rows, width), F32),
+        ),
+        grid=(units // block,),
+        in_specs=[
+            whole,
+            columns,
+            columns,
+            pl.BlockSpec((width, block), lambda i: (0, i)),
+            pl.BlockSpec((block, width), lambda i: (i, 0)),
+            whole,
+        ],
+        out_specs=(columns, pl.BlockSpec((1, block), lambda i: (0, i)), whole, whole),
+        scratch_shapes=[pltpu.VMEM((rows, width), F32)] * 2,
+        compiler_params=pltpu.CompilerParams(vmem_limit_bytes=VMEM_LIMIT),
+        cost_estimate=pl.CostEstimate(
+            flops=6 * rows * width * units,
+            bytes_accessed=4 * width * units + 8 * rows * units,
+            transcendentals=0,
+        ),
+        name="feed_back",
+    )(cot, hidden, slope, w_fc, w_proj, base)
+
+
+def split_rows(core, value, own, away):
+    count, rows = own.shape[0], own.shape[2]
+    value = value.astype(BF16)
+    half = count * rows
+    first = value[:half].reshape(count, 1, rows, -1)
+    second = value[half:].reshape(count, 1, rows, -1)
+
+    @pl.when(core == 0)
+    def _():
+        own[...] = first
+        away[...] = second
+
+    @pl.when(core == 1)
+    def _():
+        own[...] = second
+        away[...] = first
+
+
+def weight_kernel(ids, left, right, own, away):
+    split_rows(ids[1], dot(left[...], right[...], 0, 0), own, away)
+
+
+def weight_pair_kernel(ids, left, right, attn, resid, own, away):
+    units = right.shape[1]
+    total = dot(attn[0], resid[0], 1, 0)
+    for seq in range(1, attn.shape[0]):
+        total = total + dot(attn[seq], resid[seq], 1, 0)
+    split_rows(ids[1], dot(left[...], right[...], 0, 0), own.at[..., pl.ds(0, units)], away.at[..., pl.ds(0, units)])
+    split_rows(ids[1], total, own.at[..., pl.ds(units, total.shape[1])], away.at[..., pl.ds(units, total.shape[1])])
+
+
+def weight_call(kernel, counts, rows, columns, in_specs, flops, name):
+    dp_count, head_count = counts
+    spec = pl.BlockSpec((head_count, 1, rows, columns), lambda d, ids: (0, d, 0, 0))
+    shape = jax.ShapeDtypeStruct((head_count, dp_count, rows, columns), BF16)
+    return pl.pallas_call(
+        kernel,
+        out_shape=(shape, shape),
+        grid_spec=pltpu.PrefetchScalarGridSpec(
+            num_scalar_prefetch=1, grid=(dp_count,), in_specs=in_specs, out_specs=(spec, spec)
+        ),
+        compiler_params=pltpu.CompilerParams(vmem_limit_bytes=VMEM_LIMIT),
+        cost_estimate=pl.CostEstimate(
+            flops=flops, bytes_accessed=4 * head_count * dp_count * rows * columns, transcendentals=0
+        ),
+        name=name,
+    )
+
+
+def weight_terms(ids, left, right, counts, rows):
+    tokens, columns = right.shape
+    span = 2 * counts[1] * rows
+    return weight_call(
+        weight_kernel,
+        counts,
+        rows,
+        columns,
+        [
+            pl.BlockSpec((tokens, span), lambda d, ids: (0, d)),
+            pl.BlockSpec((tokens, columns), lambda d, ids: (0, 0)),
+        ],
+        2 * tokens * columns * left.shape[1],
+        "weight_terms",
+    )(ids, left, right)
+
+
+def weight_pair_terms(ids, left, right, attn, resid, counts, rows):
+    tokens, units = right.shape
+    seqs, _, features, seq_tokens = attn.shape
+    width = resid.shape[2]
+    span = 2 * counts[1] * rows
+    return weight_call(
+        weight_pair_kernel,
+        counts,
+        rows,
+        units + width,
+        [
+            pl.BlockSpec((tokens, span), lambda d, ids: (0, d)),
+            pl.BlockSpec((tokens, units), lambda d, ids: (0, 0)),
+            pl.BlockSpec((seqs, None, features, seq_tokens), lambda d, ids: (0, d ^ ids[2], 0, 0)),
+            pl.BlockSpec(resid.shape, lambda d, ids: (0, 0, 0)),
+        ],
+        2 * tokens * (units + width) * left.shape[1],
+        "weight_pair_terms",
+    )(ids, left, right, attn, resid)
+
+
 def to_attention(slots, head):
     count, features, width = slots.shape
     if count == SLOTS:
@@ -371,6 +630,7 @@
     full = [small[:, edges[i] : edges[i + 1]].reshape(-1) for i in range(len(sizes))]
     gain_one, bias_one, bias_q, bias_v, bias_out, gain_two, bias_two, bias_proj, bias_fc = full
 
+    square = head_count == 4
     stream_rows = stream_in.reshape(rows, width)
     normed_one, inv_one = normalize(stream_rows)
     act_one = (normed_one * gain_one + bias_one).astype(BF16).reshape(seq_dev, tok_rows, width)
@@ -380,18 +640,23 @@
         pick(columns, head ^ slot, 2).reshape(own_rows, 3 * group) for slot in range(head_count)
     ]
     parts = [parts[0]] + [to_xor(parts[slot], slot) for slot in range(1, head_count)]
-    shard = jnp.stack(parts)
-    theirs_z = gather_z(shard)
-    core_z = to_other_core(theirs_z)
-    group_w = place(
-        [theirs_z[:, slot] for slot in range(head_count)]
-        + [core_z[:, slot] for slot in range(head_count)],
-        ids,
-    ).reshape(width, 3 * group)
+    one_z = gather_dp(jnp.concatenate([w_fc, w_out], axis=1))
+    two_z = gather_dp(w_proj)
 
     own_half = by_half(core, pick(act_one, core), to_other_core(pick(act_one, 1 - core)))
     own_half = own_half.reshape(2 * tok_rows, width)
-    acts = gather_plane(own_half)
+    own_half, shard = together(own_half, jnp.concatenate(parts, axis=1))
+    group_z = gather_z(shard)
+    group_z = jnp.stack([pick(group_z, (dp + dp_count - k) % dp_count) for k in range(dp_count)])
+    wide = 3 * group
+    (group_w,) = place(
+        [group_z[:, :, slot * wide : (slot + 1) * wide] for slot in range(head_count)],
+        (wide,),
+        ids,
+    )
+    acts = plane_far(own_half, plane_near(own_half), 0) if square else gather_plane(own_half)
+    *acts, one_z = together(*acts, one_z)
+    one_near = plane_near(one_z) if square else gather_plane(one_z)
     qkv_bias = jnp.concatenate(
         [
             pick(bias_q.reshape(head_count, group), head),
@@ -403,110 +668,141 @@
     me, qkv = to_attention(qkv_slots, head)
     qkv = qkv.reshape(SLOTS, 3, heads, HD, -1)
     attn, lse = attend(me, qkv)
-
-    full_wout = gather_rows(w_out, ids).reshape(width, width)
-    full_wfc = gather_rows(w_fc, ids).reshape(width, hidden_width)
-    full_wproj = gather_rows(w_proj, ids).reshape(hidden_width, width)
-
+    attn, two_z, *one_near = together(attn, two_z, *one_near)
     attn_slots = from_attention(attn.reshape(SLOTS, group, -1), head, head_count)
-    attn_all = jnp.zeros((head_count, group, 2 * tok_rows), BF16)
-    for slot in range(head_count):
-        piece = attn_slots[slot]
-        piece = to_xor(piece, slot) if slot else piece
-        attn_all = lax.dynamic_update_index_in_dim(attn_all, piece, head ^ slot, 0)
-    attn_all = attn_all.reshape(width, 2, tok_rows)
-    attn_all = attn_all.reshape(width, 2 * tok_rows)
-    first, second = attn_all[:, :tok_rows], attn_all[:, tok_rows:]
+    attn_all = [attn_slots[0]] + [to_xor(attn_slots[j], j) for j in range(1, head_count)]
+    one_pieces = plane_far(one_z, one_near, 2) if square else one_near
+    attn_all = jnp.stack(attn_all)
+    first, second = attn_all[:, :, :tok_rows], attn_all[:, :, tok_rows:]
     keep = jnp.where(core == 0, first, second)
     away = jnp.where(core == 0, second, first)
     attn_cols = by_half(core, keep, to_other_core(away))
 
+    attn_cols, two_z, *one_pieces = together(attn_cols, two_z, *one_pieces)
+    two_near = plane_near(two_z) if square else gather_plane(two_z)
+    full_wfc, full_wout = place(one_pieces, (hidden_width, width), ids)
+    slot_wout = full_wout.reshape(head_count, group, width)
+    slot_wout = jnp.stack([pick(slot_wout, head ^ slot) for slot in range(head_count)])
+
     resid = (
         stream_rows
-        + jnp.einsum("sdt,de->ste", attn_cols, full_wout, preferred_element_type=F32).reshape(
+        + jnp.einsum("sjdt,jde->ste", attn_cols, slot_wout, preferred_element_type=F32).reshape(
             rows, width
         )
         + bias_out
     )
     normed_two, inv_two = normalize(resid)
     ctx = (normed_two * gain_two + bias_two).astype(BF16)
-    pre_act = dot(ctx, full_wfc, 1, 0) + bias_fc
-    gelu_val, gelu_slope = gelu_pair(pre_act)
-    hidden = gelu_val.astype(BF16)
-    stream_out = resid + dot(hidden, full_wproj, 1, 0) + bias_proj
-
+    ctx, *two_near = together(ctx, *two_near)
+    two_pieces = plane_far(two_z, two_near, 1) if square else two_near
+    hidden, slope = feed(ctx, full_wfc, bias_fc)
     cot_rows = cotangent.reshape(rows, width)
     cot_low = cot_rows.astype(BF16)
     grad_b_proj = jnp.sum(cot_rows, axis=0)
-    grad_w_proj = dot(hidden, cot_low, 0, 0).astype(BF16)
-    grad_pre = dot(cot_low, full_wproj, 1, 1) * gelu_slope
-    grad_b_fc = jnp.sum(grad_pre, axis=0)
-    pre_low = grad_pre.astype(BF16)
-    grad_w_fc = dot(ctx, pre_low, 0, 0).astype(BF16)
-    grad_ctx = dot(pre_low, full_wfc, 1, 1)
+    chips = (dp_count, head_count)
+    aligned = group == 2 * head_count * own_rows and (head_count * own_rows) % 128 == 0
+    if aligned:
+        two_own, two_away = weight_terms(ids, hidden, cot_low, chips, w_proj.shape[0])
+    else:
+        two_own, two_away = split_terms(
+            dot(hidden, cot_low, 0, 0).astype(BF16).reshape(grid + (-1, width)), core
+        )
+    two_terms = chip_terms(two_own, two_away)
+    (full_wproj,) = place(two_pieces, (width,), ids)
+    two_plane = scatter_plane(two_terms)
+    pre_low, grad_b_fc, grad_ctx, stream_out = feed_back(
+        cot_low, hidden, slope, full_wfc, full_wproj, resid + bias_proj
+    )
+    grad_b_fc = grad_b_fc.reshape(-1)
     grad_ln2_gain = jnp.sum(grad_ctx * normed_two, axis=0)
     grad_ln2_bias = jnp.sum(grad_ctx, axis=0)
     grad_resid = cot_rows + norm_back(grad_ctx * gain_two, normed_two, inv_two)
     grad_b_out = jnp.sum(grad_resid, axis=0)
     resid_low = grad_resid.astype(BF16)
     resid_three = resid_low.reshape(seq_dev, tok_rows, width)
-    grad_w_out = jnp.einsum(
-        "sdt,ste->de", attn_cols, resid_three, preferred_element_type=F32
+    grad_attn_cols = jnp.einsum(
+        "ste,jde->sjdt", resid_three, slot_wout, preferred_element_type=F32
     ).astype(BF16)
-    grad_attn_cols = jnp.einsum(
-        "ste,de->sdt", resid_three, full_wout, preferred_element_type=F32
-    ).astype(BF16)
-
-    shard_wproj = scatter_rows(grad_w_proj.reshape(grid + (-1, width)), core, head, dp)
-    shard_wfc = scatter_rows(grad_w_fc.reshape(grid + (-1, hidden_width)), core, head, dp)
-    shard_wout = scatter_rows(grad_w_out.reshape(grid + (-1, width)), core, head, dp)
-
     kept = pick(grad_attn_cols, core)
     arrived = to_other_core(pick(grad_attn_cols, 1 - core))
     grad_half = jnp.where(
         core == 0,
-        jnp.concatenate([kept, arrived], axis=1),
-        jnp.concatenate([arrived, kept], axis=1),
-    ).reshape(head_count, group, 2 * tok_rows)
-    grad_slots = jnp.stack(
-        [pick(grad_half, head)]
-        + [to_xor(pick(grad_half, head ^ slot), slot) for slot in range(1, head_count)]
-    )
-    _, grad_attn = to_attention(grad_slots, head)
+        jnp.concatenate([kept, arrived], axis=2),
+        jnp.concatenate([arrived, kept], axis=2),
+    )
+    grad_slots = [grad_half[0]] + [to_xor(grad_half[j], j) for j in range(1, head_count)]
+
+    if aligned:
+        one_own, one_away = weight_pair_terms(
+            ids, ctx, pre_low, attn_cols, resid_three, chips, own_rows
+        )
+    else:
+        grad_w_fc = dot(ctx, pre_low, 0, 0).astype(BF16)
+        grad_w_out = jnp.einsum(
+            "sjdt,ste->jde", attn_cols, resid_three, preferred_element_type=F32
+        ).astype(BF16)
+        grad_w_out = jnp.stack([pick(grad_w_out, head ^ slot) for slot in range(head_count)])
+        one_own, one_away = split_terms(
+            jnp.concatenate(
+                [
+                    grad_w_fc.reshape(grid + (-1, hidden_width)),
+                    grad_w_out.reshape(grid + (-1, width)),
+                ],
+                axis=4,
+            ),
+            core,
+        )
+    one_terms = chip_terms(one_own, one_away)
+    *grad_slots, one_terms = together(*grad_slots, one_terms)
+    one_plane = scatter_plane(one_terms)
+
+    _, grad_attn = to_attention(jnp.stack(grad_slots), head)
     grad_attn = grad_attn.reshape(SLOTS, heads, HD, -1)
     grad_qkv = attend_back(me, qkv, attn, grad_attn, lse)
     grad_qkv = from_attention(grad_qkv.reshape(SLOTS, 3 * group, -1), head, head_count)
 
-    grad_act_slots = [
-        dot(grad_qkv[slot], group_w, 0, 1).astype(BF16) for slot in range(head_count)
-    ]
-    sums = grad_act_slots[0].astype(F32)
-    for slot in range(1, head_count):
-        sums = sums + to_xor(grad_act_slots[slot], slot).astype(F32)
-    sums = sums.reshape(2, tok_rows, width)
+    act_parts = [dot(grad_qkv[slot], group_w, 0, 1) for slot in range(head_count)]
+    act_parts = [act_parts[0]] + [part.astype(BF16) for part in act_parts[1:]]
+    act_far = sum_far(act_parts, 0) if square else []
+    grad_qkv, one_plane, two_plane, *act_far = together(grad_qkv, one_plane, two_plane, *act_far)
+    both = jnp.concatenate(
+        [two_plane.reshape(dp_count, -1, width)]
+        + [
+            one_plane.reshape(dp_count, own_rows, -1)[:, :, i : i + width]
+            for i in range(0, one_plane.shape[1], width)
+        ],
+        axis=1,
+    )
+    both, *act_far = together(both, *act_far)
+    if square:
+        act_terms = sum_near(act_parts, act_far, 0)
+    else:
+        act_terms = [to_xor(act_parts[j], j) for j in range(1, head_count)]
+    sums = plane_total(act_parts[0], act_terms).reshape(2, tok_rows, width)
     grad_act = by_half(
         core, pick(sums, core), to_other_core(pick(sums, 1 - core))
     ).reshape(rows, width)
+
+    both = scatter_dp(both.reshape(-1, width))
+    shard_wproj = both[: w_proj.shape[0]]
+    columns = both[w_proj.shape[0] :].reshape(-1, own_rows, width)
+    shard_wfc = jnp.concatenate([columns[i] for i in range(hidden_width // width)], axis=1)
+    shard_wout = columns[-1]
 
     grad_group_w = dot(acts[0], grad_qkv[0], 0, 1)
     for slot in range(1, head_count):
         grad_group_w = grad_group_w + dot(acts[slot], grad_qkv[slot], 0, 1)
     grad_group_w = grad_group_w.astype(BF16).reshape(grid + (own_rows, 3 * group))
-    half_w = pick(grad_group_w, core, 1).astype(F32) + to_other_core(
-        pick(grad_group_w, 1 - core, 1)
-    ).astype(F32)
-    half_low = half_w.astype(BF16)
-    shard_w = pick(half_w, dp)
-    for step in range(1, dp_count):
-        shard_w = shard_w + to_shift(pick(half_low, lax.rem(dp + step, dp_count)), step).astype(F32)
-    shard_wqkv = jnp.zeros((own_rows, 3, head_count, group), F32)
-    for slot in range(head_count):
-        piece = pick(shard_w, head ^ slot)
-        piece = to_xor(piece, slot) if slot else piece
-        shard_wqkv = lax.dynamic_update_index_in_dim(
-            shard_wqkv, piece.reshape(own_rows, 3, group), head ^ slot, 2
-        )
-    shard_wqkv = shard_wqkv.reshape(own_rows, 3 * width)
+    half_w = pick(grad_group_w, core, 1).astype(F32) + core_terms(grad_group_w, core).astype(F32)
+    shard_w = scatter_z(half_w, dp)
+    pieces = jnp.stack(
+        [pick(shard_w, head)]
+        + [to_xor(pick(shard_w, head ^ slot), slot) for slot in range(1, head_count)]
+    )
+    ordered = [pick(pieces, head ^ slot) for slot in range(head_count)]
+    shard_wqkv = jnp.concatenate(
+        [piece[:, c * group : (c + 1) * group] for c in range(3) for piece in ordered], axis=1
+    )
 
     token_sums = jnp.sum(grad_qkv.astype(F32), axis=(0, 2)).reshape(3, group)
     grad_bias = jnp.zeros((3, head_count, group), F32)

time: 1270 us -> 490 us (0.39)
  Pallas kernels: 685 us -> 130 us
  waiting for transfers between devices: 244 us -> 161 us
  matrix products: 91.6 us -> 19.4 us
  local copies, waits for them, and re-layouts: 84.9 us -> 39.9 us
  starting transfers between devices: 98.7 us -> 71.2 us
  between operations: 2.64 us -> 15.7 us
    pallas_call x4 -> x7, Pallas kernels: 628 us -> 72.3 us  [the longest x1 21.9 us: feed_back(): pl.pallas_call(feed_back_kernel, out_shape=(jax.ShapeDtypeStruct((rows, u...]
    ppermute x42 -> x34, waiting for transfers between devices: 169 us -> 63 us  [to_xor(): return lax.ppermute(value, 'head', [(i, i ^ step) for i in range(count)])]
    dot_general x18 -> x12, matrix products: 85.8 us -> 16.6 us  [dot(): lax.dot_general(left, right, (((left_dim,), (right_dim,)), ((), ())), pre...]
    dynamic_update_slice x8 -> x0, local copies, waits for them, and re-layouts: 41.8 us -> none  [the longest x4 29.8 us: on_device(): attn_all = lax.dynamic_update_index_in_dim(attn_all, piece, head ^ slot, 0)]
    reduce_scatter x0 -> x3, waiting for transfers between devices: none -> 20 us  [the longest x2 20 us: scatter_plane(): return lax.psum_scatter(terms, 'head', scatter_dimension=0, tiled=True)]
    ppermute x32 -> x21, waiting for transfers between devices: 2.4 us -> 21.4 us  [to_other_core(): return lax.ppermute(value, 'blk', [(0, 1), (1, 0)])]
    ppermute x30 -> x12, starting transfers between devices: 44.5 us -> 26.6 us  [to_shift(): lax.ppermute(value, 'dp', [(i, (i + step) % count) for i in range(count)])]
    ppermute x30 -> x12, waiting for transfers between devices: 71.7 us -> 56.4 us  [to_shift(): lax.ppermute(value, 'dp', [(i, (i + step) % count) for i in range(count)])]
  transfers between devices with their start and end apart: 104 -> 72, of which waited for: 29 -> 40; matrix products, arithmetic and copies ran while one was open for 14% -> 14% of each run, Pallas kernels for 54% -> 22%
where the time goes in v2:
time: 490 us; the launch traced here: 484 us
  waiting for transfers between devices  161 us (33%)
  Pallas kernels  130 us (27%)
  starting transfers between devices  71.2 us (15%)
  other arithmetic  47.1 us (10%)
  local copies, waits for them, and re-layouts  39.9 us (8%)
  matrix products  19.4 us (4%)
  between operations  15.7 us (3%)
    ppermute x34, waiting for transfers between devices, to_xor(): return lax.ppermute(value, 'head', [(i, i ^ step) for i in range(count)])  63 us
    ppermute x12, waiting for transfers between devices, to_shift(): lax.ppermute(value, 'dp', [(i, (i + step) % count) for i in range(count)])  56.4 us
    ppermute x34, starting transfers between devices, to_xor(): return lax.ppermute(value, 'head', [(i, i ^ step) for i in range(count)])  40.4 us
    pallas_call x1, Pallas kernels, attend_back(): pl.pallas_call(functools.partial(backward_kernel, block), out_shape=jax.S...  38.4 us
    ppermute x12, starting transfers between devices, to_shift(): lax.ppermute(value, 'dp', [(i, (i + step) % count) for i in range(count)])  26.6 us
    pallas_call x1, Pallas kernels, feed_back(): pl.pallas_call(feed_back_kernel, out_shape=(jax.ShapeDtypeStruct((rows, u...  21.9 us
    ppermute x21, waiting for transfers between devices, to_other_core(): return lax.ppermute(value, 'blk', [(0, 1), (1, 0)])  21.4 us
    reduce_scatter x2, waiting for transfers between devices, scatter_plane(): return lax.psum_scatter(terms, 'head', scatter_dimension=0, tiled=True)  20 us
  transfers between devices with their start and end apart: 72, of which 40 were waited for; matrix products, arithmetic and copies ran while one was open for 14% of the time, Pallas kernels for 22%

profile of v2, /device:TPU:0, one launch (start us, length us, event | category | flops | bytes accessed | tf_op | source)
XLA Modules:
  0.0 483.9 jit_solution(7658085113669322483)
XLA Ops:
  8.9 5.1 %collective-permute-start.2 = (f32[1,384]{1,0:T(1,128)S(1)}, f32[1,384]{1,0:T(1,128)S(1)}, u32[]{:S(2)}, u32[]{:S(2)}) collective-permute-start(f32[1,384]{1,0:T(1,128)S(1)} %convert_element_type.132), channel_id=1, source_target_pairs={{0,24},{8,0},{16,8},{24,16},{1,25},{9,1},{17,9},{25,17},{2,26},{10... | collective-permute-start | bytes 4616 | tf_op jit(solution)/shard_map/ppermute | solution.py:58
  42.5 28.0 %collective-permute-done.12 = bf16[32,3072]{1,0:T(8,128)(2,1)S(1)} collective-permute-done((bf16[32,3072]{1,0:T(8,128)(2,1)S(1)}, bf16[32,3072]{1,0:T(8,128)(2,1)S(1)}, u32[]{:S(2)}, u32[]{:S(2)}) %collective-permute-start.12) | collective-permute-done | bytes 196640 | tf_op jit(solution)/shard_map/ppermute | solution.py:58
  93.9 18.8 %attend.1 = (bf16[4,4,64,512]{3,2,1,0:T(8,128)(2,1)S(1)}, f32[4,8,256]{2,1,0:T(8,128)S(1)}) custom-call(s32[1]{0:T(128)} %bitcast.2.me_ref, bf16[4,3,4,64,512]{4,3,2,1,0:T(8,128)(2,1)S(1)} %pad_maximum_fusion.qkv), custom_call_target="tpu_custom_call" | custom-call | flops 2147483648 | bytes 4194304 | tf_op jit(solution)/shard_map/attend/pallas_call | solution.py:333
  121.8 15.4 %collective-permute-done.26 = bf16[256,512]{1,0:T(8,128)(2,1)S(1)} collective-permute-done((bf16[256,512]{1,0:T(8,128)(2,1)S(1)}, bf16[256,512]{1,0:T(8,128)(2,1)S(1)}, u32[]{:S(2)}, u32[]{:S(2)}) %collective-permute-start.26) | collective-permute-done | bytes 262176 | tf_op jit(solution)/shard_map/ppermute | solution.py:53
  137.2 3.0 collective-permute-done.25
  152.4 8.1 %place.4 = (bf16[4,2,4,32,4096]{4,3,2,1,0:T(8,128)(2,1)}, bf16[4,2,4,32,1024]{4,3,2,1,0:T(8,128)(2,1)}) custom-call(s32[3]{0:T(128)S(1)} %pad_add_fusion.ids, bf16[4,32,5120]{2,1,0:T(8,128)(2,1)} %bitcast.38.refs_0_, bf16[4,32,5120]{2,1,0:T(8,128)(2,1)S(1)} %collective-permute-done.22.refs_1_, bf16[4,32,5120]{2,1,0:T(8,128)(2,1)} %collective-permute-done.23.refs_2_, ...), custom_call_target="tpu_custom_call" | custom-call | tf_op jit(solution)/shard_map/place/pallas_call | solution.py:100
  167.6 3.9 collective-permute-done.34.refs_1_
  172.9 13.9 %feed.1 = (bf16[512,4096]{1,0:T(8,128)(2,1)S(1)}, f32[512,4096]{1,0:T(8,128)}) custom-call(bf16[512,1024]{1,0:T(8,128)(2,1)S(1)} %add_convert_fusion.3.ctx.left, bf16[1024,4096]{1,0:T(8,128)(2,1)} %bitcast.390, f32[1,4096]{1,0:T(1,128)S(1)} %bitcast.289), custom_call_target="tpu_custom_call" | custom-call | flops 4294967296 | bytes 20971520 | tf_op jit(solution)/shard_map/feed/pallas_call | solution.py:402
  188.8 9.1 %weight_terms.1 = (bf16[4,4,128,1024]{3,2,1,0:T(8,128)(2,1)S(1)}, bf16[4,4,128,1024]{3,2,1,0:T(8,128)(2,1)}) custom-call(s32[3]{0:T(128)S(1)} %pad_add_fusion.ids, bf16[512,4096]{1,0:T(8,128)(2,1)} %copy-done.12, bf16[512,1024]{1,0:T(8,128)(2,1)S(1)} %copy-done.9), custom_call_target="tpu_custom_call" | custom-call | flops 4294967296 | bytes 8388608 | tf_op jit(solution)/shard_map/weight_terms/pallas_call | solution.py:542
  200.7 11.6 %collective-permute-done.36 = bf16[4,64,1024]{2,1,0:T(8,128)(2,1)S(1)} collective-permute-done((bf16[4,64,1024]{2,1,0:T(8,128)(2,1)S(1)}, bf16[4,64,1024]{2,1,0:T(8,128)(2,1)S(1)}, u32[]{:S(2)}, u32[]{:S(2)}) %collective-permute-start.36) | collective-permute-done | bytes 524320 | tf_op jit(solution)/shard_map/ppermute | solution.py:53
  217.5 6.2 %place.5 = bf16[4,2,4,128,1024]{4,3,2,1,0:T(8,128)(2,1)} custom-call(s32[3]{0:T(128)S(1)} %pad_add_fusion.ids, bf16[4,128,1024]{2,1,0:T(8,128)(2,1)S(1)} %bitcast.285, bf16[4,128,1024]{2,1,0:T(8,128)(2,1)S(1)} %collective-permute-done.34.refs_1_, bf16[4,128,1024]{2,1,0:T(8,128)(2,1)S(1)} %collective-permute-done.35.refs_2_, ...), custom_call_target="tpu_custom_call" | custom-call | tf_op jit(solution)/shard_map/place/pallas_call | solution.py:100
  225.3 21.9 %feed_back.1 = (bf16[512,4096]{1,0:T(8,128)(2,1)}, f32[1,4096]{1,0:T(1,128)S(1)}, f32[512,1024]{1,0:T(8,128)S(1)}, f32[512,1024]{1,0:T(8,128)}) custom-call(bf16[512,1024]{1,0:T(8,128)(2,1)S(1)} %copy-done.9, bf16[512,4096]{1,0:T(8,128)(2,1)} %copy-done.12, f32[512,4096]{1,0:T(8,128)} %get-tuple-element.83.slope, bf16[1024,4096]{1,0:T(8,128)(2,1)} %bitcast.391, ...), custom_call_target="tpu_custom_call" | custom-call | flops 12884901888 | bytes 33554432 | tf_op jit(solution)/shard_map/feed_back/pallas_call | solution.py:461
  247.2 6.4 %add_convert_fusion.1 = bf16[4,4,128,1024]{3,2,1,0:T(8,128)(2,1)} fusion(bf16[4,4,128,1024]{3,2,1,0:T(8,128)(2,1)} %collective-permute-done.47, bf16[4,4,128,1024]{3,2,1,0:T(8,128)(2,1)S(1)} %get-tuple-element.97), kind=kLoop, calls=%fused_computation.1 | loop fusion | flops 8388608 | bytes 12582912 | tf_op jit(solution)/shard_map/convert_element_type | solution.py:134
  259.4 12.0 %weight_pair_terms.1 = (bf16[4,4,32,5120]{3,2,1,0:T(8,128)(2,1)}, bf16[4,4,32,5120]{3,2,1,0:T(8,128)(2,1)}) custom-call(s32[3]{0:T(128)S(1)} %pad_add_fusion.ids, bf16[512,1024]{1,0:T(8,128)(2,1)S(1)} %copy-done.11, bf16[512,4096]{1,0:T(8,128)(2,1)} %get-tuple-element.88.right, bf16[2,4,256,256]{3,2,1,0:T(8,128)(2,1)S(1)} %copy-done.6, ...), custom_call_target="tpu_custom_call" | custom-call | flops 5368709120 | bytes 10485760 | tf_op jit(solution)/shard_map/weight_pair_terms/pallas_call | solution.py:561
  273.8 7.0 %collective-permute-done.42 = bf16[4,256,256]{2,1,0:T(8,128)(2,1)S(1)} collective-permute-done((bf16[4,256,256]{2,1,0:T(8,128)(2,1)S(1)}, bf16[4,256,256]{2,1,0:T(8,128)(2,1)S(1)}, u32[]{:S(2)}, u32[]{:S(2)}) %collective-permute-start.42) | collective-permute-done | bytes 524320 | tf_op jit(solution)/shard_map/ppermute | solution.py:62
  284.8 8.5 %add_convert_fusion = bf16[4,4,32,5120]{3,2,1,0:T(8,128)(2,1)} fusion(bf16[4,4,32,5120]{3,2,1,0:T(8,128)(2,1)} %collective-permute-done.46, bf16[4,4,32,5120]{3,2,1,0:T(8,128)(2,1)} %get-tuple-element.89), kind=kLoop, calls=%fused_computation | loop fusion | flops 10485760 | bytes 15728640 | tf_op jit(solution)/shard_map/convert_element_type | solution.py:134
  301.7 38.4 %attend_back.1 = bf16[4,3,4,64,512]{4,3,2,1,0:T(8,128)(2,1)S(1)} custom-call(s32[1]{0:T(128)} %bitcast.2.me_ref, bf16[4,3,4,64,512]{4,3,2,1,0:T(8,128)(2,1)} %copy-done, bf16[4,4,64,512]{3,2,1,0:T(8,128)(2,1)S(1)} %copy-done.8, bf16[4,4,64,512]{3,2,1,0:T(8,128)(2,1)S(1)} %pad_maximum_fusion.5.grad_attn, f32[4,8,256]{2,1,0:T(8,128)S(1)} %get-tuple-element.95.lse), custom_call_target="tpu_custom_call" | custom-call | flops 5368709120 | bytes 8388608 | tf_op jit(solution)/shard_map/attend_back/pallas_call | solution.py:363
  349.5 13.2 %collective-permute-done.48 = bf16[256,1024]{1,0:T(8,128)(2,1)} collective-permute-done((bf16[256,1024]{1,0:T(8,128)(2,1)S(1)}, bf16[256,1024]{1,0:T(8,128)(2,1)}, u32[]{:S(2)}, u32[]{:S(2)}) %collective-permute-start.48) | collective-permute-done | bytes 524320 | tf_op jit(solution)/shard_map/ppermute | solution.py:53
  362.7 20.0 %reduce-scatter.4.cloned.1.call-done = bf16[128,5120]{1,0:T(8,128)(2,1)} async-done(((bf16[512,5120]{1,0:T(8,128)(2,1)}), bf16[128,5120]{1,0:T(8,128)(2,1)}) %reduce-scatter.4.cloned.1.call-update) | async-done | bytes 1310736 | tf_op jit(solution)/shard_map/reduce_scatter | solution.py:139
  402.0 3.3 collective-permute-start.63
  407.9 3.1 collective-permute-done.63
  411.0 23.7 %collective-permute-done.62 = bf16[4,32,768]{2,1,0:T(8,128)(2,1)} collective-permute-done((bf16[4,32,768]{2,1,0:T(8,128)(2,1)}, bf16[4,32,768]{2,1,0:T(8,128)(2,1)}, u32[]{:S(2)}, u32[]{:S(2)}) %collective-permute-start.62) | collective-permute-done | bytes 196640 | tf_op jit(solution)/shard_map/ppermute | solution.py:58
  455.7 10.1 %collective-permute-start.58 = (f32[384]{0:T(512)S(1)}, f32[384]{0:T(512)S(1)}, u32[]{:S(2)}, u32[]{:S(2)}) collective-permute-start(f32[384]{0:T(512)S(1)} %get-tuple-element.122), channel_id=1, source_target_pairs={{0,16},{8,24},{16,0},{24,8},{1,17},{9,25},{17,1},{25,9},{2,18},{10... | collective-permute-start | bytes 4616 | tf_op jit(solution)/shard_map/ppermute | solution.py:58
  467.8 4.2 fusion.6
  (462 shorter events, 173.1 us)
Async XLA Ops:
  7.2 78.3 %all-gather.3.cloned.1.call-start = ((), (), s32[]{:S(2)}) async-start(), calls=%async_computation.3 | async-start | bytes 1638400 | tf_op jit(solution)/shard_map/all_gather | solution.py:122
  32.9 81.5 %all-gather.5.cloned.1.call-start = ((), (), s32[]{:S(2)}) async-start(), calls=%async_computation.4 | async-start | bytes 1310720 | tf_op jit(solution)/shard_map/all_gather | solution.py:122
  36.7 33.7 %collective-permute-start.12 = (bf16[32,3072]{1,0:T(8,128)(2,1)S(1)}, bf16[32,3072]{1,0:T(8,128)(2,1)S(1)}, u32[]{:S(2)}, u32[]{:S(2)}) collective-permute-start(bf16[32,3072]{1,0:T(8,128)(2,1)S(1)} %pad_maximum_fusion.15), channel_id=1, source_target_pairs={{0,16},{8,24},{16,0},{24,8},{1,17},{9,25},{17,1},{25,9},{2,18},{10... | collective-permute-start | bytes 589832 | tf_op jit(solution)/shard_map/ppermute | solution.py:58
  37.9 32.6 %collective-permute-start.11 = (bf16[32,3072]{1,0:T(8,128)(2,1)S(1)}, bf16[32,3072]{1,0:T(8,128)(2,1)S(1)}, u32[]{:S(2)}, u32[]{:S(2)}) collective-permute-start(bf16[32,3072]{1,0:T(8,128)(2,1)S(1)} %pad_maximum_fusion.15), channel_id=1, source_target_pairs={{0,8},{8,16},{16,24},{24,0},{1,9},{9,17},{17,25},{25,1},{2,10},{10... | collective-permute-start | bytes 589832 | tf_op jit(solution)/shard_map/ppermute | solution.py:58
  37.9 34.5 %collective-permute-start.18 = (bf16[512,1024]{1,0:T(8,128)(2,1)S(1)}, bf16[512,1024]{1,0:T(8,128)(2,1)S(1)}, u32[]{:S(2)}, u32[]{:S(2)}) collective-permute-start(bf16[512,1024]{1,0:T(8,128)(2,1)S(1)} %bitcast.293), channel_id=1, source_target_pairs={{0,1},{1,0},{2,3},{3,2},{4,5},{5,4},{6,7},{7,6},{8,9},{9,8},{10,11... | collective-permute-start | bytes 3145736 | tf_op jit(solution)/shard_map/ppermute | solution.py:53
  39.4 31.4 %collective-permute-start.19 = (bf16[512,1024]{1,0:T(8,128)(2,1)S(1)}, bf16[512,1024]{1,0:T(8,128)(2,1)S(1)}, u32[]{:S(2)}, u32[]{:S(2)}) collective-permute-start(bf16[512,1024]{1,0:T(8,128)(2,1)S(1)} %bitcast.294), channel_id=1, source_target_pairs={{0,2},{1,3},{2,0},{3,1},{4,6},{5,7},{6,4},{7,5},{8,10},{9,11},{10,... | collective-permute-start | bytes 3145736 | tf_op jit(solution)/shard_map/ppermute | solution.py:53
  75.0 287.7 %reduce-scatter.6.cloned.1.call-start = ((), (), s32[]{:S(2)}) async-start(), calls=%async_computation.6 | async-start | bytes 5242880 | tf_op jit(solution)/shard_map/reduce_scatter | solution.py:139
  85.5 28.9 %collective-permute-start.22 = (bf16[4,32,5120]{2,1,0:T(8,128)(2,1)}, bf16[4,32,5120]{2,1,0:T(8,128)(2,1)S(1)}, u32[]{:S(2)}, u32[]{:S(2)}) collective-permute-start(bf16[4,32,5120]{2,1,0:T(8,128)(2,1)} %bitcast.38.refs_0_), channel_id=1, source_target_pairs={{0,1},{1,0},{2,3},{3,2},{4,5},{5,4},{6,7},{7,6},{8,9},{9,8},{10,11... | collective-permute-start | bytes 3932168 | tf_op jit(solution)/shard_map/ppermute | solution.py:53
  86.0 28.4 %collective-permute-start.23 = (bf16[4,32,5120]{2,1,0:T(8,128)(2,1)}, bf16[4,32,5120]{2,1,0:T(8,128)(2,1)}, u32[]{:S(2)}, u32[]{:S(2)}) collective-permute-start(bf16[4,32,5120]{2,1,0:T(8,128)(2,1)} %bitcast.38.refs_0_), channel_id=1, source_target_pairs={{0,2},{1,3},{2,0},{3,1},{4,6},{5,7},{6,4},{7,5},{8,10},{9,11},{10,... | collective-permute-start | bytes 3932168 | tf_op jit(solution)/shard_map/ppermute | solution.py:53
  116.0 24.6 %collective-permute-start.29 = (bf16[4,32,2560]{2,1,0:T(8,128)(2,1)S(1)}, bf16[4,32,2560]{2,1,0:T(8,128)(2,1)S(1)}, u32[]{:S(2)}, u32[]{:S(2)}) collective-permute-start(bf16[4,32,2560]{2,1,0:T(8,128)(2,1)S(1)} %slice.280), channel_id=1, source_target_pairs={{0,1},{1,0},{2,3},{3,2},{4,5},{5,4},{6,7},{7,6},{8,9},{9,8},{10,11... | collective-permute-start | bytes 1966088 | tf_op jit(solution)/shard_map/ppermute | solution.py:53
  117.6 22.9 %collective-permute-start.28 = (bf16[4,32,2560]{2,1,0:T(8,128)(2,1)S(1)}, bf16[4,32,2560]{2,1,0:T(8,128)(2,1)S(1)}, u32[]{:S(2)}, u32[]{:S(2)}) collective-permute-start(bf16[4,32,2560]{2,1,0:T(8,128)(2,1)S(1)} %slice.279), channel_id=1, source_target_pairs={{0,2},{1,3},{2,0},{3,1},{4,6},{5,7},{6,4},{7,5},{8,10},{9,11},{10,... | collective-permute-start | bytes 1966088 | tf_op jit(solution)/shard_map/ppermute | solution.py:53
  119.8 20.4 %collective-permute-start.25 = (bf16[256,512]{1,0:T(8,128)(2,1)S(1)}, bf16[256,512]{1,0:T(8,128)(2,1)S(1)}, u32[]{:S(2)}, u32[]{:S(2)}) collective-permute-start(bf16[256,512]{1,0:T(8,128)(2,1)S(1)} %bitcast.335), channel_id=1, source_target_pairs={{0,2},{1,3},{2,0},{3,1},{4,6},{5,7},{6,4},{7,5},{8,10},{9,11},{10,... | collective-permute-start | bytes 786440 | tf_op jit(solution)/shard_map/ppermute | solution.py:53
  120.3 19.9 %collective-permute-start.24 = (bf16[256,512]{1,0:T(8,128)(2,1)S(1)}, bf16[256,512]{1,0:T(8,128)(2,1)S(1)}, u32[]{:S(2)}, u32[]{:S(2)}) collective-permute-start(bf16[256,512]{1,0:T(8,128)(2,1)S(1)} %bitcast.333), channel_id=1, source_target_pairs={{0,1},{1,0},{2,3},{3,2},{4,5},{5,4},{6,7},{7,6},{8,9},{9,8},{10,11... | collective-permute-start | bytes 786440 | tf_op jit(solution)/shard_map/ppermute | solution.py:53
  146.1 25.4 %collective-permute-start.34 = (bf16[4,128,1024]{2,1,0:T(8,128)(2,1)}, bf16[4,128,1024]{2,1,0:T(8,128)(2,1)S(1)}, u32[]{:S(2)}, u32[]{:S(2)}) collective-permute-start(bf16[4,128,1024]{2,1,0:T(8,128)(2,1)} %bitcast.282), channel_id=1, source_target_pairs={{0,1},{1,0},{2,3},{3,2},{4,5},{5,4},{6,7},{7,6},{8,9},{9,8},{10,11... | collective-permute-start | bytes 3145736 | tf_op jit(solution)/shard_map/ppermute | solution.py:53
  147.5 25.4 %collective-permute-start.35 = (bf16[4,128,1024]{2,1,0:T(8,128)(2,1)}, bf16[4,128,1024]{2,1,0:T(8,128)(2,1)S(1)}, u32[]{:S(2)}, u32[]{:S(2)}) collective-permute-start(bf16[4,128,1024]{2,1,0:T(8,128)(2,1)} %bitcast.283), channel_id=1, source_target_pairs={{0,2},{1,3},{2,0},{3,1},{4,6},{5,7},{6,4},{7,5},{8,10},{9,11},{10,... | collective-permute-start | bytes 3145736 | tf_op jit(solution)/shard_map/ppermute | solution.py:53
  197.9 49.3 %collective-permute-start.47 = (bf16[4,4,128,1024]{3,2,1,0:T(8,128)(2,1)}, bf16[4,4,128,1024]{3,2,1,0:T(8,128)(2,1)}, u32[]{:S(2)}, u32[]{:S(2)}) collective-permute-start(bf16[4,4,128,1024]{3,2,1,0:T(8,128)(2,1)} %get-tuple-element.98), channel_id=1, source_target_pairs={{0,4},{4,0},{1,5},{5,1},{2,6},{6,2},{3,7},{7,3},{8,12},{12,8},{9,1... | collective-permute-start | bytes 12582920 | tf_op jit(solution)/shard_map/ppermute | solution.py:62
  253.6 129.1 %reduce-scatter.4.cloned.1.call-start = ((), (), s32[]{:S(2)}) async-start(), calls=%async_computation.5 | async-start | bytes 6553600 | tf_op jit(solution)/shard_map/reduce_scatter | solution.py:139
  296.5 177.2 %reduce-scatter.8.cloned.1.call-start = ((), (), s32[]{:S(2)}) async-start(), calls=%async_computation.7 | async-start | bytes 2949120 | tf_op jit(solution)/shard_map/reduce_scatter | solution.py:143
  343.0 19.7 %collective-permute-start.48 = (bf16[256,1024]{1,0:T(8,128)(2,1)S(1)}, bf16[256,1024]{1,0:T(8,128)(2,1)}, u32[]{:S(2)}, u32[]{:S(2)}) collective-permute-start(bf16[256,1024]{1,0:T(8,128)(2,1)S(1)} %get-tuple-element.144), channel_id=1, source_target_pairs={{0,1},{1,0},{2,3},{3,2},{4,5},{5,4},{6,7},{7,6},{8,9},{9,8},{10,11... | collective-permute-start | bytes 1572872 | tf_op jit(solution)/shard_map/ppermute | solution.py:53
  343.7 19.0 %collective-permute-start.49 = (bf16[256,1024]{1,0:T(8,128)(2,1)S(1)}, bf16[256,1024]{1,0:T(8,128)(2,1)}, u32[]{:S(2)}, u32[]{:S(2)}) collective-permute-start(bf16[256,1024]{1,0:T(8,128)(2,1)S(1)} %get-tuple-element.143), channel_id=1, source_target_pairs={{0,2},{1,3},{2,0},{3,1},{4,6},{5,7},{6,4},{7,5},{8,10},{9,11},{10,... | collective-permute-start | bytes 1572872 | tf_op jit(solution)/shard_map/ppermute | solution.py:53
  394.7 44.7 %collective-permute-start.51 = (bf16[512,1024]{1,0:T(8,128)(2,1)}, bf16[512,1024]{1,0:T(8,128)(2,1)}, u32[]{:S(2)}, u32[]{:S(2)}) collective-permute-start(bf16[512,1024]{1,0:T(8,128)(2,1)} %pad_maximum_fusion.7), channel_id=1, source_target_pairs={{0,2},{1,3},{2,0},{3,1},{4,6},{5,7},{6,4},{7,5},{8,10},{9,11},{10,... | collective-permute-start | bytes 3145736 | tf_op jit(solution)/shard_map/ppermute | solution.py:53
  398.3 41.1 %collective-permute-start.50 = (bf16[512,1024]{1,0:T(8,128)(2,1)}, bf16[512,1024]{1,0:T(8,128)(2,1)}, u32[]{:S(2)}, u32[]{:S(2)}) collective-permute-start(bf16[512,1024]{1,0:T(8,128)(2,1)} %pad_maximum_fusion.6), channel_id=1, source_target_pairs={{0,1},{1,0},{2,3},{3,2},{4,5},{5,4},{6,7},{7,6},{8,9},{9,8},{10,11... | collective-permute-start | bytes 3145736 | tf_op jit(solution)/shard_map/ppermute | solution.py:53
  405.4 29.3 %collective-permute-start.62 = (bf16[4,32,768]{2,1,0:T(8,128)(2,1)}, bf16[4,32,768]{2,1,0:T(8,128)(2,1)}, u32[]{:S(2)}, u32[]{:S(2)}) collective-permute-start(bf16[4,32,768]{2,1,0:T(8,128)(2,1)} %get-tuple-element.161), channel_id=1, source_target_pairs={{0,16},{8,24},{16,0},{24,8},{1,17},{9,25},{17,1},{25,9},{2,18},{10... | collective-permute-start | bytes 589832 | tf_op jit(solution)/shard_map/ppermute | solution.py:58
  405.4 29.3 %collective-permute-start.61 = (bf16[4,32,768]{2,1,0:T(8,128)(2,1)S(1)}, bf16[4,32,768]{2,1,0:T(8,128)(2,1)}, u32[]{:S(2)}, u32[]{:S(2)}) collective-permute-start(bf16[4,32,768]{2,1,0:T(8,128)(2,1)S(1)} %get-tuple-element.159), channel_id=1, source_target_pairs={{0,8},{8,16},{16,24},{24,0},{1,9},{9,17},{17,25},{25,1},{2,10},{10... | collective-permute-start | bytes 589832 | tf_op jit(solution)/shard_map/ppermute | solution.py:58
  (129 other events, 827.1 us)
Sparse Core Ops, SparseCore 0:
  33.0 43.8 all-gather.2
  78.5 27.5 all-gather.4
  253.7 57.7 reduce-scatter.5
  314.7 67.9 reduce-scatter.3
  408.0 53.1 reduce-scatter.7

commit v3 on v2

--- a/solution.py
+++ b/solution.py
@@ -34,12 +34,10 @@
 
 
 def gelu_pair(pre_act):
-    tangent = jnp.tanh(ROOT_TWO_PI * (pre_act + GELU_COEF * pre_act * pre_act * pre_act))
-    value = 0.5 * pre_act * (1.0 + tangent)
-    slope = 0.5 * (1.0 + tangent) + 0.5 * pre_act * (1.0 - tangent * tangent) * ROOT_TWO_PI * (
-        1.0 + 3.0 * GELU_COEF * pre_act * pre_act
-    )
-    return (value, slope)
+    square = pre_act * pre_act
+    upper = 0.5 + 0.5 * jnp.tanh(pre_act * (ROOT_TWO_PI + (ROOT_TWO_PI * GELU_COEF) * square))
+    bend = 2.0 * ROOT_TWO_PI + (6.0 * ROOT_TWO_PI * GELU_COEF) * square
+    return (pre_act * upper, upper + upper * (pre_act * (1.0 - upper)) * bend)
 
 
 def dot(left, right, left_dim, right_dim):
@@ -160,34 +158,6 @@
     lower = to_xor(lax.slice_in_dim(near[0], 0, half, axis=axis), 2)
     upper = to_xor(lax.slice_in_dim(near[1], half, 2 * half, axis=axis), 1)
     return [own, near[0], near[1], jnp.concatenate([lower, upper], axis=axis)]
-
-
-def sum_far(parts, axis):
-    half = parts[3].shape[axis] // 2
-    return (
-        to_xor(lax.slice_in_dim(parts[3], 0, half, axis=axis), 1),
-        to_xor(lax.slice_in_dim(parts[3], half, 2 * half, axis=axis), 2),
-    )
-
-
-def sum_near(parts, arrived, axis):
-    half = parts[3].shape[axis] // 2
-    cut = lambda value, low: lax.slice_in_dim(value, low, low + half, axis=axis)
-    to_y = jnp.concatenate(
-        [
-            (cut(parts[2], 0).astype(F32) + arrived[0].astype(F32)).astype(BF16),
-            cut(parts[2], half),
-        ],
-        axis=axis,
-    )
-    to_x = jnp.concatenate(
-        [
-            cut(parts[1], 0),
-            (cut(parts[1], half).astype(F32) + arrived[1].astype(F32)).astype(BF16),
-        ],
-        axis=axis,
-    )
-    return to_xor(to_x, 1), to_xor(to_y, 2)
 
 
 def core_terms(grad, core):
@@ -696,6 +666,7 @@
     ctx, *two_near = together(ctx, *two_near)
     two_pieces = plane_far(two_z, two_near, 1) if square else two_near
     hidden, slope = feed(ctx, full_wfc, bias_fc)
+    hidden, *two_pieces = together(hidden, *two_pieces)
     cot_rows = cotangent.reshape(rows, width)
     cot_low = cot_rows.astype(BF16)
     grad_b_proj = jnp.sum(cot_rows, axis=0)
@@ -709,6 +680,7 @@
         )
     two_terms = chip_terms(two_own, two_away)
     (full_wproj,) = place(two_pieces, (width,), ids)
+    two_terms, cot_low = together(two_terms, cot_low)
     two_plane = scatter_plane(two_terms)
     pre_low, grad_b_fc, grad_ctx, stream_out = feed_back(
         cot_low, hidden, slope, full_wfc, full_wproj, resid + bias_proj
@@ -730,6 +702,8 @@
         jnp.concatenate([kept, arrived], axis=2),
         jnp.concatenate([arrived, kept], axis=2),
     )
+    grad_half, two_plane = together(grad_half, two_plane)
+    shard_wproj = scatter_dp(two_plane)
     grad_slots = [grad_half[0]] + [to_xor(grad_half[j], j) for j in range(1, head_count)]
 
     if aligned:
@@ -763,58 +737,20 @@
 
     act_parts = [dot(grad_qkv[slot], group_w, 0, 1) for slot in range(head_count)]
     act_parts = [act_parts[0]] + [part.astype(BF16) for part in act_parts[1:]]
-    act_far = sum_far(act_parts, 0) if square else []
-    grad_qkv, one_plane, two_plane, *act_far = together(grad_qkv, one_plane, two_plane, *act_far)
-    both = jnp.concatenate(
-        [two_plane.reshape(dp_count, -1, width)]
-        + [
-            one_plane.reshape(dp_count, own_rows, -1)[:, :, i : i + width]
-            for i in range(0, one_plane.shape[1], width)
-        ],
-        axis=1,
-    )
-    both, *act_far = together(both, *act_far)
-    if square:
-        act_terms = sum_near(act_parts, act_far, 0)
-    else:
-        act_terms = [to_xor(act_parts[j], j) for j in range(1, head_count)]
-    sums = plane_total(act_parts[0], act_terms).reshape(2, tok_rows, width)
-    grad_act = by_half(
-        core, pick(sums, core), to_other_core(pick(sums, 1 - core))
-    ).reshape(rows, width)
-
-    both = scatter_dp(both.reshape(-1, width))
-    shard_wproj = both[: w_proj.shape[0]]
-    columns = both[w_proj.shape[0] :].reshape(-1, own_rows, width)
-    shard_wfc = jnp.concatenate([columns[i] for i in range(hidden_width // width)], axis=1)
-    shard_wout = columns[-1]
-
+    act_terms = [to_xor(act_parts[j], j) for j in range(1, head_count)]
     grad_group_w = dot(acts[0], grad_qkv[0], 0, 1)
     for slot in range(1, head_count):
         grad_group_w = grad_group_w + dot(acts[slot], grad_qkv[slot], 0, 1)
-    grad_group_w = grad_group_w.astype(BF16).reshape(grid + (own_rows, 3 * group))
-    half_w = pick(grad_group_w, core, 1).astype(F32) + core_terms(grad_group_w, core).astype(F32)
-    shard_w = scatter_z(half_w, dp)
-    pieces = jnp.stack(
-        [pick(shard_w, head)]
-        + [to_xor(pick(shard_w, head ^ slot), slot) for slot in range(1, head_count)]
-    )
-    ordered = [pick(pieces, head ^ slot) for slot in range(head_count)]
-    shard_wqkv = jnp.concatenate(
-        [piece[:, c * group : (c + 1) * group] for c in range(3) for piece in ordered], axis=1
-    )
-
     token_sums = jnp.sum(grad_qkv.astype(F32), axis=(0, 2)).reshape(3, group)
     grad_bias = jnp.zeros((3, head_count, group), F32)
     grad_bias = lax.dynamic_update_index_in_dim(grad_bias, token_sums, head, 1).reshape(3, width)
 
-    grad_ln1_gain = jnp.sum(grad_act * normed_one, axis=0)
-    grad_ln1_bias = jnp.sum(grad_act, axis=0)
-    grad_rows_in = grad_resid + norm_back(grad_act * gain_one, normed_one, inv_one)
-
+    wide_w = group_w.astype(F32)
+    act_sum = jnp.sum(wide_w * token_sums.reshape(1, -1), axis=1)
+    act_product = jnp.sum(wide_w * grad_group_w, axis=1)
     vectors = [
-        grad_ln1_gain,
-        grad_ln1_bias,
+        act_product,
+        act_sum,
         grad_bias[0],
         grad_bias[2],
         grad_b_out,
@@ -825,11 +761,33 @@
     ]
     packed = jnp.concatenate([v.reshape(devices, -1) for v in vectors], axis=1)
     mine = scatter_small(packed.reshape(grid + (-1,)), core, head, dp)
+    grad_group_w = grad_group_w.astype(BF16).reshape(grid + (own_rows, 3 * group))
+    half_w = pick(grad_group_w, core, 1).astype(F32) + core_terms(grad_group_w, core).astype(F32)
+    shard_w = scatter_z(half_w, dp)
+    act_terms[0], one_plane, mine = together(act_terms[0], one_plane, mine)
+    shard_w, shard_one, *act_terms = together(shard_w, scatter_dp(one_plane), *act_terms)
+    sums = plane_total(act_parts[0], act_terms).reshape(2, tok_rows, width)
+    grad_act = by_half(
+        core, pick(sums, core), to_other_core(pick(sums, 1 - core))
+    ).reshape(rows, width)
+
+    pieces = jnp.stack(
+        [pick(shard_w, head)]
+        + [to_xor(pick(shard_w, head ^ slot), slot) for slot in range(1, head_count)]
+    )
+    ordered = [pick(pieces, head ^ slot) for slot in range(head_count)]
+    shard_wqkv = jnp.concatenate(
+        [piece[:, c * group : (c + 1) * group] for c in range(3) for piece in ordered], axis=1
+    )
+
+    shard_wfc, shard_wout = shard_one[:, :hidden_width], shard_one[:, hidden_width:]
+    grad_rows_in = grad_resid + norm_back(grad_act * gain_one, normed_one, inv_one)
+
     cut = [mine[edges[i] : edges[i + 1]] for i in range(len(sizes))]
     return (
         stream_out.reshape(seq_dev, tok_rows, width),
         grad_rows_in.reshape(seq_dev, tok_rows, width),
-        cut[0],
+        (cut[0] - ln1_bias.astype(F32) * cut[1]) / ln1_gain.astype(F32),
         cut[1],
         shard_wqkv,
         jnp.stack([cut[2], cut[3]]),

time: 490 us -> 468 us (0.955)
  local copies, waits for them, and re-layouts: 39.9 us -> 31.8 us
  other arithmetic: 47.1 us -> 39.3 us
  starting transfers between devices: 71.2 us -> 64.4 us
  waiting for transfers between devices: 161 us -> 155 us
  matrix products: 19.4 us -> 25 us
    reduce_scatter x2, waiting for transfers between devices: 20 us -> 0.04 us  [scatter_plane(): return lax.psum_scatter(terms, 'head', scatter_dimension=0, tiled=True)]
    ppermute x12, waiting for transfers between devices: 56.4 us -> 39.8 us  [to_shift(): lax.ppermute(value, 'dp', [(i, (i + step) % count) for i in range(count)])]
    reduce_scatter x1 -> x2, waiting for transfers between devices: 0.01 us -> 14 us  [scatter_dp(): lax.psum_scatter(terms, 'dp', scatter_dimension=0, tiled=True).astype(F32)]
    ppermute x21, waiting for transfers between devices: 21.4 us -> 30.5 us  [to_other_core(): return lax.ppermute(value, 'blk', [(0, 1), (1, 0)])]
    ppermute x34 -> x33, waiting for transfers between devices: 63 us -> 70.2 us  [to_xor(): return lax.ppermute(value, 'head', [(i, i ^ step) for i in range(count)])]
    ppermute x12, starting transfers between devices: 26.6 us -> 20.3 us  [to_shift(): lax.ppermute(value, 'dp', [(i, (i + step) % count) for i in range(count)])]
    unnamed x188 -> x152, local copies, waits for them, and re-layouts: 17.7 us -> 12 us
    dot_general x12, matrix products: 16.6 us -> 22.2 us  [dot(): lax.dot_general(left, right, (((left_dim,), (right_dim,)), ((), ())), pre...]
  transfers between devices with their start and end apart: 72 -> 72, of which waited for: 40 -> 39; matrix products, arithmetic and copies ran while one was open for 14% -> 16% of each run, Pallas kernels for 22% -> 26%
where the time goes in v3:
time: 468 us; the launch traced here: 462 us
  waiting for transfers between devices  155 us (33%)
  Pallas kernels  131 us (28%)
  starting transfers between devices  64.4 us (14%)
  other arithmetic  39.3 us (8%)
  local copies, waits for them, and re-layouts  31.8 us (7%)
  matrix products  25 us (5%)
  between operations  15.8 us (3%)
    ppermute x33, waiting for transfers between devices, to_xor(): return lax.ppermute(value, 'head', [(i, i ^ step) for i in range(count)])  70.2 us
    ppermute x12, waiting for transfers between devices, to_shift(): lax.ppermute(value, 'dp', [(i, (i + step) % count) for i in range(count)])  39.8 us
    ppermute x33, starting transfers between devices, to_xor(): return lax.ppermute(value, 'head', [(i, i ^ step) for i in range(count)])  39.7 us
    pallas_call x1, Pallas kernels, attend_back(): pl.pallas_call(functools.partial(backward_kernel, block), out_shape=jax.S...  38.4 us
    ppermute x21, waiting for transfers between devices, to_other_core(): return lax.ppermute(value, 'blk', [(0, 1), (1, 0)])  30.5 us
    pallas_call x1, Pallas kernels, feed_back(): pl.pallas_call(feed_back_kernel, out_shape=(jax.ShapeDtypeStruct((rows, u...  22.3 us
    dot_general x12, matrix products, dot(): lax.dot_general(left, right, (((left_dim,), (right_dim,)), ((), ())), pre...  22.2 us
    ppermute x12, starting transfers between devices, to_shift(): lax.ppermute(value, 'dp', [(i, (i + step) % count) for i in range(count)])  20.3 us
  transfers between devices with their start and end apart: 72, of which 39 were waited for; matrix products, arithmetic and copies ran while one was open for 16% of the time, Pallas kernels for 26%

profile of v3, /device:TPU:0, one launch (start us, length us, event | category | flops | bytes accessed | tf_op | source)
XLA Modules:
  0.0 462.2 jit_solution(9738404148832930961)
XLA Ops:
  8.9 3.1 collective-permute-start
  42.7 4.6 collective-permute-done.11
  47.2 15.5 %collective-permute-done.12 = bf16[32,3072]{1,0:T(8,128)(2,1)S(1)} collective-permute-done((bf16[32,3072]{1,0:T(8,128)(2,1)S(1)}, bf16[32,3072]{1,0:T(8,128)(2,1)S(1)}, u32[]{:S(2)}, u32[]{:S(2)}) %collective-permute-start.12) | collective-permute-done | bytes 196640 | tf_op jit(solution)/shard_map/ppermute | solution.py:56
  72.5 5.6 %collective-permute-done.20 = bf16[256,1024]{1,0:T(8,128)(2,1)} collective-permute-done((bf16[256,1024]{1,0:T(8,128)(2,1)S(1)}, bf16[256,1024]{1,0:T(8,128)(2,1)}, u32[]{:S(2)}, u32[]{:S(2)}) %collective-permute-start.20) | collective-permute-done | bytes 524320 | tf_op jit(solution)/shard_map/ppermute | solution.py:51
  89.7 18.8 %attend.1 = (bf16[4,4,64,512]{3,2,1,0:T(8,128)(2,1)S(1)}, f32[4,8,256]{2,1,0:T(8,128)S(1)}) custom-call(s32[1]{0:T(128)} %bitcast.2.me_ref, bf16[4,3,4,64,512]{4,3,2,1,0:T(8,128)(2,1)S(1)} %pad_maximum_fusion.qkv), custom_call_target="tpu_custom_call" | custom-call | flops 2147483648 | bytes 4194304 | tf_op jit(solution)/shard_map/attend/pallas_call | solution.py:303
  119.6 16.8 %collective-permute-done.24 = bf16[256,512]{1,0:T(8,128)(2,1)S(1)} collective-permute-done((bf16[256,512]{1,0:T(8,128)(2,1)S(1)}, bf16[256,512]{1,0:T(8,128)(2,1)S(1)}, u32[]{:S(2)}, u32[]{:S(2)}) %collective-permute-start.24) | collective-permute-done | bytes 262176 | tf_op jit(solution)/shard_map/ppermute | solution.py:51
  151.5 8.4 %place.4 = (bf16[4,2,4,32,4096]{4,3,2,1,0:T(8,128)(2,1)}, bf16[4,2,4,32,1024]{4,3,2,1,0:T(8,128)(2,1)}) custom-call(s32[3]{0:T(128)S(1)} %pad_add_fusion.ids, bf16[4,32,5120]{2,1,0:T(8,128)(2,1)} %bitcast.37.refs_0_, bf16[4,32,5120]{2,1,0:T(8,128)(2,1)} %collective-permute-done.22.refs_1_, bf16[4,32,5120]{2,1,0:T(8,128)(2,1)} %collective-permute-done.23.refs_2_, ...), custom_call_target="tpu_custom_call" | custom-call | tf_op jit(solution)/shard_map/place/pallas_call | solution.py:98
  176.9 13.5 %feed.1 = (bf16[512,4096]{1,0:T(8,128)(2,1)S(1)}, f32[512,4096]{1,0:T(8,128)}) custom-call(bf16[512,1024]{1,0:T(8,128)(2,1)S(1)} %add_convert_fusion.2.ctx.left, bf16[1024,4096]{1,0:T(8,128)(2,1)} %bitcast.364, f32[1,4096]{1,0:T(1,128)S(1)} %bitcast.267), custom_call_target="tpu_custom_call" | custom-call | flops 4294967296 | bytes 20971520 | tf_op jit(solution)/shard_map/feed/pallas_call | solution.py:372
  192.5 9.1 %weight_terms.1 = (bf16[4,4,128,1024]{3,2,1,0:T(8,128)(2,1)S(1)}, bf16[4,4,128,1024]{3,2,1,0:T(8,128)(2,1)}) custom-call(s32[3]{0:T(128)S(1)} %pad_add_fusion.ids, bf16[512,4096]{1,0:T(8,128)(2,1)} %copy-done.10, bf16[512,1024]{1,0:T(8,128)(2,1)S(1)} %get-tuple-element.97.right.cot), custom_call_target="tpu_custom_call" | custom-call | flops 4294967296 | bytes 8388608 | tf_op jit(solution)/shard_map/weight_terms/pallas_call | solution.py:512
  202.6 12.3 %collective-permute-done.38 = bf16[4,4,128,1024]{3,2,1,0:T(8,128)(2,1)S(1)} collective-permute-done((bf16[4,4,128,1024]{3,2,1,0:T(8,128)(2,1)}, bf16[4,4,128,1024]{3,2,1,0:T(8,128)(2,1)S(1)}, u32[]{:S(2)}, u32[]{:S(2)}) %collective-permute-start.38) | collective-permute-done | bytes 4194336 | tf_op jit(solution)/shard_map/ppermute | solution.py:60
  214.9 4.3 add_convert_fusion.1
  219.3 7.4 %place.5 = bf16[4,2,4,128,1024]{4,3,2,1,0:T(8,128)(2,1)} custom-call(s32[3]{0:T(128)S(1)} %pad_add_fusion.ids, bf16[4,128,1024]{2,1,0:T(8,128)(2,1)} %bitcast.44.refs_0_, bf16[4,128,1024]{2,1,0:T(8,128)(2,1)} %collective-permute-done.34.refs_1_, bf16[4,128,1024]{2,1,0:T(8,128)(2,1)} %collective-permute-done.35.refs_2_, ...), custom_call_target="tpu_custom_call" | custom-call | tf_op jit(solution)/shard_map/place/pallas_call | solution.py:98
  226.8 22.3 %feed_back.1 = (bf16[512,4096]{1,0:T(8,128)(2,1)}, f32[1,4096]{1,0:T(1,128)S(1)}, f32[512,1024]{1,0:T(8,128)S(1)}, f32[512,1024]{1,0:T(8,128)}) custom-call(bf16[512,1024]{1,0:T(8,128)(2,1)S(1)} %copy-done.9, bf16[512,4096]{1,0:T(8,128)(2,1)} %copy-done.10, f32[512,4096]{1,0:T(8,128)} %get-tuple-element.98.slope, bf16[1024,4096]{1,0:T(8,128)(2,1)} %bitcast.365, ...), custom_call_target="tpu_custom_call" | custom-call | flops 12884901888 | bytes 33554432 | tf_op jit(solution)/shard_map/feed_back/pallas_call | solution.py:431
  253.9 11.8 %weight_pair_terms.1 = (bf16[4,4,32,5120]{3,2,1,0:T(8,128)(2,1)}, bf16[4,4,32,5120]{3,2,1,0:T(8,128)(2,1)}) custom-call(s32[3]{0:T(128)S(1)} %pad_add_fusion.ids, bf16[512,1024]{1,0:T(8,128)(2,1)S(1)} %copy-done.7, bf16[512,4096]{1,0:T(8,128)(2,1)} %get-tuple-element.107.right, bf16[2,4,256,256]{3,2,1,0:T(8,128)(2,1)S(1)} %copy-done.3, ...), custom_call_target="tpu_custom_call" | custom-call | flops 5368709120 | bytes 10485760 | tf_op jit(solution)/shard_map/weight_pair_terms/pallas_call | solution.py:531
  268.8 6.5 %collective-permute-done.43 = bf16[4,256,256]{2,1,0:T(8,128)(2,1)S(1)} collective-permute-done((bf16[4,256,256]{2,1,0:T(8,128)(2,1)}, bf16[4,256,256]{2,1,0:T(8,128)(2,1)S(1)}, u32[]{:S(2)}, u32[]{:S(2)}) %collective-permute-start.43) | collective-permute-done | bytes 524320 | tf_op jit(solution)/shard_map/ppermute | solution.py:60
  281.3 8.3 %add_convert_fusion = bf16[4,4,32,5120]{3,2,1,0:T(8,128)(2,1)} fusion(bf16[4,4,32,5120]{3,2,1,0:T(8,128)(2,1)} %collective-permute-done.47, bf16[4,4,32,5120]{3,2,1,0:T(8,128)(2,1)} %get-tuple-element.108), kind=kLoop, calls=%fused_computation | loop fusion | flops 10485760 | bytes 15728640 | tf_op jit(solution)/shard_map/convert_element_type | solution.py:132
  294.5 38.4 %attend_back.1 = bf16[4,3,4,64,512]{4,3,2,1,0:T(8,128)(2,1)S(1)} custom-call(s32[1]{0:T(128)} %bitcast.2.me_ref, bf16[4,3,4,64,512]{4,3,2,1,0:T(8,128)(2,1)} %copy-done, bf16[4,4,64,512]{3,2,1,0:T(8,128)(2,1)S(1)} %copy-done.5, bf16[4,4,64,512]{3,2,1,0:T(8,128)(2,1)S(1)} %pad_maximum_fusion.6.grad_attn, f32[4,8,256]{2,1,0:T(8,128)S(1)} %get-tuple-element.114.lse), custom_call_target="tpu_custom_call" | custom-call | flops 5368709120 | bytes 8388608 | tf_op jit(solution)/shard_map/attend_back/pallas_call | solution.py:333
  343.3 3.1 convolution_convert_fusion.2
  353.4 27.2 %collective-permute-done.54 = f32[4,384]{1,0:T(4,128)S(1)} collective-permute-done((f32[4,384]{1,0:T(4,128)S(1)}, f32[4,384]{1,0:T(4,128)S(1)}, u32[]{:S(2)}, u32[]{:S(2)}) %collective-permute-start.54) | collective-permute-done | bytes 6176 | tf_op jit(solution)/shard_map/ppermute | solution.py:51
  389.3 3.2 convolution_convert_fusion.1
  397.8 3.2 collective-permute-start.50
  403.3 3.3 collective-permute-done.49
  406.7 14.2 %collective-permute-done.50 = bf16[4,32,768]{2,1,0:T(8,128)(2,1)S(1)} collective-permute-done((bf16[4,32,768]{2,1,0:T(8,128)(2,1)S(1)}, bf16[4,32,768]{2,1,0:T(8,128)(2,1)S(1)}, u32[]{:S(2)}, u32[]{:S(2)}) %collective-permute-start.50) | collective-permute-done | bytes 196640 | tf_op jit(solution)/shard_map/ppermute | solution.py:56
  424.6 14.0 %reduce-scatter.9.cloned.1.call-done = bf16[32,5120]{1,0:T(8,128)(2,1)} async-done(((bf16[128,5120]{1,0:T(8,128)(2,1)}), bf16[32,5120]{1,0:T(8,128)(2,1)}) %reduce-scatter.9.cloned.1.call-update) | async-done | bytes 327696 | tf_op jit(solution)/shard_map/reduce_scatter | solution.py:141
  (420 shorter events, 171.4 us)
Async XLA Ops:
  7.2 74.7 %all-gather.3.cloned.1.call-start = ((), (), s32[]{:S(2)}) async-start(), calls=%async_computation.4 | async-start | bytes 1638400 | tf_op jit(solution)/shard_map/all_gather | solution.py:120
  35.8 74.5 %all-gather.5.cloned.1.call-start = ((), (), s32[]{:S(2)}) async-start(), calls=%async_computation.5 | async-start | bytes 1310720 | tf_op jit(solution)/shard_map/all_gather | solution.py:120
  37.4 25.3 %collective-permute-start.12 = (bf16[32,3072]{1,0:T(8,128)(2,1)S(1)}, bf16[32,3072]{1,0:T(8,128)(2,1)S(1)}, u32[]{:S(2)}, u32[]{:S(2)}) collective-permute-start(bf16[32,3072]{1,0:T(8,128)(2,1)S(1)} %pad_maximum_fusion.13), channel_id=1, source_target_pairs={{0,16},{8,24},{16,0},{24,8},{1,17},{9,25},{17,1},{25,9},{2,18},{10... | collective-permute-start | bytes 589832 | tf_op jit(solution)/shard_map/ppermute | solution.py:56
  37.8 24.9 %collective-permute-start.13 = (bf16[32,3072]{1,0:T(8,128)(2,1)S(1)}, bf16[32,3072]{1,0:T(8,128)(2,1)S(1)}, u32[]{:S(2)}, u32[]{:S(2)}) collective-permute-start(bf16[32,3072]{1,0:T(8,128)(2,1)S(1)} %pad_maximum_fusion.13), channel_id=1, source_target_pairs={{0,24},{8,0},{16,8},{24,16},{1,25},{9,1},{17,9},{25,17},{2,26},{10... | collective-permute-start | bytes 589832 | tf_op jit(solution)/shard_map/ppermute | solution.py:56
  40.6 24.7 %collective-permute-start.18 = (bf16[512,1024]{1,0:T(8,128)(2,1)S(1)}, bf16[512,1024]{1,0:T(8,128)(2,1)S(1)}, u32[]{:S(2)}, u32[]{:S(2)}) collective-permute-start(bf16[512,1024]{1,0:T(8,128)(2,1)S(1)} %bitcast.272), channel_id=1, source_target_pairs={{0,1},{1,0},{2,3},{3,2},{4,5},{5,4},{6,7},{7,6},{8,9},{9,8},{10,11... | collective-permute-start | bytes 3145736 | tf_op jit(solution)/shard_map/ppermute | solution.py:51
  41.1 25.9 %collective-permute-start.19 = (bf16[512,1024]{1,0:T(8,128)(2,1)S(1)}, bf16[512,1024]{1,0:T(8,128)(2,1)S(1)}, u32[]{:S(2)}, u32[]{:S(2)}) collective-permute-start(bf16[512,1024]{1,0:T(8,128)(2,1)S(1)} %bitcast.273), channel_id=1, source_target_pairs={{0,2},{1,3},{2,0},{3,1},{4,6},{5,7},{6,4},{7,5},{8,10},{9,11},{10,... | collective-permute-start | bytes 3145736 | tf_op jit(solution)/shard_map/ppermute | solution.py:51
  68.5 209.2 %reduce-scatter.5.cloned.1.call-start = ((), (), s32[]{:S(2)}) async-start(), calls=%async_computation.6 | async-start | bytes 5242880 | tf_op jit(solution)/shard_map/reduce_scatter | solution.py:137
  81.9 28.7 %collective-permute-start.22 = (bf16[4,32,5120]{2,1,0:T(8,128)(2,1)}, bf16[4,32,5120]{2,1,0:T(8,128)(2,1)}, u32[]{:S(2)}, u32[]{:S(2)}) collective-permute-start(bf16[4,32,5120]{2,1,0:T(8,128)(2,1)} %bitcast.37.refs_0_), channel_id=1, source_target_pairs={{0,1},{1,0},{2,3},{3,2},{4,5},{5,4},{6,7},{7,6},{8,9},{9,8},{10,11... | collective-permute-start | bytes 3932168 | tf_op jit(solution)/shard_map/ppermute | solution.py:51
  82.4 28.3 %collective-permute-start.23 = (bf16[4,32,5120]{2,1,0:T(8,128)(2,1)}, bf16[4,32,5120]{2,1,0:T(8,128)(2,1)}, u32[]{:S(2)}, u32[]{:S(2)}) collective-permute-start(bf16[4,32,5120]{2,1,0:T(8,128)(2,1)} %bitcast.37.refs_0_), channel_id=1, source_target_pairs={{0,2},{1,3},{2,0},{3,1},{4,6},{5,7},{6,4},{7,5},{8,10},{9,11},{10,... | collective-permute-start | bytes 3932168 | tf_op jit(solution)/shard_map/ppermute | solution.py:51
  111.8 27.7 %collective-permute-start.28 = (bf16[4,32,2560]{2,1,0:T(8,128)(2,1)S(1)}, bf16[4,32,2560]{2,1,0:T(8,128)(2,1)S(1)}, u32[]{:S(2)}, u32[]{:S(2)}) collective-permute-start(bf16[4,32,2560]{2,1,0:T(8,128)(2,1)S(1)} %slice.215), channel_id=1, source_target_pairs={{0,2},{1,3},{2,0},{3,1},{4,6},{5,7},{6,4},{7,5},{8,10},{9,11},{10,... | collective-permute-start | bytes 1966088 | tf_op jit(solution)/shard_map/ppermute | solution.py:51
  114.3 25.2 %collective-permute-start.29 = (bf16[4,32,2560]{2,1,0:T(8,128)(2,1)S(1)}, bf16[4,32,2560]{2,1,0:T(8,128)(2,1)S(1)}, u32[]{:S(2)}, u32[]{:S(2)}) collective-permute-start(bf16[4,32,2560]{2,1,0:T(8,128)(2,1)S(1)} %slice.216), channel_id=1, source_target_pairs={{0,1},{1,0},{2,3},{3,2},{4,5},{5,4},{6,7},{7,6},{8,9},{9,8},{10,11... | collective-permute-start | bytes 1966088 | tf_op jit(solution)/shard_map/ppermute | solution.py:51
  117.3 21.9 %collective-permute-start.26 = (bf16[256,512]{1,0:T(8,128)(2,1)S(1)}, bf16[256,512]{1,0:T(8,128)(2,1)S(1)}, u32[]{:S(2)}, u32[]{:S(2)}) collective-permute-start(bf16[256,512]{1,0:T(8,128)(2,1)S(1)} %bitcast.307), channel_id=1, source_target_pairs={{0,3},{1,2},{2,1},{3,0},{4,7},{5,6},{6,5},{7,4},{8,11},{9,10},{10,... | collective-permute-start | bytes 786440 | tf_op jit(solution)/shard_map/ppermute | solution.py:51
  144.4 25.5 %collective-permute-start.34 = (bf16[4,128,1024]{2,1,0:T(8,128)(2,1)}, bf16[4,128,1024]{2,1,0:T(8,128)(2,1)}, u32[]{:S(2)}, u32[]{:S(2)}) collective-permute-start(bf16[4,128,1024]{2,1,0:T(8,128)(2,1)} %bitcast.44.refs_0_), channel_id=1, source_target_pairs={{0,1},{1,0},{2,3},{3,2},{4,5},{5,4},{6,7},{7,6},{8,9},{9,8},{10,11... | collective-permute-start | bytes 3145736 | tf_op jit(solution)/shard_map/ppermute | solution.py:51
  146.0 25.4 %collective-permute-start.35 = (bf16[4,128,1024]{2,1,0:T(8,128)(2,1)}, bf16[4,128,1024]{2,1,0:T(8,128)(2,1)}, u32[]{:S(2)}, u32[]{:S(2)}) collective-permute-start(bf16[4,128,1024]{2,1,0:T(8,128)(2,1)} %bitcast.44.refs_0_), channel_id=1, source_target_pairs={{0,2},{1,3},{2,0},{3,1},{4,6},{5,7},{6,4},{7,5},{8,10},{9,11},{10,... | collective-permute-start | bytes 3145736 | tf_op jit(solution)/shard_map/ppermute | solution.py:51
  219.2 169.9 %reduce-scatter.7.cloned.1.call-start = ((), (), s32[]{:S(2)}) async-start(), calls=%async_computation.7 | async-start | bytes 6553600 | tf_op jit(solution)/shard_map/reduce_scatter | solution.py:137
  292.8 128.2 %reduce-scatter.11.cloned.1.call-start = ((), (), s32[]{:S(2)}) async-start(), calls=%async_computation.9 | async-start | bytes 1310720 | tf_op jit(solution)/shard_map/reduce_scatter | solution.py:141
  293.4 145.3 %reduce-scatter.9.cloned.1.call-start = ((), (), s32[]{:S(2)}) async-start(), calls=%async_computation.8 | async-start | bytes 1638400 | tf_op jit(solution)/shard_map/reduce_scatter | solution.py:141
  346.5 42.6 %collective-permute-start.52 = (bf16[512,1024]{1,0:T(8,128)(2,1)}, bf16[512,1024]{1,0:T(8,128)(2,1)}, u32[]{:S(2)}, u32[]{:S(2)}) collective-permute-start(bf16[512,1024]{1,0:T(8,128)(2,1)} %convolution_convert_fusion.2), channel_id=1, source_target_pairs={{0,1},{1,0},{2,3},{3,2},{4,5},{5,4},{6,7},{7,6},{8,9},{9,8},{10,11... | collective-permute-start | bytes 3145736 | tf_op jit(solution)/shard_map/ppermute | solution.py:51
  349.8 30.7 %collective-permute-start.54 = (f32[4,384]{1,0:T(4,128)S(1)}, f32[4,384]{1,0:T(4,128)S(1)}, u32[]{:S(2)}, u32[]{:S(2)}) collective-permute-start(f32[4,384]{1,0:T(4,128)S(1)} %bitcast.345), channel_id=1, source_target_pairs={{0,1},{1,0},{2,3},{3,2},{4,5},{5,4},{6,7},{7,6},{8,9},{9,8},{10,11... | collective-permute-start | bytes 18440 | tf_op jit(solution)/shard_map/ppermute | solution.py:51
  350.4 30.1 %collective-permute-start.55 = (f32[4,384]{1,0:T(4,128)S(1)}, f32[4,384]{1,0:T(4,128)S(1)}, u32[]{:S(2)}, u32[]{:S(2)}) collective-permute-start(f32[4,384]{1,0:T(4,128)S(1)} %bitcast.346), channel_id=1, source_target_pairs={{0,2},{1,3},{2,0},{3,1},{4,6},{5,7},{6,4},{7,5},{8,10},{9,11},{10,... | collective-permute-start | bytes 18440 | tf_op jit(solution)/shard_map/ppermute | solution.py:51
  351.7 29.8 %collective-permute-start.56 = (f32[4,384]{1,0:T(4,128)S(1)}, f32[4,384]{1,0:T(4,128)S(1)}, u32[]{:S(2)}, u32[]{:S(2)}) collective-permute-start(f32[4,384]{1,0:T(4,128)S(1)} %bitcast.347), channel_id=1, source_target_pairs={{0,3},{1,2},{2,1},{3,0},{4,7},{5,6},{6,5},{7,4},{8,11},{9,10},{10,... | collective-permute-start | bytes 18440 | tf_op jit(solution)/shard_map/ppermute | solution.py:51
  392.6 48.3 %collective-permute-start.60 = (bf16[512,1024]{1,0:T(8,128)(2,1)}, bf16[512,1024]{1,0:T(8,128)(2,1)}, u32[]{:S(2)}, u32[]{:S(2)}) collective-permute-start(bf16[512,1024]{1,0:T(8,128)(2,1)} %convolution_convert_fusion.1), channel_id=1, source_target_pairs={{0,2},{1,3},{2,0},{3,1},{4,6},{5,7},{6,4},{7,5},{8,10},{9,11},{10,... | collective-permute-start | bytes 3145736 | tf_op jit(solution)/shard_map/ppermute | solution.py:51
  395.5 45.4 %collective-permute-start.61 = (bf16[512,1024]{1,0:T(8,128)(2,1)}, bf16[512,1024]{1,0:T(8,128)(2,1)}, u32[]{:S(2)}, u32[]{:S(2)}) collective-permute-start(bf16[512,1024]{1,0:T(8,128)(2,1)} %convolution_convert_fusion), channel_id=1, source_target_pairs={{0,3},{1,2},{2,1},{3,0},{4,7},{5,6},{6,5},{7,4},{8,11},{9,10},{10,... | collective-permute-start | bytes 3145736 | tf_op jit(solution)/shard_map/ppermute | solution.py:51
  397.8 23.1 %collective-permute-start.50 = (bf16[4,32,768]{2,1,0:T(8,128)(2,1)S(1)}, bf16[4,32,768]{2,1,0:T(8,128)(2,1)S(1)}, u32[]{:S(2)}, u32[]{:S(2)}) collective-permute-start(bf16[4,32,768]{2,1,0:T(8,128)(2,1)S(1)} %get-tuple-element.179), channel_id=1, source_target_pairs={{0,16},{8,24},{16,0},{24,8},{1,17},{9,25},{17,1},{25,9},{2,18},{10... | collective-permute-start | bytes 589832 | tf_op jit(solution)/shard_map/ppermute | solution.py:56
  (112 other events, 909.3 us)
Sparse Core Ops, SparseCore 0:
  35.9 43.1 all-gather.2
  80.7 25.3 all-gather.4
  219.3 56.3 reduce-scatter.4
  292.9 75.3 reduce-scatter.6
  370.6 29.9 reduce-scatter.10
  402.7 35.8 reduce-scatter.8

commit v4 on v3

--- a/solution.py
+++ b/solution.py
@@ -425,7 +425,7 @@
 def feed_back(cot, hidden, slope, w_fc, w_proj, base):
     rows, width = cot.shape
     units = hidden.shape[1]
-    block = min(512, units)
+    block = min(1024, units)
     whole = pl.BlockSpec((rows, width), lambda i: (0, 0))
     columns = pl.BlockSpec((rows, block), lambda i: (0, i))
     return pl.pallas_call(
@@ -733,6 +733,7 @@
     _, grad_attn = to_attention(jnp.stack(grad_slots), head)
     grad_attn = grad_attn.reshape(SLOTS, heads, HD, -1)
     grad_qkv = attend_back(me, qkv, attn, grad_attn, lse)
+    grad_qkv, shard_wproj = together(grad_qkv, shard_wproj)
     grad_qkv = from_attention(grad_qkv.reshape(SLOTS, 3 * group, -1), head, head_count)
 
     act_parts = [dot(grad_qkv[slot], group_w, 0, 1) for slot in range(head_count)]
@@ -764,8 +765,9 @@
     grad_group_w = grad_group_w.astype(BF16).reshape(grid + (own_rows, 3 * group))
     half_w = pick(grad_group_w, core, 1).astype(F32) + core_terms(grad_group_w, core).astype(F32)
     shard_w = scatter_z(half_w, dp)
-    act_terms[0], one_plane, mine = together(act_terms[0], one_plane, mine)
-    shard_w, shard_one, *act_terms = together(shard_w, scatter_dp(one_plane), *act_terms)
+    *near_terms, shard_w, one_plane = together(*act_terms[:2], shard_w, one_plane)
+    act_terms = near_terms + act_terms[2:]
+    mine, shard_one, *act_terms = together(mine, scatter_dp(one_plane), *act_terms)
     sums = plane_total(act_parts[0], act_terms).reshape(2, tok_rows, width)
     grad_act = by_half(
         core, pick(sums, core), to_other_core(pick(sums, 1 - core))

time: 468 us -> 448 us (0.957)
  waiting for transfers between devices: 155 us -> 125 us
  starting transfers between devices: 64.4 us -> 71.3 us
    reduce_scatter x2, waiting for transfers between devices: 14 us -> 0.02 us  [scatter_dp(): lax.psum_scatter(terms, 'dp', scatter_dimension=0, tiled=True).astype(F32)]
    ppermute x12, waiting for transfers between devices: 39.8 us -> 28.1 us  [to_shift(): lax.ppermute(value, 'dp', [(i, (i + step) % count) for i in range(count)])]
    ppermute x12, starting transfers between devices: 20.3 us -> 26.6 us  [to_shift(): lax.ppermute(value, 'dp', [(i, (i + step) % count) for i in range(count)])]
    unnamed x152 -> x150, local copies, waits for them, and re-layouts: 12 us -> 13 us
  transfers between devices with their start and end apart: 72 -> 72, of which waited for: 39 -> 31; matrix products, arithmetic and copies ran while one was open for 16% -> 17% of each run, Pallas kernels for 26% -> 27%
where the time goes in v4:
time: 448 us; the launch traced here: 442 us
  Pallas kernels  130 us (29%)
  waiting for transfers between devices  125 us (28%)
  starting transfers between devices  71.3 us (16%)
  other arithmetic  42.7 us (10%)
  local copies, waits for them, and re-layouts  34.4 us (8%)
  matrix products  22.2 us (5%)
  between operations  16.1 us (4%)
    ppermute x33, waiting for transfers between devices, to_xor(): return lax.ppermute(value, 'head', [(i, i ^ step) for i in range(count)])  68.7 us
    ppermute x33, starting transfers between devices, to_xor(): return lax.ppermute(value, 'head', [(i, i ^ step) for i in range(count)])  40.4 us
    pallas_call x1, Pallas kernels, attend_back(): pl.pallas_call(functools.partial(backward_kernel, block), out_shape=jax.S...  38.4 us
    ppermute x21, waiting for transfers between devices, to_other_core(): return lax.ppermute(value, 'blk', [(0, 1), (1, 0)])  28.2 us
    ppermute x12, waiting for transfers between devices, to_shift(): lax.ppermute(value, 'dp', [(i, (i + step) % count) for i in range(count)])  28.1 us
    ppermute x12, starting transfers between devices, to_shift(): lax.ppermute(value, 'dp', [(i, (i + step) % count) for i in range(count)])  26.6 us
    pallas_call x1, Pallas kernels, feed_back(): pl.pallas_call(feed_back_kernel, out_shape=(jax.ShapeDtypeStruct((rows, u...  21.3 us
    dot_general x12, matrix products, dot(): lax.dot_general(left, right, (((left_dim,), (right_dim,)), ((), ())), pre...  19.3 us
  transfers between devices with their start and end apart: 72, of which 31 were waited for; matrix products, arithmetic and copies ran while one was open for 17% of the time, Pallas kernels for 27%

profile of v4, /device:TPU:0, one launch (start us, length us, event | category | flops | bytes accessed | tf_op | source)
XLA Modules:
  0.0 441.6 jit_solution(11844371736399291696)
XLA Ops:
  8.9 3.1 collective-permute-start
  37.7 2.8 collective-permute-start.13
  42.6 4.6 %collective-permute-done.11 = bf16[32,3072]{1,0:T(8,128)(2,1)S(1)} collective-permute-done((bf16[32,3072]{1,0:T(8,128)(2,1)S(1)}, bf16[32,3072]{1,0:T(8,128)(2,1)S(1)}, u32[]{:S(2)}, u32[]{:S(2)}) %collective-permute-start.11) | collective-permute-done | bytes 196640 | tf_op jit(solution)/shard_map/ppermute | solution.py:56
  47.2 15.5 %collective-permute-done.12 = bf16[32,3072]{1,0:T(8,128)(2,1)S(1)} collective-permute-done((bf16[32,3072]{1,0:T(8,128)(2,1)S(1)}, bf16[32,3072]{1,0:T(8,128)(2,1)S(1)}, u32[]{:S(2)}, u32[]{:S(2)}) %collective-permute-start.12) | collective-permute-done | bytes 196640 | tf_op jit(solution)/shard_map/ppermute | solution.py:56
  72.5 5.6 %collective-permute-done.20 = bf16[256,1024]{1,0:T(8,128)(2,1)} collective-permute-done((bf16[256,1024]{1,0:T(8,128)(2,1)S(1)}, bf16[256,1024]{1,0:T(8,128)(2,1)}, u32[]{:S(2)}, u32[]{:S(2)}) %collective-permute-start.20) | collective-permute-done | bytes 524320 | tf_op jit(solution)/shard_map/ppermute | solution.py:51
  89.7 18.8 %attend.1 = (bf16[4,4,64,512]{3,2,1,0:T(8,128)(2,1)S(1)}, f32[4,8,256]{2,1,0:T(8,128)S(1)}) custom-call(s32[1]{0:T(128)} %bitcast.2.me_ref, bf16[4,3,4,64,512]{4,3,2,1,0:T(8,128)(2,1)S(1)} %pad_maximum_fusion.qkv), custom_call_target="tpu_custom_call" | custom-call | flops 2147483648 | bytes 4194304 | tf_op jit(solution)/shard_map/attend/pallas_call | solution.py:303
  119.5 16.8 %collective-permute-done.24 = bf16[256,512]{1,0:T(8,128)(2,1)S(1)} collective-permute-done((bf16[256,512]{1,0:T(8,128)(2,1)S(1)}, bf16[256,512]{1,0:T(8,128)(2,1)S(1)}, u32[]{:S(2)}, u32[]{:S(2)}) %collective-permute-start.24) | collective-permute-done | bytes 262176 | tf_op jit(solution)/shard_map/ppermute | solution.py:51
  151.5 8.5 %place.4 = (bf16[4,2,4,32,4096]{4,3,2,1,0:T(8,128)(2,1)}, bf16[4,2,4,32,1024]{4,3,2,1,0:T(8,128)(2,1)}) custom-call(s32[3]{0:T(128)S(1)} %pad_add_fusion.ids, bf16[4,32,5120]{2,1,0:T(8,128)(2,1)} %bitcast.37.refs_0_, bf16[4,32,5120]{2,1,0:T(8,128)(2,1)} %collective-permute-done.22.refs_1_, bf16[4,32,5120]{2,1,0:T(8,128)(2,1)} %collective-permute-done.23.refs_2_, ...), custom_call_target="tpu_custom_call" | custom-call | tf_op jit(solution)/shard_map/place/pallas_call | solution.py:98
  167.1 2.8 collective-permute-done.34.refs_1_
  176.9 13.6 %feed.1 = (bf16[512,4096]{1,0:T(8,128)(2,1)S(1)}, f32[512,4096]{1,0:T(8,128)}) custom-call(bf16[512,1024]{1,0:T(8,128)(2,1)S(1)} %add_convert_fusion.2.ctx.left, bf16[1024,4096]{1,0:T(8,128)(2,1)} %bitcast.364, f32[1,4096]{1,0:T(1,128)S(1)} %bitcast.267), custom_call_target="tpu_custom_call" | custom-call | flops 4294967296 | bytes 20971520 | tf_op jit(solution)/shard_map/feed/pallas_call | solution.py:372
  192.5 9.1 %weight_terms.1 = (bf16[4,4,128,1024]{3,2,1,0:T(8,128)(2,1)S(1)}, bf16[4,4,128,1024]{3,2,1,0:T(8,128)(2,1)}) custom-call(s32[3]{0:T(128)S(1)} %pad_add_fusion.ids, bf16[512,4096]{1,0:T(8,128)(2,1)} %copy-done.11, bf16[512,1024]{1,0:T(8,128)(2,1)S(1)} %get-tuple-element.100.right.cot), custom_call_target="tpu_custom_call" | custom-call | flops 4294967296 | bytes 8388608 | tf_op jit(solution)/shard_map/weight_terms/pallas_call | solution.py:512
  202.6 12.3 %collective-permute-done.38 = bf16[4,4,128,1024]{3,2,1,0:T(8,128)(2,1)S(1)} collective-permute-done((bf16[4,4,128,1024]{3,2,1,0:T(8,128)(2,1)}, bf16[4,4,128,1024]{3,2,1,0:T(8,128)(2,1)S(1)}, u32[]{:S(2)}, u32[]{:S(2)}) %collective-permute-start.38) | collective-permute-done | bytes 4194336 | tf_op jit(solution)/shard_map/ppermute | solution.py:60
  214.9 4.3 add_convert_fusion.1
  219.3 7.4 %place.5 = bf16[4,2,4,128,1024]{4,3,2,1,0:T(8,128)(2,1)} custom-call(s32[3]{0:T(128)S(1)} %pad_add_fusion.ids, bf16[4,128,1024]{2,1,0:T(8,128)(2,1)} %bitcast.44.refs_0_, bf16[4,128,1024]{2,1,0:T(8,128)(2,1)} %collective-permute-done.34.refs_1_, bf16[4,128,1024]{2,1,0:T(8,128)(2,1)} %collective-permute-done.35.refs_2_, ...), custom_call_target="tpu_custom_call" | custom-call | tf_op jit(solution)/shard_map/place/pallas_call | solution.py:98
  226.8 21.3 %feed_back.1 = (bf16[512,4096]{1,0:T(8,128)(2,1)}, f32[1,4096]{1,0:T(1,128)S(1)}, f32[512,1024]{1,0:T(8,128)S(1)}, f32[512,1024]{1,0:T(8,128)}) custom-call(bf16[512,1024]{1,0:T(8,128)(2,1)S(1)} %copy-done.10, bf16[512,4096]{1,0:T(8,128)(2,1)} %copy-done.11, f32[512,4096]{1,0:T(8,128)} %get-tuple-element.101.slope, bf16[1024,4096]{1,0:T(8,128)(2,1)} %bitcast.365, ...), custom_call_target="tpu_custom_call" | custom-call | flops 12884901888 | bytes 33554432 | tf_op jit(solution)/shard_map/feed_back/pallas_call | solution.py:431
  252.7 11.7 %weight_pair_terms.1 = (bf16[4,4,32,5120]{3,2,1,0:T(8,128)(2,1)}, bf16[4,4,32,5120]{3,2,1,0:T(8,128)(2,1)}) custom-call(s32[3]{0:T(128)S(1)} %pad_add_fusion.ids, bf16[512,1024]{1,0:T(8,128)(2,1)S(1)} %copy-done.8, bf16[512,4096]{1,0:T(8,128)(2,1)} %get-tuple-element.110.right, bf16[2,4,256,256]{3,2,1,0:T(8,128)(2,1)S(1)} %copy-done.4, ...), custom_call_target="tpu_custom_call" | custom-call | flops 5368709120 | bytes 10485760 | tf_op jit(solution)/shard_map/weight_pair_terms/pallas_call | solution.py:531
  267.6 6.5 %collective-permute-done.43 = bf16[4,256,256]{2,1,0:T(8,128)(2,1)S(1)} collective-permute-done((bf16[4,256,256]{2,1,0:T(8,128)(2,1)}, bf16[4,256,256]{2,1,0:T(8,128)(2,1)S(1)}, u32[]{:S(2)}, u32[]{:S(2)}) %collective-permute-start.43) | collective-permute-done | bytes 524320 | tf_op jit(solution)/shard_map/ppermute | solution.py:60
  280.2 8.3 %add_convert_fusion = bf16[4,4,32,5120]{3,2,1,0:T(8,128)(2,1)} fusion(bf16[4,4,32,5120]{3,2,1,0:T(8,128)(2,1)} %collective-permute-done.47, bf16[4,4,32,5120]{3,2,1,0:T(8,128)(2,1)} %get-tuple-element.111), kind=kLoop, calls=%fused_computation | loop fusion | flops 10485760 | bytes 15728640 | tf_op jit(solution)/shard_map/convert_element_type | solution.py:132
  293.0 38.4 %attend_back.1 = bf16[4,3,4,64,512]{4,3,2,1,0:T(8,128)(2,1)S(1)} custom-call(s32[1]{0:T(128)} %bitcast.2.me_ref, bf16[4,3,4,64,512]{4,3,2,1,0:T(8,128)(2,1)} %copy-done.1, bf16[4,4,64,512]{3,2,1,0:T(8,128)(2,1)S(1)} %copy-done.6, bf16[4,4,64,512]{3,2,1,0:T(8,128)(2,1)S(1)} %pad_maximum_fusion.6.grad_attn, f32[4,8,256]{2,1,0:T(8,128)S(1)} %get-tuple-element.117.lse), custom_call_target="tpu_custom_call" | custom-call | flops 5368709120 | bytes 8388608 | tf_op jit(solution)/shard_map/attend_back/pallas_call | solution.py:333
  353.5 3.6 fusion.51
  358.5 7.7 %collective-permute-start.58 = (bf16[4,32,768]{2,1,0:T(8,128)(2,1)S(1)}, bf16[4,32,768]{2,1,0:T(8,128)(2,1)S(1)}, u32[]{:S(2)}, u32[]{:S(2)}) collective-permute-start(bf16[4,32,768]{2,1,0:T(8,128)(2,1)S(1)} %get-tuple-element.183), channel_id=1, source_target_pairs={{0,8},{8,16},{16,24},{24,0},{1,9},{9,17},{17,25},{25,1},{2,10},{10... | collective-permute-start | bytes 589832 | tf_op jit(solution)/shard_map/ppermute | solution.py:56
  372.9 5.3 %collective-permute-done.59 = bf16[4,32,768]{2,1,0:T(8,128)(2,1)S(1)} collective-permute-done((bf16[4,32,768]{2,1,0:T(8,128)(2,1)S(1)}, bf16[4,32,768]{2,1,0:T(8,128)(2,1)S(1)}, u32[]{:S(2)}, u32[]{:S(2)}) %collective-permute-start.59) | collective-permute-done | bytes 196640 | tf_op jit(solution)/shard_map/ppermute | solution.py:56
  381.3 7.1 %collective-permute-done.55 = bf16[512,1024]{1,0:T(8,128)(2,1)} collective-permute-done((bf16[512,1024]{1,0:T(8,128)(2,1)}, bf16[512,1024]{1,0:T(8,128)(2,1)}, u32[]{:S(2)}, u32[]{:S(2)}) %collective-permute-start.55) | collective-permute-done | bytes 1048608 | tf_op jit(solution)/shard_map/ppermute | solution.py:51
  403.9 19.5 %collective-permute-done.64 = f32[32,768]{1,0:T(8,128)S(1)} collective-permute-done((f32[32,768]{1,0:T(8,128)S(1)}, f32[32,768]{1,0:T(8,128)S(1)}, u32[]{:S(2)}, u32[]{:S(2)}) %collective-permute-start.64) | collective-permute-done | bytes 98336 | tf_op jit(solution)/shard_map/ppermute | solution.py:51
  (419 shorter events, 170.9 us)
Async XLA Ops:
  7.2 74.6 %all-gather.3.cloned.1.call-start = ((), (), s32[]{:S(2)}) async-start(), calls=%async_computation.4 | async-start | bytes 1638400 | tf_op jit(solution)/shard_map/all_gather | solution.py:120
  35.7 74.5 %all-gather.5.cloned.1.call-start = ((), (), s32[]{:S(2)}) async-start(), calls=%async_computation.5 | async-start | bytes 1310720 | tf_op jit(solution)/shard_map/all_gather | solution.py:120
  37.4 25.3 %collective-permute-start.12 = (bf16[32,3072]{1,0:T(8,128)(2,1)S(1)}, bf16[32,3072]{1,0:T(8,128)(2,1)S(1)}, u32[]{:S(2)}, u32[]{:S(2)}) collective-permute-start(bf16[32,3072]{1,0:T(8,128)(2,1)S(1)} %pad_maximum_fusion.13), channel_id=1, source_target_pairs={{0,16},{8,24},{16,0},{24,8},{1,17},{9,25},{17,1},{25,9},{2,18},{10... | collective-permute-start | bytes 589832 | tf_op jit(solution)/shard_map/ppermute | solution.py:56
  37.7 24.9 %collective-permute-start.13 = (bf16[32,3072]{1,0:T(8,128)(2,1)S(1)}, bf16[32,3072]{1,0:T(8,128)(2,1)S(1)}, u32[]{:S(2)}, u32[]{:S(2)}) collective-permute-start(bf16[32,3072]{1,0:T(8,128)(2,1)S(1)} %pad_maximum_fusion.13), channel_id=1, source_target_pairs={{0,24},{8,0},{16,8},{24,16},{1,25},{9,1},{17,9},{25,17},{2,26},{10... | collective-permute-start | bytes 589832 | tf_op jit(solution)/shard_map/ppermute | solution.py:56
  40.5 24.7 %collective-permute-start.18 = (bf16[512,1024]{1,0:T(8,128)(2,1)S(1)}, bf16[512,1024]{1,0:T(8,128)(2,1)S(1)}, u32[]{:S(2)}, u32[]{:S(2)}) collective-permute-start(bf16[512,1024]{1,0:T(8,128)(2,1)S(1)} %bitcast.272), channel_id=1, source_target_pairs={{0,1},{1,0},{2,3},{3,2},{4,5},{5,4},{6,7},{7,6},{8,9},{9,8},{10,11... | collective-permute-start | bytes 3145736 | tf_op jit(solution)/shard_map/ppermute | solution.py:51
  41.1 25.9 %collective-permute-start.19 = (bf16[512,1024]{1,0:T(8,128)(2,1)S(1)}, bf16[512,1024]{1,0:T(8,128)(2,1)S(1)}, u32[]{:S(2)}, u32[]{:S(2)}) collective-permute-start(bf16[512,1024]{1,0:T(8,128)(2,1)S(1)} %bitcast.273), channel_id=1, source_target_pairs={{0,2},{1,3},{2,0},{3,1},{4,6},{5,7},{6,4},{7,5},{8,10},{9,11},{10,... | collective-permute-start | bytes 3145736 | tf_op jit(solution)/shard_map/ppermute | solution.py:51
  68.5 208.0 %reduce-scatter.5.cloned.1.call-start = ((), (), s32[]{:S(2)}) async-start(), calls=%async_computation.6 | async-start | bytes 5242880 | tf_op jit(solution)/shard_map/reduce_scatter | solution.py:137
  81.8 28.7 %collective-permute-start.22 = (bf16[4,32,5120]{2,1,0:T(8,128)(2,1)}, bf16[4,32,5120]{2,1,0:T(8,128)(2,1)}, u32[]{:S(2)}, u32[]{:S(2)}) collective-permute-start(bf16[4,32,5120]{2,1,0:T(8,128)(2,1)} %bitcast.37.refs_0_), channel_id=1, source_target_pairs={{0,1},{1,0},{2,3},{3,2},{4,5},{5,4},{6,7},{7,6},{8,9},{9,8},{10,11... | collective-permute-start | bytes 3932168 | tf_op jit(solution)/shard_map/ppermute | solution.py:51
  82.3 28.3 %collective-permute-start.23 = (bf16[4,32,5120]{2,1,0:T(8,128)(2,1)}, bf16[4,32,5120]{2,1,0:T(8,128)(2,1)}, u32[]{:S(2)}, u32[]{:S(2)}) collective-permute-start(bf16[4,32,5120]{2,1,0:T(8,128)(2,1)} %bitcast.37.refs_0_), channel_id=1, source_target_pairs={{0,2},{1,3},{2,0},{3,1},{4,6},{5,7},{6,4},{7,5},{8,10},{9,11},{10,... | collective-permute-start | bytes 3932168 | tf_op jit(solution)/shard_map/ppermute | solution.py:51
  111.8 27.7 %collective-permute-start.28 = (bf16[4,32,2560]{2,1,0:T(8,128)(2,1)S(1)}, bf16[4,32,2560]{2,1,0:T(8,128)(2,1)S(1)}, u32[]{:S(2)}, u32[]{:S(2)}) collective-permute-start(bf16[4,32,2560]{2,1,0:T(8,128)(2,1)S(1)} %slice.215), channel_id=1, source_target_pairs={{0,2},{1,3},{2,0},{3,1},{4,6},{5,7},{6,4},{7,5},{8,10},{9,11},{10,... | collective-permute-start | bytes 1966088 | tf_op jit(solution)/shard_map/ppermute | solution.py:51
  114.2 25.2 %collective-permute-start.29 = (bf16[4,32,2560]{2,1,0:T(8,128)(2,1)S(1)}, bf16[4,32,2560]{2,1,0:T(8,128)(2,1)S(1)}, u32[]{:S(2)}, u32[]{:S(2)}) collective-permute-start(bf16[4,32,2560]{2,1,0:T(8,128)(2,1)S(1)} %slice.216), channel_id=1, source_target_pairs={{0,1},{1,0},{2,3},{3,2},{4,5},{5,4},{6,7},{7,6},{8,9},{9,8},{10,11... | collective-permute-start | bytes 1966088 | tf_op jit(solution)/shard_map/ppermute | solution.py:51
  117.2 21.9 %collective-permute-start.26 = (bf16[256,512]{1,0:T(8,128)(2,1)S(1)}, bf16[256,512]{1,0:T(8,128)(2,1)S(1)}, u32[]{:S(2)}, u32[]{:S(2)}) collective-permute-start(bf16[256,512]{1,0:T(8,128)(2,1)S(1)} %bitcast.307), channel_id=1, source_target_pairs={{0,3},{1,2},{2,1},{3,0},{4,7},{5,6},{6,5},{7,4},{8,11},{9,10},{10,... | collective-permute-start | bytes 786440 | tf_op jit(solution)/shard_map/ppermute | solution.py:51
  144.4 25.5 %collective-permute-start.34 = (bf16[4,128,1024]{2,1,0:T(8,128)(2,1)}, bf16[4,128,1024]{2,1,0:T(8,128)(2,1)}, u32[]{:S(2)}, u32[]{:S(2)}) collective-permute-start(bf16[4,128,1024]{2,1,0:T(8,128)(2,1)} %bitcast.44.refs_0_), channel_id=1, source_target_pairs={{0,1},{1,0},{2,3},{3,2},{4,5},{5,4},{6,7},{7,6},{8,9},{9,8},{10,11... | collective-permute-start | bytes 3145736 | tf_op jit(solution)/shard_map/ppermute | solution.py:51
  146.0 25.4 %collective-permute-start.35 = (bf16[4,128,1024]{2,1,0:T(8,128)(2,1)}, bf16[4,128,1024]{2,1,0:T(8,128)(2,1)}, u32[]{:S(2)}, u32[]{:S(2)}) collective-permute-start(bf16[4,128,1024]{2,1,0:T(8,128)(2,1)} %bitcast.44.refs_0_), channel_id=1, source_target_pairs={{0,2},{1,3},{2,0},{3,1},{4,6},{5,7},{6,4},{7,5},{8,10},{9,11},{10,... | collective-permute-start | bytes 3145736 | tf_op jit(solution)/shard_map/ppermute | solution.py:51
  219.2 113.9 %reduce-scatter.7.cloned.1.call-start = ((), (), s32[]{:S(2)}) async-start(), calls=%async_computation.7 | async-start | bytes 1310720 | tf_op jit(solution)/shard_map/reduce_scatter | solution.py:141
  276.5 114.6 %reduce-scatter.9.cloned.1.call-start = ((), (), s32[]{:S(2)}) async-start(), calls=%async_computation.8 | async-start | bytes 6553600 | tf_op jit(solution)/shard_map/reduce_scatter | solution.py:137
  291.5 132.1 %reduce-scatter.11.cloned.1.call-start = ((), (), s32[]{:S(2)}) async-start(), calls=%async_computation.9 | async-start | bytes 1638400 | tf_op jit(solution)/shard_map/reduce_scatter | solution.py:141
  348.3 40.1 %collective-permute-start.55 = (bf16[512,1024]{1,0:T(8,128)(2,1)}, bf16[512,1024]{1,0:T(8,128)(2,1)}, u32[]{:S(2)}, u32[]{:S(2)}) collective-permute-start(bf16[512,1024]{1,0:T(8,128)(2,1)} %convolution_convert_fusion.2), channel_id=1, source_target_pairs={{0,1},{1,0},{2,3},{3,2},{4,5},{5,4},{6,7},{7,6},{8,9},{9,8},{10,11... | collective-permute-start | bytes 3145736 | tf_op jit(solution)/shard_map/ppermute | solution.py:51
  352.0 39.2 %collective-permute-start.56 = (bf16[512,1024]{1,0:T(8,128)(2,1)}, bf16[512,1024]{1,0:T(8,128)(2,1)}, u32[]{:S(2)}, u32[]{:S(2)}) collective-permute-start(bf16[512,1024]{1,0:T(8,128)(2,1)} %convolution_convert_fusion.1), channel_id=1, source_target_pairs={{0,2},{1,3},{2,0},{3,1},{4,6},{5,7},{6,4},{7,5},{8,10},{9,11},{10,... | collective-permute-start | bytes 3145736 | tf_op jit(solution)/shard_map/ppermute | solution.py:51
  371.5 23.2 %collective-permute-start.49 = (f32[4,384]{1,0:T(4,128)S(1)}, f32[4,384]{1,0:T(4,128)S(1)}, u32[]{:S(2)}, u32[]{:S(2)}) collective-permute-start(f32[4,384]{1,0:T(4,128)S(1)} %bitcast.347), channel_id=1, source_target_pairs={{0,1},{1,0},{2,3},{3,2},{4,5},{5,4},{6,7},{7,6},{8,9},{9,8},{10,11... | collective-permute-start | bytes 18440 | tf_op jit(solution)/shard_map/ppermute | solution.py:51
  393.2 31.4 %collective-permute-start.61 = (bf16[512,1024]{1,0:T(8,128)(2,1)}, bf16[512,1024]{1,0:T(8,128)(2,1)}, u32[]{:S(2)}, u32[]{:S(2)}) collective-permute-start(bf16[512,1024]{1,0:T(8,128)(2,1)} %convolution_convert_fusion), channel_id=1, source_target_pairs={{0,3},{1,2},{2,1},{3,0},{4,7},{5,6},{6,5},{7,4},{8,11},{9,10},{10,... | collective-permute-start | bytes 3145736 | tf_op jit(solution)/shard_map/ppermute | solution.py:51
  400.3 23.0 %collective-permute-start.64 = (f32[32,768]{1,0:T(8,128)S(1)}, f32[32,768]{1,0:T(8,128)S(1)}, u32[]{:S(2)}, u32[]{:S(2)}) collective-permute-start(f32[32,768]{1,0:T(8,128)S(1)} %get-tuple-element.200), channel_id=1, source_target_pairs={{0,2},{1,3},{2,0},{3,1},{4,6},{5,7},{6,4},{7,5},{8,10},{9,11},{10,... | collective-permute-start | bytes 294920 | tf_op jit(solution)/shard_map/ppermute | solution.py:51
  401.8 21.6 %collective-permute-start.65 = (f32[32,768]{1,0:T(8,128)S(1)}, f32[32,768]{1,0:T(8,128)S(1)}, u32[]{:S(2)}, u32[]{:S(2)}) collective-permute-start(f32[32,768]{1,0:T(8,128)S(1)} %get-tuple-element.199), channel_id=1, source_target_pairs={{0,3},{1,2},{2,1},{3,0},{4,7},{5,6},{6,5},{7,4},{8,11},{9,10},{10,... | collective-permute-start | bytes 294920 | tf_op jit(solution)/shard_map/ppermute | solution.py:51
  402.9 20.5 %collective-permute-start.63 = (f32[32,768]{1,0:T(8,128)S(1)}, f32[32,768]{1,0:T(8,128)S(1)}, u32[]{:S(2)}, u32[]{:S(2)}) collective-permute-start(f32[32,768]{1,0:T(8,128)S(1)} %get-tuple-element.201), channel_id=1, source_target_pairs={{0,1},{1,0},{2,3},{3,2},{4,5},{5,4},{6,7},{7,6},{8,9},{9,8},{10,11... | collective-permute-start | bytes 294920 | tf_op jit(solution)/shard_map/ppermute | solution.py:51
  (111 other events, 862.8 us)
Sparse Core Ops, SparseCore 0:
  35.8 43.1 all-gather.2
  80.6 25.3 all-gather.4
  219.3 56.3 reduce-scatter.4
  278.0 29.1 reduce-scatter.6
  309.9 74.1 reduce-scatter.8
  391.3 30.7 reduce-scatter.10

commit v5 on v4

--- a/solution.py
+++ b/solution.py
@@ -138,7 +138,7 @@
 
 
 def scatter_dp(terms):
-    return lax.psum_scatter(terms, "dp", scatter_dimension=0, tiled=True).astype(F32)
+    return lax.psum_scatter(terms, "dp", scatter_dimension=0, tiled=True)
 
 
 def gather_z(shard):
@@ -767,7 +767,10 @@
     shard_w = scatter_z(half_w, dp)
     *near_terms, shard_w, one_plane = together(*act_terms[:2], shard_w, one_plane)
     act_terms = near_terms + act_terms[2:]
-    mine, shard_one, *act_terms = together(mine, scatter_dp(one_plane), *act_terms)
+    mine, shard_one, shard_wproj, *act_terms = together(
+        mine, scatter_dp(one_plane), shard_wproj, *act_terms
+    )
+    shard_one, shard_wproj = shard_one.astype(F32), shard_wproj.astype(F32)
     sums = plane_total(act_parts[0], act_terms).reshape(2, tok_rows, width)
     grad_act = by_half(
         core, pick(sums, core), to_other_core(pick(sums, 1 - core))

time: 448 us -> 446 us (level)
    unnamed x150 -> x154, local copies, waits for them, and re-layouts: 13 us -> 13.6 us
  transfers between devices with their start and end apart: 72 -> 72, of which waited for: 31 -> 32; matrix products, arithmetic and copies ran while one was open for 17% -> 17% of each run, Pallas kernels for 27% -> 27%
where the time goes in v5:
time: 446 us; the launch traced here: 440 us
  Pallas kernels  130 us (29%)
  waiting for transfers between devices  125 us (28%)
  starting transfers between devices  72.4 us (16%)
  other arithmetic  40.7 us (9%)
  local copies, waits for them, and re-layouts  35 us (8%)
  matrix products  21.4 us (5%)
  between operations  16.1 us (4%)
    ppermute x33, waiting for transfers between devices, to_xor(): return lax.ppermute(value, 'head', [(i, i ^ step) for i in range(count)])  67.3 us
    ppermute x33, starting transfers between devices, to_xor(): return lax.ppermute(value, 'head', [(i, i ^ step) for i in range(count)])  40.2 us
    pallas_call x1, Pallas kernels, attend_back(): pl.pallas_call(functools.partial(backward_kernel, block), out_shape=jax.S...  38.4 us
    ppermute x21, waiting for transfers between devices, to_other_core(): return lax.ppermute(value, 'blk', [(0, 1), (1, 0)])  28.2 us
    ppermute x12, waiting for transfers between devices, to_shift(): lax.ppermute(value, 'dp', [(i, (i + step) % count) for i in range(count)])  28.2 us
    ppermute x12, starting transfers between devices, to_shift(): lax.ppermute(value, 'dp', [(i, (i + step) % count) for i in range(count)])  28 us
    pallas_call x1, Pallas kernels, feed_back(): pl.pallas_call(feed_back_kernel, out_shape=(jax.ShapeDtypeStruct((rows, u...  21.3 us
    pallas_call x1, Pallas kernels, attend(): pl.pallas_call(functools.partial(forward_kernel, block), out_shape=(jax.S...  18.8 us
  transfers between devices with their start and end apart: 72, of which 32 were waited for; matrix products, arithmetic and copies ran while one was open for 17% of the time, Pallas kernels for 27%

profile of v5, /device:TPU:0, one launch (start us, length us, event | category | flops | bytes accessed | tf_op | source)
XLA Modules:
  0.0 440.2 jit_solution(16002751790811552477)
XLA Ops:
  8.9 3.1 collective-permute-start
  42.6 4.5 %collective-permute-done.11 = bf16[32,3072]{1,0:T(8,128)(2,1)S(1)} collective-permute-done((bf16[32,3072]{1,0:T(8,128)(2,1)S(1)}, bf16[32,3072]{1,0:T(8,128)(2,1)S(1)}, u32[]{:S(2)}, u32[]{:S(2)}) %collective-permute-start.11) | collective-permute-done | bytes 196640 | tf_op jit(solution)/shard_map/ppermute | solution.py:56
  47.2 15.5 %collective-permute-done.12 = bf16[32,3072]{1,0:T(8,128)(2,1)S(1)} collective-permute-done((bf16[32,3072]{1,0:T(8,128)(2,1)S(1)}, bf16[32,3072]{1,0:T(8,128)(2,1)S(1)}, u32[]{:S(2)}, u32[]{:S(2)}) %collective-permute-start.12) | collective-permute-done | bytes 196640 | tf_op jit(solution)/shard_map/ppermute | solution.py:56
  72.5 5.6 %collective-permute-done.20 = bf16[256,1024]{1,0:T(8,128)(2,1)} collective-permute-done((bf16[256,1024]{1,0:T(8,128)(2,1)S(1)}, bf16[256,1024]{1,0:T(8,128)(2,1)}, u32[]{:S(2)}, u32[]{:S(2)}) %collective-permute-start.20) | collective-permute-done | bytes 524320 | tf_op jit(solution)/shard_map/ppermute | solution.py:51
  89.7 18.8 %attend.1 = (bf16[4,4,64,512]{3,2,1,0:T(8,128)(2,1)S(1)}, f32[4,8,256]{2,1,0:T(8,128)S(1)}) custom-call(s32[1]{0:T(128)} %bitcast.2.me_ref, bf16[4,3,4,64,512]{4,3,2,1,0:T(8,128)(2,1)S(1)} %pad_maximum_fusion.qkv), custom_call_target="tpu_custom_call" | custom-call | flops 2147483648 | bytes 4194304 | tf_op jit(solution)/shard_map/attend/pallas_call | solution.py:303
  119.6 16.8 %collective-permute-done.24 = bf16[256,512]{1,0:T(8,128)(2,1)S(1)} collective-permute-done((bf16[256,512]{1,0:T(8,128)(2,1)S(1)}, bf16[256,512]{1,0:T(8,128)(2,1)S(1)}, u32[]{:S(2)}, u32[]{:S(2)}) %collective-permute-start.24) | collective-permute-done | bytes 262176 | tf_op jit(solution)/shard_map/ppermute | solution.py:51
  151.5 8.5 %place.4 = (bf16[4,2,4,32,4096]{4,3,2,1,0:T(8,128)(2,1)}, bf16[4,2,4,32,1024]{4,3,2,1,0:T(8,128)(2,1)}) custom-call(s32[3]{0:T(128)S(1)} %pad_add_fusion.ids, bf16[4,32,5120]{2,1,0:T(8,128)(2,1)} %bitcast.37.refs_0_, bf16[4,32,5120]{2,1,0:T(8,128)(2,1)} %collective-permute-done.22.refs_1_, bf16[4,32,5120]{2,1,0:T(8,128)(2,1)} %collective-permute-done.23.refs_2_, ...), custom_call_target="tpu_custom_call" | custom-call | tf_op jit(solution)/shard_map/place/pallas_call | solution.py:98
  176.9 13.5 %feed.1 = (bf16[512,4096]{1,0:T(8,128)(2,1)S(1)}, f32[512,4096]{1,0:T(8,128)}) custom-call(bf16[512,1024]{1,0:T(8,128)(2,1)S(1)} %add_convert_fusion.2.ctx.left, bf16[1024,4096]{1,0:T(8,128)(2,1)} %bitcast.364, f32[1,4096]{1,0:T(1,128)S(1)} %bitcast.267), custom_call_target="tpu_custom_call" | custom-call | flops 4294967296 | bytes 20971520 | tf_op jit(solution)/shard_map/feed/pallas_call | solution.py:372
  192.5 9.1 %weight_terms.1 = (bf16[4,4,128,1024]{3,2,1,0:T(8,128)(2,1)S(1)}, bf16[4,4,128,1024]{3,2,1,0:T(8,128)(2,1)}) custom-call(s32[3]{0:T(128)S(1)} %pad_add_fusion.ids, bf16[512,4096]{1,0:T(8,128)(2,1)} %copy-done.11, bf16[512,1024]{1,0:T(8,128)(2,1)S(1)} %get-tuple-element.101.right.cot), custom_call_target="tpu_custom_call" | custom-call | flops 4294967296 | bytes 8388608 | tf_op jit(solution)/shard_map/weight_terms/pallas_call | solution.py:512
  202.6 12.3 %collective-permute-done.38 = bf16[4,4,128,1024]{3,2,1,0:T(8,128)(2,1)S(1)} collective-permute-done((bf16[4,4,128,1024]{3,2,1,0:T(8,128)(2,1)}, bf16[4,4,128,1024]{3,2,1,0:T(8,128)(2,1)S(1)}, u32[]{:S(2)}, u32[]{:S(2)}) %collective-permute-start.38) | collective-permute-done | bytes 4194336 | tf_op jit(solution)/shard_map/ppermute | solution.py:60
  215.0 4.3 add_convert_fusion.1
  219.3 7.4 %place.5 = bf16[4,2,4,128,1024]{4,3,2,1,0:T(8,128)(2,1)} custom-call(s32[3]{0:T(128)S(1)} %pad_add_fusion.ids, bf16[4,128,1024]{2,1,0:T(8,128)(2,1)} %bitcast.44.refs_0_, bf16[4,128,1024]{2,1,0:T(8,128)(2,1)} %collective-permute-done.34.refs_1_, bf16[4,128,1024]{2,1,0:T(8,128)(2,1)} %collective-permute-done.35.refs_2_, ...), custom_call_target="tpu_custom_call" | custom-call | tf_op jit(solution)/shard_map/place/pallas_call | solution.py:98
  226.8 21.3 %feed_back.1 = (bf16[512,4096]{1,0:T(8,128)(2,1)}, f32[1,4096]{1,0:T(1,128)S(1)}, f32[512,1024]{1,0:T(8,128)S(1)}, f32[512,1024]{1,0:T(8,128)}) custom-call(bf16[512,1024]{1,0:T(8,128)(2,1)S(1)} %copy-done.10, bf16[512,4096]{1,0:T(8,128)(2,1)} %copy-done.11, f32[512,4096]{1,0:T(8,128)} %get-tuple-element.102.slope, bf16[1024,4096]{1,0:T(8,128)(2,1)} %bitcast.365, ...), custom_call_target="tpu_custom_call" | custom-call | flops 12884901888 | bytes 33554432 | tf_op jit(solution)/shard_map/feed_back/pallas_call | solution.py:431
  252.7 11.7 %weight_pair_terms.1 = (bf16[4,4,32,5120]{3,2,1,0:T(8,128)(2,1)}, bf16[4,4,32,5120]{3,2,1,0:T(8,128)(2,1)}) custom-call(s32[3]{0:T(128)S(1)} %pad_add_fusion.ids, bf16[512,1024]{1,0:T(8,128)(2,1)S(1)} %copy-done.8, bf16[512,4096]{1,0:T(8,128)(2,1)} %get-tuple-element.111.right, bf16[2,4,256,256]{3,2,1,0:T(8,128)(2,1)S(1)} %copy-done.4, ...), custom_call_target="tpu_custom_call" | custom-call | flops 5368709120 | bytes 10485760 | tf_op jit(solution)/shard_map/weight_pair_terms/pallas_call | solution.py:531
  267.5 6.5 %collective-permute-done.43 = bf16[4,256,256]{2,1,0:T(8,128)(2,1)S(1)} collective-permute-done((bf16[4,256,256]{2,1,0:T(8,128)(2,1)}, bf16[4,256,256]{2,1,0:T(8,128)(2,1)S(1)}, u32[]{:S(2)}, u32[]{:S(2)}) %collective-permute-start.43) | collective-permute-done | bytes 524320 | tf_op jit(solution)/shard_map/ppermute | solution.py:60
  280.1 8.4 %add_convert_fusion = bf16[4,4,32,5120]{3,2,1,0:T(8,128)(2,1)} fusion(bf16[4,4,32,5120]{3,2,1,0:T(8,128)(2,1)} %collective-permute-done.47, bf16[4,4,32,5120]{3,2,1,0:T(8,128)(2,1)} %get-tuple-element.112), kind=kLoop, calls=%fused_computation | loop fusion | flops 10485760 | bytes 15728640 | tf_op jit(solution)/shard_map/convert_element_type | solution.py:132
  293.0 38.4 %attend_back.1 = bf16[4,3,4,64,512]{4,3,2,1,0:T(8,128)(2,1)S(1)} custom-call(s32[1]{0:T(128)} %bitcast.2.me_ref, bf16[4,3,4,64,512]{4,3,2,1,0:T(8,128)(2,1)} %copy-done.1, bf16[4,4,64,512]{3,2,1,0:T(8,128)(2,1)S(1)} %copy-done.6, bf16[4,4,64,512]{3,2,1,0:T(8,128)(2,1)S(1)} %pad_maximum_fusion.6.grad_attn, f32[4,8,256]{2,1,0:T(8,128)S(1)} %get-tuple-element.118.lse), custom_call_target="tpu_custom_call" | custom-call | flops 5368709120 | bytes 8388608 | tf_op jit(solution)/shard_map/attend_back/pallas_call | solution.py:333
  351.8 3.8 fusion.51
  357.0 7.6 %collective-permute-start.58 = (bf16[4,32,768]{2,1,0:T(8,128)(2,1)S(1)}, bf16[4,32,768]{2,1,0:T(8,128)(2,1)S(1)}, u32[]{:S(2)}, u32[]{:S(2)}) collective-permute-start(bf16[4,32,768]{2,1,0:T(8,128)(2,1)S(1)} %get-tuple-element.185), channel_id=1, source_target_pairs={{0,8},{8,16},{16,24},{24,0},{1,9},{9,17},{17,25},{25,1},{2,10},{10... | collective-permute-start | bytes 589832 | tf_op jit(solution)/shard_map/ppermute | solution.py:56
  371.3 5.4 %collective-permute-done.59 = bf16[4,32,768]{2,1,0:T(8,128)(2,1)S(1)} collective-permute-done((bf16[4,32,768]{2,1,0:T(8,128)(2,1)S(1)}, bf16[4,32,768]{2,1,0:T(8,128)(2,1)S(1)}, u32[]{:S(2)}, u32[]{:S(2)}) %collective-permute-start.59) | collective-permute-done | bytes 196640 | tf_op jit(solution)/shard_map/ppermute | solution.py:56
  379.6 6.9 %collective-permute-done.55 = bf16[512,1024]{1,0:T(8,128)(2,1)} collective-permute-done((bf16[512,1024]{1,0:T(8,128)(2,1)}, bf16[512,1024]{1,0:T(8,128)(2,1)}, u32[]{:S(2)}, u32[]{:S(2)}) %collective-permute-start.55) | collective-permute-done | bytes 1048608 | tf_op jit(solution)/shard_map/ppermute | solution.py:51
  386.5 3.4 collective-permute-done.56
  396.3 3.1 collective-permute-start.54
  403.0 17.6 %collective-permute-done.64 = f32[32,768]{1,0:T(8,128)S(1)} collective-permute-done((f32[32,768]{1,0:T(8,128)S(1)}, f32[32,768]{1,0:T(8,128)S(1)}, u32[]{:S(2)}, u32[]{:S(2)}) %collective-permute-start.64) | collective-permute-done | bytes 98336 | tf_op jit(solution)/shard_map/ppermute | solution.py:51
  (422 shorter events, 170.6 us)
Async XLA Ops:
  7.2 74.6 %all-gather.3.cloned.1.call-start = ((), (), s32[]{:S(2)}) async-start(), calls=%async_computation.4 | async-start | bytes 1638400 | tf_op jit(solution)/shard_map/all_gather | solution.py:120
  35.7 74.5 %all-gather.5.cloned.1.call-start = ((), (), s32[]{:S(2)}) async-start(), calls=%async_computation.5 | async-start | bytes 1310720 | tf_op jit(solution)/shard_map/all_gather | solution.py:120
  37.4 25.3 %collective-permute-start.12 = (bf16[32,3072]{1,0:T(8,128)(2,1)S(1)}, bf16[32,3072]{1,0:T(8,128)(2,1)S(1)}, u32[]{:S(2)}, u32[]{:S(2)}) collective-permute-start(bf16[32,3072]{1,0:T(8,128)(2,1)S(1)} %pad_maximum_fusion.13), channel_id=1, source_target_pairs={{0,16},{8,24},{16,0},{24,8},{1,17},{9,25},{17,1},{25,9},{2,18},{10... | collective-permute-start | bytes 589832 | tf_op jit(solution)/shard_map/ppermute | solution.py:56
  37.8 24.9 %collective-permute-start.13 = (bf16[32,3072]{1,0:T(8,128)(2,1)S(1)}, bf16[32,3072]{1,0:T(8,128)(2,1)S(1)}, u32[]{:S(2)}, u32[]{:S(2)}) collective-permute-start(bf16[32,3072]{1,0:T(8,128)(2,1)S(1)} %pad_maximum_fusion.13), channel_id=1, source_target_pairs={{0,24},{8,0},{16,8},{24,16},{1,25},{9,1},{17,9},{25,17},{2,26},{10... | collective-permute-start | bytes 589832 | tf_op jit(solution)/shard_map/ppermute | solution.py:56
  40.6 24.7 %collective-permute-start.18 = (bf16[512,1024]{1,0:T(8,128)(2,1)S(1)}, bf16[512,1024]{1,0:T(8,128)(2,1)S(1)}, u32[]{:S(2)}, u32[]{:S(2)}) collective-permute-start(bf16[512,1024]{1,0:T(8,128)(2,1)S(1)} %bitcast.272), channel_id=1, source_target_pairs={{0,1},{1,0},{2,3},{3,2},{4,5},{5,4},{6,7},{7,6},{8,9},{9,8},{10,11... | collective-permute-start | bytes 3145736 | tf_op jit(solution)/shard_map/ppermute | solution.py:51
  41.1 25.9 %collective-permute-start.19 = (bf16[512,1024]{1,0:T(8,128)(2,1)S(1)}, bf16[512,1024]{1,0:T(8,128)(2,1)S(1)}, u32[]{:S(2)}, u32[]{:S(2)}) collective-permute-start(bf16[512,1024]{1,0:T(8,128)(2,1)S(1)} %bitcast.273), channel_id=1, source_target_pairs={{0,2},{1,3},{2,0},{3,1},{4,6},{5,7},{6,4},{7,5},{8,10},{9,11},{10,... | collective-permute-start | bytes 3145736 | tf_op jit(solution)/shard_map/ppermute | solution.py:51
  68.5 207.9 %reduce-scatter.5.cloned.1.call-start = ((), (), s32[]{:S(2)}) async-start(), calls=%async_computation.6 | async-start | bytes 5242880 | tf_op jit(solution)/shard_map/reduce_scatter | solution.py:137
  81.8 28.7 %collective-permute-start.22 = (bf16[4,32,5120]{2,1,0:T(8,128)(2,1)}, bf16[4,32,5120]{2,1,0:T(8,128)(2,1)}, u32[]{:S(2)}, u32[]{:S(2)}) collective-permute-start(bf16[4,32,5120]{2,1,0:T(8,128)(2,1)} %bitcast.37.refs_0_), channel_id=1, source_target_pairs={{0,1},{1,0},{2,3},{3,2},{4,5},{5,4},{6,7},{7,6},{8,9},{9,8},{10,11... | collective-permute-start | bytes 3932168 | tf_op jit(solution)/shard_map/ppermute | solution.py:51
  82.3 28.3 %collective-permute-start.23 = (bf16[4,32,5120]{2,1,0:T(8,128)(2,1)}, bf16[4,32,5120]{2,1,0:T(8,128)(2,1)}, u32[]{:S(2)}, u32[]{:S(2)}) collective-permute-start(bf16[4,32,5120]{2,1,0:T(8,128)(2,1)} %bitcast.37.refs_0_), channel_id=1, source_target_pairs={{0,2},{1,3},{2,0},{3,1},{4,6},{5,7},{6,4},{7,5},{8,10},{9,11},{10,... | collective-permute-start | bytes 3932168 | tf_op jit(solution)/shard_map/ppermute | solution.py:51
  111.8 27.7 %collective-permute-start.28 = (bf16[4,32,2560]{2,1,0:T(8,128)(2,1)S(1)}, bf16[4,32,2560]{2,1,0:T(8,128)(2,1)S(1)}, u32[]{:S(2)}, u32[]{:S(2)}) collective-permute-start(bf16[4,32,2560]{2,1,0:T(8,128)(2,1)S(1)} %slice.215), channel_id=1, source_target_pairs={{0,2},{1,3},{2,0},{3,1},{4,6},{5,7},{6,4},{7,5},{8,10},{9,11},{10,... | collective-permute-start | bytes 1966088 | tf_op jit(solution)/shard_map/ppermute | solution.py:51
  114.3 25.2 %collective-permute-start.29 = (bf16[4,32,2560]{2,1,0:T(8,128)(2,1)S(1)}, bf16[4,32,2560]{2,1,0:T(8,128)(2,1)S(1)}, u32[]{:S(2)}, u32[]{:S(2)}) collective-permute-start(bf16[4,32,2560]{2,1,0:T(8,128)(2,1)S(1)} %slice.216), channel_id=1, source_target_pairs={{0,1},{1,0},{2,3},{3,2},{4,5},{5,4},{6,7},{7,6},{8,9},{9,8},{10,11... | collective-permute-start | bytes 1966088 | tf_op jit(solution)/shard_map/ppermute | solution.py:51
  116.0 20.3 %collective-permute-start.24 = (bf16[256,512]{1,0:T(8,128)(2,1)S(1)}, bf16[256,512]{1,0:T(8,128)(2,1)S(1)}, u32[]{:S(2)}, u32[]{:S(2)}) collective-permute-start(bf16[256,512]{1,0:T(8,128)(2,1)S(1)} %bitcast.311), channel_id=1, source_target_pairs={{0,1},{1,0},{2,3},{3,2},{4,5},{5,4},{6,7},{7,6},{8,9},{9,8},{10,11... | collective-permute-start | bytes 786440 | tf_op jit(solution)/shard_map/ppermute | solution.py:51
  117.3 21.9 %collective-permute-start.26 = (bf16[256,512]{1,0:T(8,128)(2,1)S(1)}, bf16[256,512]{1,0:T(8,128)(2,1)S(1)}, u32[]{:S(2)}, u32[]{:S(2)}) collective-permute-start(bf16[256,512]{1,0:T(8,128)(2,1)S(1)} %bitcast.307), channel_id=1, source_target_pairs={{0,3},{1,2},{2,1},{3,0},{4,7},{5,6},{6,5},{7,4},{8,11},{9,10},{10,... | collective-permute-start | bytes 786440 | tf_op jit(solution)/shard_map/ppermute | solution.py:51
  144.4 25.5 %collective-permute-start.34 = (bf16[4,128,1024]{2,1,0:T(8,128)(2,1)}, bf16[4,128,1024]{2,1,0:T(8,128)(2,1)}, u32[]{:S(2)}, u32[]{:S(2)}) collective-permute-start(bf16[4,128,1024]{2,1,0:T(8,128)(2,1)} %bitcast.44.refs_0_), channel_id=1, source_target_pairs={{0,1},{1,0},{2,3},{3,2},{4,5},{5,4},{6,7},{7,6},{8,9},{9,8},{10,11... | collective-permute-start | bytes 3145736 | tf_op jit(solution)/shard_map/ppermute | solution.py:51
  146.0 25.4 %collective-permute-start.35 = (bf16[4,128,1024]{2,1,0:T(8,128)(2,1)}, bf16[4,128,1024]{2,1,0:T(8,128)(2,1)}, u32[]{:S(2)}, u32[]{:S(2)}) collective-permute-start(bf16[4,128,1024]{2,1,0:T(8,128)(2,1)} %bitcast.44.refs_0_), channel_id=1, source_target_pairs={{0,2},{1,3},{2,0},{3,1},{4,6},{5,7},{6,4},{7,5},{8,10},{9,11},{10,... | collective-permute-start | bytes 3145736 | tf_op jit(solution)/shard_map/ppermute | solution.py:51
  172.5 19.9 %collective-permute-start.36 = (bf16[4,64,1024]{2,1,0:T(8,128)(2,1)S(1)}, bf16[4,64,1024]{2,1,0:T(8,128)(2,1)S(1)}, u32[]{:S(2)}, u32[]{:S(2)}) collective-permute-start(bf16[4,64,1024]{2,1,0:T(8,128)(2,1)S(1)} %slice.221), channel_id=1, source_target_pairs={{0,2},{1,3},{2,0},{3,1},{4,6},{5,7},{6,4},{7,5},{8,10},{9,11},{10,... | collective-permute-start | bytes 1572872 | tf_op jit(solution)/shard_map/ppermute | solution.py:51
  219.2 113.9 %reduce-scatter.7.cloned.1.call-start = ((), (), s32[]{:S(2)}) async-start(), calls=%async_computation.7 | async-start | bytes 1310720 | tf_op jit(solution)/shard_map/reduce_scatter | solution.py:141
  276.4 113.5 %reduce-scatter.9.cloned.1.call-start = ((), (), s32[]{:S(2)}) async-start(), calls=%async_computation.8 | async-start | bytes 6553600 | tf_op jit(solution)/shard_map/reduce_scatter | solution.py:137
  291.4 130.2 %reduce-scatter.11.cloned.1.call-start = ((), (), s32[]{:S(2)}) async-start(), calls=%async_computation.9 | async-start | bytes 1638400 | tf_op jit(solution)/shard_map/reduce_scatter | solution.py:141
  346.5 40.1 %collective-permute-start.55 = (bf16[512,1024]{1,0:T(8,128)(2,1)}, bf16[512,1024]{1,0:T(8,128)(2,1)}, u32[]{:S(2)}, u32[]{:S(2)}) collective-permute-start(bf16[512,1024]{1,0:T(8,128)(2,1)} %convolution_convert_fusion.2), channel_id=1, source_target_pairs={{0,1},{1,0},{2,3},{3,2},{4,5},{5,4},{6,7},{7,6},{8,9},{9,8},{10,11... | collective-permute-start | bytes 3145736 | tf_op jit(solution)/shard_map/ppermute | solution.py:51
  350.0 39.8 %collective-permute-start.56 = (bf16[512,1024]{1,0:T(8,128)(2,1)}, bf16[512,1024]{1,0:T(8,128)(2,1)}, u32[]{:S(2)}, u32[]{:S(2)}) collective-permute-start(bf16[512,1024]{1,0:T(8,128)(2,1)} %convolution_convert_fusion.1), channel_id=1, source_target_pairs={{0,2},{1,3},{2,0},{3,1},{4,6},{5,7},{6,4},{7,5},{8,10},{9,11},{10,... | collective-permute-start | bytes 3145736 | tf_op jit(solution)/shard_map/ppermute | solution.py:51
  369.9 22.4 %collective-permute-start.49 = (f32[4,384]{1,0:T(4,128)S(1)}, f32[4,384]{1,0:T(4,128)S(1)}, u32[]{:S(2)}, u32[]{:S(2)}) collective-permute-start(f32[4,384]{1,0:T(4,128)S(1)} %bitcast.347), channel_id=1, source_target_pairs={{0,1},{1,0},{2,3},{3,2},{4,5},{5,4},{6,7},{7,6},{8,9},{9,8},{10,11... | collective-permute-start | bytes 18440 | tf_op jit(solution)/shard_map/ppermute | solution.py:51
  391.0 29.8 %collective-permute-start.61 = (bf16[512,1024]{1,0:T(8,128)(2,1)S(1)}, bf16[512,1024]{1,0:T(8,128)(2,1)}, u32[]{:S(2)}, u32[]{:S(2)}) collective-permute-start(bf16[512,1024]{1,0:T(8,128)(2,1)S(1)} %convolution_convert_fusion), channel_id=1, source_target_pairs={{0,3},{1,2},{2,1},{3,0},{4,7},{5,6},{6,5},{7,4},{8,11},{9,10},{10,... | collective-permute-start | bytes 3145736 | tf_op jit(solution)/shard_map/ppermute | solution.py:51
  399.4 21.1 %collective-permute-start.64 = (f32[32,768]{1,0:T(8,128)S(1)}, f32[32,768]{1,0:T(8,128)S(1)}, u32[]{:S(2)}, u32[]{:S(2)}) collective-permute-start(f32[32,768]{1,0:T(8,128)S(1)} %get-tuple-element.202), channel_id=1, source_target_pairs={{0,2},{1,3},{2,0},{3,1},{4,6},{5,7},{6,4},{7,5},{8,10},{9,11},{10,... | collective-permute-start | bytes 294920 | tf_op jit(solution)/shard_map/ppermute | solution.py:51
  (113 other events, 873.9 us)
Sparse Core Ops, SparseCore 0:
  35.9 43.1 all-gather.2
  80.7 25.3 all-gather.4
  219.4 56.3 reduce-scatter.4
  278.0 28.9 reduce-scatter.6
  309.9 74.1 reduce-scatter.8
  390.0 31.5 reduce-scatter.10
